TPU v7x, 32 devices: a whole 2x2x4 slice. The times are simulated.
32 devices in a mesh: sec: 2 (over y), blk: 16 (over z, x, core).
Axes of the slice: x: 2, y: 2, z: 4, core: 2. Of those that a mesh axis runs over, the one named last changes fastest.
Arguments:
- wave_speed: float32 [2, 125, 4096], P('sec', None, 'blk'), may hold values from 0.5 to 2
- inverse_mass: float32 [2, 125, 4096], P('sec', None, 'blk'), may hold values from 0.5 to 2
- source_field: float32 [2, 125, 4096], P('sec', None, 'blk'), may hold values from -4 to 4
- source_time: float32 [2, 12], P('sec'), may hold values from -4 to 4
- face_links: int32 [2, 3, 2048], P('sec', None, 'blk'), may hold values from 0 to 255, as said below
- coupling_links: int32 [5, 8192], P(None, 'blk'), may hold values from -1 to 255, as said below
Outputs:
- adjoint_now: float32 [2, 125, 4096], P('sec', None, 'blk')
- adjoint_before: float32 [2, 125, 4096], P('sec', None, 'blk')
Inputs may be any that keep to these rules, and one draw needn't show every extreme that they name: `face_links`: in each section record k of block b and record k of its peer name each other; the peer is b XOR 2^j for a bit j that depends on the section and k only, and equals b for unlinked records, which are the trailing ones. A block's records name distinct elements. A block has at most 16 records with one peer and exactly 16 with some peer. `coupling_links`: owner -1 marks unused points, which are the trailing points of a block. A box block has at most 4 points with one owner, and every box block has exactly 4 points with one common owner.
All inputs are finite; a program needn't handle non-finite values.
Results may differ from a plain program's by a relative error of at most 0.0001.
Values sent between devices are 32-bit elements; how exact they have to be, the bound alone decides.
No kernel may reach another device: no remote copies, remote signals or barrier semaphores. Data moves between devices by JAX's collectives and lax.ppermute only.
A program may use at most 64 MiB of HBM per device.

v0:
```python
import jax
import jax.numpy as jnp
import numpy as np
from jax import lax
from jax.sharding import PartitionSpec as P

CAPC = 4
STEPS = 12


DT_SQUARED = 0.05
PENALTY = 10.0


def partner_2(value, axis, stride):
    return lax.ppermute(value, axis, [(i, i ^ 1 << stride) for i in range(lax.axis_size(axis))])


def node_tables():
    abscissae = np.array([-1.0, -np.sqrt(3.0 / 7.0), 0.0, np.sqrt(3.0 / 7.0), 1.0])
    weights = np.array([0.1, 49.0 / 90.0, 32.0 / 45.0, 49.0 / 90.0, 0.1])
    legendre = (35.0 * abscissae**4 - 30.0 * abscissae**2 + 3.0) / 8.0
    derivative = np.zeros((5, 5))
    for i in range(5):
        for j in range(5):
            if i != j:
                derivative[i, j] = legendre[i] / (legendre[j] * (abscissae[i] - abscissae[j]))
    derivative[0, 0] = -2.5
    derivative[4, 4] = 2.5
    identity = np.eye(5)
    operator = np.concatenate(
        [
            np.kron(np.kron(derivative, identity), identity),
            np.kron(np.kron(identity, derivative), identity),
            np.kron(np.kron(identity, identity), derivative),
        ],
        axis=0,
    )
    weight_cube = weights[:, None, None] * weights[None, :, None] * weights[None, None, :]
    lattice = np.arange(125).reshape(5, 5, 5)
    face_nodes = np.stack(
        [
            lattice[0].ravel(),
            lattice[4].ravel(),
            lattice[:, 0].ravel(),
            lattice[:, 4].ravel(),
            lattice[:, :, 0].ravel(),
            lattice[:, :, 4].ravel(),
        ]
    )
    return (
        operator.astype(np.float32),
        weight_cube.reshape(125, 1).astype(np.float32),
        face_nodes.astype(np.int32),
    )


def stiffness(field_in, speed_sq, operator, weight_cube):
    columns = field_in.shape[-1]
    scaling = weight_cube * speed_sq
    grads = jnp.dot(
        operator, field_in, precision=lax.Precision.HIGHEST, preferred_element_type=jnp.float32
    )
    scaled = (grads.reshape(3, 125, columns) * scaling[None]).reshape(375, columns)
    return jnp.dot(
        operator.T, scaled, precision=lax.Precision.HIGHEST, preferred_element_type=jnp.float32
    )


def body(wave_speed, inverse_mass, source_field, source_time, face_links, coupling_links):
    operator_np, weight_np, faces_np = node_tables()
    operator = jnp.asarray(operator_np)
    weight_cube = jnp.asarray(weight_np)
    picker_np = np.zeros((150, 125), np.float32)
    for side_number in range(6):
        for node_number in range(25):
            picker_np[side_number * 25 + node_number, faces_np[side_number, node_number]] = 1.0
    picker = jnp.asarray(picker_np)
    spreader = jnp.asarray(picker_np.T.copy())
    speed_sq = wave_speed[0]
    inverse = inverse_mass[0]
    forcing = source_field[0]
    timing = source_time[0]
    element = face_links[0, 0]
    face_side = face_links[0, 1]
    face_peer = face_links[0, 2]
    blocks = lax.axis_size("blk")
    bit_count = blocks.bit_length() - 1
    myself = lax.axis_index("blk")
    is_box = lax.axis_index("sec") == 0
    records = element.shape[0]
    per_peer = records // 8
    ordinal = jnp.arange(records)
    linked = face_peer != myself
    side_mask = face_side[None, None, :] == jnp.arange(6, dtype=jnp.int32)[:, None, None]
    earlier = ordinal[None, :] < ordinal[:, None]
    face_slot = jnp.sum(
        ((face_peer[:, None] == face_peer[None, :]) & earlier).astype(jnp.int32), axis=1
    )
    offset_bits = jnp.bitwise_xor(face_peer, myself)
    bit_index = jnp.zeros((records,), jnp.int32)
    for bit_number in range(bit_count):
        bit_index = bit_index + bit_number * (offset_bits == 1 << bit_number).astype(jnp.int32)
    pair_column = jnp.where(linked, bit_index * per_peer + face_slot, 0)
    point_element = coupling_links[0]
    point_node = coupling_links[1]
    point_owner = coupling_links[2]
    target_element = coupling_links[3]
    target_node = coupling_links[4]
    in_use = point_owner >= 0
    owner_safe = jnp.maximum(point_owner, 0)
    point_ordinal = jnp.arange(point_owner.shape[0])
    point_earlier = point_ordinal[None, :] < point_ordinal[:, None]
    point_slot = jnp.sum(
        ((point_owner[:, None] == point_owner[None, :]) & point_earlier).astype(jnp.int32), axis=1
    )
    point_column = jnp.where(in_use, point_slot * blocks + owner_safe, 0)
    slot_total = CAPC * blocks
    outbound = jnp.zeros((3, slot_total), jnp.int32)
    outbound = outbound.at[0, point_column].add(jnp.where(in_use, target_element, 0))
    outbound = outbound.at[1, point_column].add(jnp.where(in_use, target_node, 0))
    outbound = outbound.at[2, point_column].add(in_use.astype(jnp.int32))
    inbound = lax.all_to_all(
        outbound.reshape(3, CAPC, blocks), "blk", split_axis=2, concat_axis=2, tiled=True
    ).reshape(3, slot_total)
    remote_element = inbound[0]
    remote_node = inbound[1]
    remote_flag = inbound[2].astype(jnp.float32)
    target_rows = jnp.concatenate([point_node, remote_node])
    target_cols = jnp.concatenate([point_element, remote_element])
    current = jnp.zeros(speed_sq.shape, jnp.float32)
    previous = jnp.zeros(speed_sq.shape, jnp.float32)
    for moment in range(STEPS):
        internal = stiffness(current, speed_sq, operator, weight_cube)
        stacked = jnp.dot(
            picker,
            internal[:, element],
            precision=lax.Precision.HIGHEST,
            preferred_element_type=jnp.float32,
        ).reshape(6, 25, records)
        payload = jnp.sum(jnp.where(side_mask, stacked, 0.0), axis=0)
        payload = jnp.where(linked[None, :], payload, 0.0)
        outgoing = (
            jnp.zeros((25, bit_count * per_peer), jnp.float32).at[:, pair_column].add(payload)
        )
        arrived = []
        for bit_number in range(bit_count):
            piece = outgoing[:, bit_number * per_peer : (bit_number + 1) * per_peer]
            arrived.append(partner_2(piece, "blk", bit_number))
        partner = jnp.concatenate(arrived, axis=1)[:, pair_column]
        partner = jnp.where(linked[None, :], partner, 0.0)
        masked = jnp.where(side_mask, partner[None], 0.0).reshape(150, records)
        assembled = internal.at[:, element].add(
            jnp.dot(
                spreader,
                masked,
                precision=lax.Precision.HIGHEST,
                preferred_element_type=jnp.float32,
            )
        )
        velocity = current - previous
        traction = assembled[point_node, point_element]
        box_send = (
            jnp.zeros((slot_total,), jnp.float32)
            .at[point_column]
            .add(jnp.where(in_use, traction, 0.0))
        )
        global_send = velocity[remote_node, remote_element] * remote_flag
        dispatch = jnp.where(is_box, box_send, global_send).reshape(CAPC, blocks)
        crossed = partner_2(dispatch, "sec", 0)
        received = lax.all_to_all(crossed, "blk", split_axis=1, concat_axis=1, tiled=True)
        received = received.reshape(slot_total)
        remote_velocity = received[point_column]
        box_terms = jnp.where(
            in_use, PENALTY * (remote_velocity - velocity[point_node, point_element]), 0.0
        )
        values = jnp.concatenate(
            [jnp.where(is_box, box_terms, 0.0), jnp.where(is_box, 0.0, received * remote_flag)]
        )
        driving = timing[moment] * forcing - assembled
        driving = driving.at[target_rows, target_cols].add(values)
        advanced = 2.0 * current - previous + DT_SQUARED * inverse * driving
        previous = current
        current = advanced
    return (current[None], previous[None])


def solution(mesh):
    in_specs = (
        P("sec", None, "blk"),
        P("sec", None, "blk"),
        P("sec", None, "blk"),
        P("sec", None),
        P("sec", None, "blk"),
        P(None, "blk"),
    )
    out_specs = (P("sec", None, "blk"), P("sec", None, "blk"))
    return jax.shard_map(body, mesh=mesh, in_specs=in_specs, out_specs=out_specs, check_vma=False)
```

profile of v0, /device:TPU:0, one launch (start us, length us, event | category | flops | bytes accessed | tf_op | source)
XLA Modules:
  0.0 1408.7 jit_solution(6198110718570769417)
XLA Ops:
  128.0 40.1 %fusion.83 = (f32[512]{0:T(512)S(1)}, pred[512]{0:T(512)(128)(4,1)S(1)}, pred[512]{0:T(512)(128)(4,1)S(1)}, pred[512]{0:T(512)(128)(4,1)S(1)}, pred[512]{0:T(512...) fusion(pred[512]{0:T(512)(128)(4,1)S(1)} %get-tuple-element.99,, ...), kind=kLoop, calls=%fused_computation.341 | loop fusion | flops 66560 | bytes 39169 | tf_op jit(solution)/shard_map/jit(_where)/select_n | solution.py:178
  168.1 30.1 %scatter_fusion.4 = f32[125,256]{1,0:T(8,128)S(1)} fusion(f32[125,256]{1,0:T(8,128)S(1)} %copy.421, s32[576]{0:T(1024)S(1)} %fusion.42, f32[576]{0:T(1024)S(1)} %pad_maximum_fusion.12), kind=kCustom, calls=%fused_computation.66 | custom fusion | flops 576 | bytes 11520 | tf_op jit(solution)/shard_map/scatter-add | solution.py:181
  238.2 40.1 %fusion.80 = f32[512]{0:T(512)S(1)} fusion(pred[512]{0:T(512)(128)(4,1)S(1)} %get-tuple-element.99, f32[512]{0:T(512)S(1)} %gather_fusion.9, pred[512]{0:T(512)(128)(4,1)S(1)} %get-tuple-element.97, pred[512]{0:T(512)(128)(4,1)S(1)} %get-tuple-element.96, pred[512]{0:T(512)(128)(4,1)S(1)} %get-tuple-element.95, pred[512]{0:T(512)(128)(4,1)S(1)} %get-tuple-element.94, ...), kind=kLoop, calls=%fused_computation.337 | loop fusion | flops 34304 | bytes 37121 | tf_op jit(solution)/shard_map/jit(_where)/select_n | solution.py:178
  278.3 30.1 %scatter_fusion.6 = f32[125,256]{1,0:T(8,128)S(1)} fusion(f32[125,256]{1,0:T(8,128)S(1)} %copy.429, s32[576]{0:T(1024)S(1)} %fusion.42, f32[576]{0:T(1024)S(1)} %pad_maximum_fusion.13), kind=kCustom, calls=%fused_computation.70 | custom fusion | flops 576 | bytes 11520 | tf_op jit(solution)/shard_map/scatter-add | solution.py:181
  347.9 40.0 %fusion.77 = f32[512]{0:T(512)S(1)} fusion(pred[512]{0:T(512)(128)(4,1)S(1)} %get-tuple-element.99, f32[512]{0:T(512)S(1)} %gather_fusion.14, pred[512]{0:T(512)(128)(4,1)S(1)} %get-tuple-element.97, pred[512]{0:T(512)(128)(4,1)S(1)} %get-tuple-element.96, pred[512]{0:T(512)(128)(4,1)S(1)} %get-tuple-element.95, pred[512]{0:T(512)(128)(4,1)S(1)} %get-tuple-element.94, ...), kind=kLoop, calls=%fused_computation.333 | loop fusion | flops 34304 | bytes 37121 | tf_op jit(solution)/shard_map/jit(_where)/select_n | solution.py:178
  387.9 30.1 %scatter_fusion.8 = f32[125,256]{1,0:T(8,128)S(1)} fusion(f32[125,256]{1,0:T(8,128)S(1)} %copy.437, s32[576]{0:T(1024)S(1)} %fusion.42, f32[576]{0:T(1024)S(1)} %pad_maximum_fusion.14), kind=kCustom, calls=%fused_computation.74 | custom fusion | flops 576 | bytes 11520 | tf_op jit(solution)/shard_map/scatter-add | solution.py:181
  458.2 40.1 %fusion.74 = f32[512]{0:T(512)S(1)} fusion(pred[512]{0:T(512)(128)(4,1)S(1)} %get-tuple-element.99, f32[512]{0:T(512)S(1)} %gather_fusion.19, pred[512]{0:T(512)(128)(4,1)S(1)} %get-tuple-element.97, pred[512]{0:T(512)(128)(4,1)S(1)} %get-tuple-element.96, pred[512]{0:T(512)(128)(4,1)S(1)} %get-tuple-element.95, pred[512]{0:T(512)(128)(4,1)S(1)} %get-tuple-element.94, ...), kind=kLoop, calls=%fused_computation.329 | loop fusion | flops 34304 | bytes 37121 | tf_op jit(solution)/shard_map/jit(_where)/select_n | solution.py:178
  498.3 30.1 %scatter_fusion.10 = f32[125,256]{1,0:T(8,128)S(1)} fusion(f32[125,256]{1,0:T(8,128)S(1)} %copy.445, s32[576]{0:T(1024)S(1)} %fusion.42, f32[576]{0:T(1024)S(1)} %pad_maximum_fusion.15), kind=kCustom, calls=%fused_computation.78 | custom fusion | flops 576 | bytes 11520 | tf_op jit(solution)/shard_map/scatter-add | solution.py:181
  567.4 39.9 %fusion.71 = f32[512]{0:T(512)S(1)} fusion(pred[512]{0:T(512)(128)(4,1)S(1)} %get-tuple-element.99, f32[512]{0:T(512)S(1)} %gather_fusion.24, pred[512]{0:T(512)(128)(4,1)S(1)} %get-tuple-element.97, pred[512]{0:T(512)(128)(4,1)S(1)} %get-tuple-element.96, pred[512]{0:T(512)(128)(4,1)S(1)} %get-tuple-element.95, pred[512]{0:T(512)(128)(4,1)S(1)} %get-tuple-element.94, ...), kind=kLoop, calls=%fused_computation.325 | loop fusion | flops 34304 | bytes 37121 | tf_op jit(solution)/shard_map/jit(_where)/select_n | solution.py:178
  607.4 30.1 %scatter_fusion.12 = f32[125,256]{1,0:T(8,128)S(1)} fusion(f32[125,256]{1,0:T(8,128)S(1)} %copy.453, s32[576]{0:T(1024)S(1)} %fusion.42, f32[576]{0:T(1024)S(1)} %pad_maximum_fusion.16), kind=kCustom, calls=%fused_computation.82 | custom fusion | flops 576 | bytes 11520 | tf_op jit(solution)/shard_map/scatter-add | solution.py:181
  677.7 40.0 %fusion.68 = f32[512]{0:T(512)S(1)} fusion(pred[512]{0:T(512)(128)(4,1)S(1)} %get-tuple-element.99, f32[512]{0:T(512)S(1)} %gather_fusion.29, pred[512]{0:T(512)(128)(4,1)S(1)} %get-tuple-element.97, pred[512]{0:T(512)(128)(4,1)S(1)} %get-tuple-element.96, pred[512]{0:T(512)(128)(4,1)S(1)} %get-tuple-element.95, pred[512]{0:T(512)(128)(4,1)S(1)} %get-tuple-element.94, ...), kind=kLoop, calls=%fused_computation.321 | loop fusion | flops 34304 | bytes 37121 | tf_op jit(solution)/shard_map/jit(_where)/select_n | solution.py:178
  717.8 30.1 %scatter_fusion.14 = f32[125,256]{1,0:T(8,128)S(1)} fusion(f32[125,256]{1,0:T(8,128)S(1)} %copy.461, s32[576]{0:T(1024)S(1)} %fusion.42, f32[576]{0:T(1024)S(1)} %pad_maximum_fusion.17), kind=kCustom, calls=%fused_computation.86 | custom fusion | flops 576 | bytes 11520 | tf_op jit(solution)/shard_map/scatter-add | solution.py:181
  787.3 40.0 %fusion.65 = f32[512]{0:T(512)S(1)} fusion(pred[512]{0:T(512)(128)(4,1)S(1)} %get-tuple-element.99, f32[512]{0:T(512)S(1)} %gather_fusion.34, pred[512]{0:T(512)(128)(4,1)S(1)} %get-tuple-element.97, pred[512]{0:T(512)(128)(4,1)S(1)} %get-tuple-element.96, pred[512]{0:T(512)(128)(4,1)S(1)} %get-tuple-element.95, pred[512]{0:T(512)(128)(4,1)S(1)} %get-tuple-element.94, ...), kind=kLoop, calls=%fused_computation.317 | loop fusion | flops 34304 | bytes 37121 | tf_op jit(solution)/shard_map/jit(_where)/select_n | solution.py:178
  827.3 30.1 %scatter_fusion.16 = f32[125,256]{1,0:T(8,128)S(1)} fusion(f32[125,256]{1,0:T(8,128)S(1)} %copy.469, s32[576]{0:T(1024)S(1)} %fusion.42, f32[576]{0:T(1024)S(1)} %pad_maximum_fusion.18), kind=kCustom, calls=%fused_computation.90 | custom fusion | flops 576 | bytes 11520 | tf_op jit(solution)/shard_map/scatter-add | solution.py:181
  897.4 40.0 %fusion.62 = f32[512]{0:T(512)S(1)} fusion(pred[512]{0:T(512)(128)(4,1)S(1)} %get-tuple-element.99, f32[512]{0:T(512)S(1)} %gather_fusion.39, pred[512]{0:T(512)(128)(4,1)S(1)} %get-tuple-element.97, pred[512]{0:T(512)(128)(4,1)S(1)} %get-tuple-element.96, pred[512]{0:T(512)(128)(4,1)S(1)} %get-tuple-element.95, pred[512]{0:T(512)(128)(4,1)S(1)} %get-tuple-element.94, ...), kind=kLoop, calls=%fused_computation.313 | loop fusion | flops 34304 | bytes 37121 | tf_op jit(solution)/shard_map/jit(_where)/select_n | solution.py:178
  937.4 30.1 %scatter_fusion.18 = f32[125,256]{1,0:T(8,128)S(1)} fusion(f32[125,256]{1,0:T(8,128)S(1)} %copy.477, s32[576]{0:T(1024)S(1)} %fusion.42, f32[576]{0:T(1024)S(1)} %pad_maximum_fusion.19), kind=kCustom, calls=%fused_computation.94 | custom fusion | flops 576 | bytes 11520 | tf_op jit(solution)/shard_map/scatter-add | solution.py:181
  1006.8 40.0 %fusion.59 = f32[512]{0:T(512)S(1)} fusion(pred[512]{0:T(512)(128)(4,1)S(1)} %get-tuple-element.99, f32[512]{0:T(512)S(1)} %gather_fusion.44, pred[512]{0:T(512)(128)(4,1)S(1)} %get-tuple-element.97, pred[512]{0:T(512)(128)(4,1)S(1)} %get-tuple-element.96, pred[512]{0:T(512)(128)(4,1)S(1)} %get-tuple-element.95, pred[512]{0:T(512)(128)(4,1)S(1)} %get-tuple-element.94, ...), kind=kLoop, calls=%fused_computation.309 | loop fusion | flops 34304 | bytes 37121 | tf_op jit(solution)/shard_map/jit(_where)/select_n | solution.py:178
  1046.8 30.1 %scatter_fusion.20 = f32[125,256]{1,0:T(8,128)S(1)} fusion(f32[125,256]{1,0:T(8,128)S(1)} %copy.485, s32[576]{0:T(1024)S(1)} %fusion.42, f32[576]{0:T(1024)S(1)} %pad_maximum_fusion.20), kind=kCustom, calls=%fused_computation.98 | custom fusion | flops 576 | bytes 11520 | tf_op jit(solution)/shard_map/scatter-add | solution.py:181
  1117.2 40.0 %fusion.56 = f32[512]{0:T(512)S(1)} fusion(pred[512]{0:T(512)(128)(4,1)S(1)} %get-tuple-element.99, f32[512]{0:T(512)S(1)} %gather_fusion.49, pred[512]{0:T(512)(128)(4,1)S(1)} %get-tuple-element.97, pred[512]{0:T(512)(128)(4,1)S(1)} %get-tuple-element.96, pred[512]{0:T(512)(128)(4,1)S(1)} %get-tuple-element.95, pred[512]{0:T(512)(128)(4,1)S(1)} %get-tuple-element.94, ...), kind=kLoop, calls=%fused_computation.305 | loop fusion | flops 34304 | bytes 37121 | tf_op jit(solution)/shard_map/jit(_where)/select_n | solution.py:178
  1157.2 30.1 %scatter_fusion.22 = f32[125,256]{1,0:T(8,128)S(1)} fusion(f32[125,256]{1,0:T(8,128)S(1)} %copy.493, s32[576]{0:T(1024)S(1)} %fusion.42, f32[576]{0:T(1024)S(1)} %pad_maximum_fusion.21), kind=kCustom, calls=%fused_computation.102 | custom fusion | flops 576 | bytes 11520 | tf_op jit(solution)/shard_map/scatter-add | solution.py:181
  1226.3 39.9 %fusion.53 = f32[512]{0:T(512)S(1)} fusion(pred[512]{0:T(512)(128)(4,1)S(1)} %get-tuple-element.99, f32[512]{0:T(512)S(1)} %gather_fusion.54, pred[512]{0:T(512)(128)(4,1)S(1)} %get-tuple-element.97, pred[512]{0:T(512)(128)(4,1)S(1)} %get-tuple-element.96, pred[512]{0:T(512)(128)(4,1)S(1)} %get-tuple-element.95, pred[512]{0:T(512)(128)(4,1)S(1)} %get-tuple-element.94, ...), kind=kLoop, calls=%fused_computation.301 | loop fusion | flops 34304 | bytes 37121 | tf_op jit(solution)/shard_map/jit(_where)/select_n | solution.py:178
  1266.2 30.1 %scatter_fusion.24 = f32[125,256]{1,0:T(8,128)S(1)} fusion(f32[125,256]{1,0:T(8,128)S(1)} %copy.501, s32[576]{0:T(1024)S(1)} %fusion.42, f32[576]{0:T(1024)S(1)} %pad_maximum_fusion.22), kind=kCustom, calls=%fused_computation.106 | custom fusion | flops 576 | bytes 11520 | tf_op jit(solution)/shard_map/scatter-add | solution.py:181
  1337.4 39.9 %fusion.50 = f32[512]{0:T(512)S(1)} fusion(pred[512]{0:T(512)(128)(4,1)S(1)} %get-tuple-element.99, f32[512]{0:T(512)S(1)} %gather_fusion.59, pred[512]{0:T(512)(128)(4,1)S(1)} %get-tuple-element.97, pred[512]{0:T(512)(128)(4,1)S(1)} %get-tuple-element.96, pred[512]{0:T(512)(128)(4,1)S(1)} %get-tuple-element.95, pred[512]{0:T(512)(128)(4,1)S(1)} %get-tuple-element.94, ...), kind=kLoop, calls=%fused_computation.297 | loop fusion | flops 34304 | bytes 37121 | tf_op jit(solution)/shard_map/jit(_where)/select_n | solution.py:178
  1377.3 30.1 %scatter_fusion.26 = f32[125,256]{1,0:T(8,128)S(1)} fusion(f32[125,256]{1,0:T(8,128)S(1)} %copy.509, s32[576]{0:T(1024)S(1)} %fusion.42, f32[576]{0:T(1024)S(1)} %pad_maximum_fusion.23), kind=kCustom, calls=%fused_computation.110 | custom fusion | flops 576 | bytes 11520 | tf_op jit(solution)/shard_map/scatter-add | solution.py:181
  (646 shorter events, 563.6 us)
Async XLA Ops:
  7.8 7.6 collective-permute-start
  8.3 7.1 collective-permute-start.3
  93.6 13.0 all-to-all-start
  112.4 12.6 all-to-all-start.1
  217.5 6.0 collective-permute-start.9
  224.3 11.0 all-to-all-start.2
  328.1 5.0 collective-permute-start.14
  333.9 11.0 all-to-all-start.3
  437.3 6.0 collective-permute-start.19
  444.0 11.2 all-to-all-start.4
  547.7 5.0 collective-permute-start.24
  553.4 11.0 all-to-all-start.5
  657.0 6.0 collective-permute-start.29
  663.7 11.0 all-to-all-start.6
  767.2 5.0 collective-permute-start.34
  772.9 11.4 all-to-all-start.7
  876.7 6.1 collective-permute-start.39
  883.4 11.0 all-to-all-start.8
  992.7 11.0 all-to-all-start.9
  1096.2 6.0 collective-permute-start.49
  1103.0 11.2 all-to-all-start.10
  1212.3 11.0 all-to-all-start.11
  1315.9 6.8 collective-permute-start.59
  1323.4 11.0 all-to-all-start.12
  (58 other events, 260.3 us)
where the time goes:
time: 1420 us; the launch traced here: 1410 us
  other arithmetic  1000 us (70%)
  local copies, waits for them, and re-layouts  181 us (13%)
  starting transfers between devices  102 us (7%)
  waiting for transfers between devices  95.3 us (7%)
  matrix products  23.9 us (2%)
    select_n x12, other arithmetic, body(): jnp.where(is_box, box_terms, 0.0)  480 us
    scatter-add x12, other arithmetic, body(): driving = driving.at[target_rows, target_cols].add(values)  361 us
    all_to_all x12, waiting for transfers between devices, body(): lax.all_to_all(crossed, 'blk', split_axis=1, concat_axis=1, tiled=True)  67.6 us
    all_to_all x12, starting transfers between devices, body(): lax.all_to_all(crossed, 'blk', split_axis=1, concat_axis=1, tiled=True)  57.9 us
    gather x12, local copies, waits for them, and re-layouts, body(): velocity[point_node, point_element]  54.2 us
    scatter-add x12, other arithmetic, body(): box_send = jnp.zeros((slot_total,), jnp.float32).at[point_column].add(jnp...  49 us
    gather x12, local copies, waits for them, and re-layouts, body(): traction = assembled[point_node, point_element]  45 us
    ppermute x60, starting transfers between devices, partner_2(): lax.ppermute(value, axis, [(i, i ^ 1 << stride) for i in range(lax.axis_s...  40.2 us
  transfers between devices with their start and end apart: 73, of which 37 were waited for; matrix products, arithmetic and copies ran while one was open for 6% of the time, Pallas kernels for 0%

commit v1 on v0

--- a/solution.py
+++ b/solution.py
@@ -2,6 +2,8 @@
 import jax.numpy as jnp
 import numpy as np
 from jax import lax
+from jax.experimental import pallas as pl
+from jax.experimental.pallas import tpu as pltpu
 from jax.sharding import PartitionSpec as P
 
 CAPC = 4
@@ -67,7 +69,7 @@
     )
 
 
-def body(wave_speed, inverse_mass, source_field, source_time, face_links, coupling_links):
+def general_body(wave_speed, inverse_mass, source_field, source_time, face_links, coupling_links):
     operator_np, weight_np, faces_np = node_tables()
     operator = jnp.asarray(operator_np)
     weight_cube = jnp.asarray(weight_np)
@@ -130,7 +132,8 @@
     target_cols = jnp.concatenate([point_element, remote_element])
     current = jnp.zeros(speed_sq.shape, jnp.float32)
     previous = jnp.zeros(speed_sq.shape, jnp.float32)
-    for moment in range(STEPS):
+    def one_step(moment, state):
+        current, previous = state
         internal = stiffness(current, speed_sq, operator, weight_cube)
         stacked = jnp.dot(
             picker,
@@ -180,9 +183,588 @@
         driving = timing[moment] * forcing - assembled
         driving = driving.at[target_rows, target_cols].add(values)
         advanced = 2.0 * current - previous + DT_SQUARED * inverse * driving
-        previous = current
-        current = advanced
+        return advanced, current
+
+    current, previous = lax.fori_loop(0, STEPS, one_step, (current, previous))
     return (current[None], previous[None])
+
+
+LANES = 128
+HALF = 64
+SLOTS = 6
+LAGS = 10
+PAIRS = LAGS // 2
+FREE_ROWS = STEPS // 2
+GAIN_ROW = FREE_ROWS
+INDEX_ROW = GAIN_ROW + SLOTS * PAIRS
+FLAG_ROW = INDEX_ROW + SLOTS // 2
+PAYLOAD = FLAG_ROW + 1
+NODES = 125
+EXACT = lax.Precision.HIGHEST
+
+
+def line_matrix():
+    abscissae = np.array([-1.0, -np.sqrt(3.0 / 7.0), 0.0, np.sqrt(3.0 / 7.0), 1.0])
+    legendre = (35.0 * abscissae**4 - 30.0 * abscissae**2 + 3.0) / 8.0
+    derivative = np.zeros((5, 5))
+    for i in range(5):
+        for j in range(5):
+            if i != j:
+                derivative[i, j] = legendre[i] / (legendre[j] * (abscissae[i] - abscissae[j]))
+    derivative[0, 0] = -2.5
+    derivative[4, 4] = 2.5
+    return derivative
+
+
+def apply_line(matrix, x):
+    odd = [x[0] - x[4], x[1] - x[3]]
+    even = [x[0] + x[4], x[1] + x[3]]
+    out = [None] * 5
+    for i in range(2):
+        symmetric = (
+            float(0.5 * (matrix[i, 0] - matrix[i, 4])) * odd[0]
+            + float(0.5 * (matrix[i, 1] - matrix[i, 3])) * odd[1]
+        )
+        skew = (
+            float(0.5 * (matrix[i, 0] + matrix[i, 4])) * even[0]
+            + float(0.5 * (matrix[i, 1] + matrix[i, 3])) * even[1]
+            + float(matrix[i, 2]) * x[2]
+        )
+        out[i] = symmetric + skew
+        out[4 - i] = symmetric - skew
+    out[2] = float(matrix[2, 0]) * odd[0] + float(matrix[2, 1]) * odd[1]
+    return out
+
+
+def stiffness_lines(x_ref, scale_ref, y_ref):
+    forward = line_matrix()
+    backward = forward.T.copy()
+
+    def along(index):
+        x = [x_ref[k] for k in index]
+        grads = apply_line(forward, x)
+        scaled = [g * scale_ref[k] for g, k in zip(grads, index)]
+        return apply_line(backward, scaled)
+
+    for b in range(5):
+        for c in range(5):
+            index = [25 * j + 5 * b + c for j in range(5)]
+            for k, value in zip(index, along(index)):
+                y_ref[k] = value
+    for a in range(5):
+        total = [y_ref[25 * a + k] for k in range(25)]
+        for c in range(5):
+            local = [5 * j + c for j in range(5)]
+            for k, value in zip(local, along([25 * a + k for k in local])):
+                total[k] = total[k] + value
+        for b in range(5):
+            local = [5 * b + j for j in range(5)]
+            for k, value in zip(local, along([25 * a + k for k in local])):
+                total[k] = total[k] + value
+        for k in range(25):
+            y_ref[25 * a + k] = total[k]
+
+
+def partner_faces(load, side):
+    _, _, faces = node_tables()
+    masks = [side == q for q in range(6)]
+    arrived = []
+    for t in range(25):
+        value = jnp.zeros(side.shape, jnp.float32)
+        for q in range(6):
+            value = jnp.where(masks[q], load(int(faces[q, t])), value)
+        arrived.append(pltpu.roll(value, HALF, 1))
+    extra = [None] * NODES
+    for q in range(6):
+        for t in range(25):
+            node = int(faces[q, t])
+            before = extra[node]
+            zero = jnp.zeros(side.shape, jnp.float32) if before is None else before
+            extra[node] = jnp.where(masks[q], arrived[t], zero)
+    return extra
+
+
+def response_kernel(
+    coef_ref,
+    data_ref,
+    side_ref,
+    start_ref,
+    list_ref,
+    index_ref,
+    out_ref,
+    scale_ref,
+    x_ref,
+    h_ref,
+    y_ref,
+    t_ref,
+    in_ref,
+    rec_ref,
+    seen_ref,
+):
+    row = lax.broadcasted_iota(jnp.int32, (8, LANES), 0)
+    low = lax.broadcasted_iota(jnp.int32, (8, LANES), 1) < HALF
+    first = row == 0
+    side = side_ref[...]
+    wanted = list_ref[...]
+    forced = row == SLOTS
+    shape = (8, LANES)
+
+    def tile(ref, k, n):
+        return jnp.broadcast_to(ref[k, n], shape)
+
+    for n in range(NODES):
+        x_ref[n] = jnp.where(row == 1, jnp.broadcast_to(start_ref[n], shape), 0.0)
+        h_ref[n] = jnp.zeros(shape, jnp.float32)
+        y_ref[n] = jnp.zeros(shape, jnp.float32)
+        scale_ref[n] = tile(data_ref, 0, n)
+
+    def step(moment, _):
+        drive = coef_ref[0, moment]
+        keep = coef_ref[1, moment]
+        stiff = coef_ref[2, moment]
+        begin = coef_ref[3, moment]
+        is_box = coef_ref[4, 0]
+        for n in range(NODES):
+            t_ref[n] = jnp.where(first, y_ref[n], x_ref[n])
+        extra = partner_faces(lambda k: t_ref[k], side)
+        for n in range(NODES):
+            assembled = t_ref[n] if extra[n] is None else t_ref[n] + extra[n]
+            inverse = tile(data_ref, 1, n)
+            force = tile(data_ref, 2, n)
+            damp = tile(data_ref, 3, n)
+            x = x_ref[n]
+            h = h_ref[n]
+            advanced = 2.0 * x - h + inverse * (drive * force - assembled - damp * x)
+            in_ref[n] = jnp.where(first, advanced, assembled)
+            rec_ref[n] = is_box * assembled + (1.0 - is_box) * (x - h)
+        stiffness_lines(in_ref, scale_ref, y_ref)
+        seen = jnp.zeros(shape, jnp.float32)
+        for n in range(NODES):
+            inverse = tile(data_ref, 1, n)
+            damp = tile(data_ref, 3, n)
+            x = x_ref[n]
+            h = h_ref[n]
+            dx = damp * x
+            adjoint = 2.0 * keep * x - h + inverse * (stiff * y_ref[n] - keep * dx + begin * x)
+            x_ref[n] = jnp.where(first, in_ref[n], adjoint)
+            h_ref[n] = keep * (x - inverse * dx) + begin * (inverse * x)
+            source = jnp.where(
+                forced,
+                jnp.broadcast_to(rec_ref[n][0:1], shape),
+                jnp.broadcast_to(adjoint[1:2], shape),
+            )
+            seen = seen + jnp.where(wanted == n, source, 0.0)
+        seen_ref[moment] = seen + pltpu.roll(seen, HALF, 1)
+        return 0
+
+    lax.fori_loop(0, STEPS, step, 0)
+    pair_low = lax.broadcasted_iota(jnp.int32, (1, LANES), 1) < HALF
+    for k in range(FREE_ROWS):
+        out_ref[0, k : k + 1] = jnp.where(
+            pair_low,
+            seen_ref[2 * k][SLOTS : SLOTS + 1],
+            seen_ref[2 * k + 1][SLOTS : SLOTS + 1],
+        )
+    for q in range(SLOTS):
+        for k in range(PAIRS):
+            r = GAIN_ROW + q * PAIRS + k
+            out_ref[0, r : r + 1] = jnp.where(
+                pair_low, seen_ref[2 * k][q : q + 1], seen_ref[2 * k + 1][q : q + 1]
+            )
+    out_ref[0, INDEX_ROW:PAYLOAD] = index_ref[...]
+    for k in range(1, out_ref.shape[0]):
+        out_ref[k] = out_ref[0]
+
+
+def gather_packed(packed, at):
+    rows = at // LANES
+    lanes = at % LANES
+    out = jnp.zeros(at.shape, jnp.float32)
+    for k in range(8):
+        source = jnp.broadcast_to(packed[k : k + 1], at.shape)
+        picked = jnp.take_along_axis(source, lanes, axis=1, mode="promise_in_bounds")
+        out = jnp.where(rows == k, picked, out)
+    return out
+
+
+def final_kernel(
+    where_ref,
+    time_ref,
+    mine_ref,
+    other_ref,
+    data_ref,
+    side_ref,
+    at_ref,
+    node_ref,
+    key_ref,
+    lane_key_ref,
+    home_ref,
+    now_ref,
+    before_ref,
+    both_ref,
+    spread_ref,
+    input_ref,
+    x_ref,
+    h_ref,
+    y_ref,
+    kick_ref,
+    flat_ref,
+):
+    is_box = where_ref[0] == 0
+    parity = where_ref[1]
+    both_ref[parity] = mine_ref[...]
+    both_ref[1 - parity] = other_ref[...]
+    low = lax.broadcasted_iota(jnp.int32, (8, LANES), 1) < HALF
+
+    def rows(section, core, r):
+        return both_ref[core, section * 8 : section * 8 + 8, r, :]
+
+    index = {}
+    for s in range(2):
+        for p in range(2):
+            for k in range(SLOTS // 2):
+                pair = rows(s, p, INDEX_ROW + k).astype(jnp.int32)
+                turned = pltpu.roll(pair, HALF, 1)
+                index[s, p, 2 * k] = jnp.where(low, pair, turned)
+                index[s, p, 2 * k + 1] = jnp.where(low, turned, pair)
+    at = at_ref[...]
+    packed = {}
+    pairs = {}
+    last = {}
+    zero = jnp.zeros((8, LANES), jnp.float32)
+    for n in range(1, STEPS):
+        value = {}
+        for s in range(2):
+            for p in range(2):
+                free = rows(s, p, n // 2)
+                total = jnp.where(low, free, 0.0) if n % 2 == 0 else jnp.where(low, 0.0, free)
+                for q in range(SLOTS):
+                    for k in range(PAIRS):
+                        m = n - 2 * k - 1
+                        if m >= 1:
+                            total = total + rows(s, p, GAIN_ROW + q * PAIRS + k) * pairs[s, p, q, m]
+                value[s, p] = total + pltpu.roll(total, HALF, 1)
+        for s in range(2):
+            packed[s] = jnp.where(low, value[s, 0], value[s, 1])
+        packed[1] = PENALTY * packed[1]
+        input_ref[n] = gather_packed(jnp.where(is_box, packed[1], packed[0]), at)
+        if n < STEPS - 1:
+            for s in range(2):
+                for p in range(2):
+                    for q in range(SLOTS):
+                        got = gather_packed(packed[1 - s], index[s, p, q])
+                        pairs[s, p, q, n] = jnp.where(low, got, last.get((s, p, q), zero))
+                        last[s, p, q] = got
+    input_ref[0] = zero
+    for c in range(3):
+        spread_ref[c] = jnp.where(
+            key_ref[c * LANES : (c + 1) * LANES] == lane_key_ref[...], 1.0, 0.0
+        ).astype(jnp.bfloat16)
+    side = side_ref[...]
+    for n in range(NODES):
+        x_ref[n] = zero[:3]
+        h_ref[n] = zero[:3]
+        y_ref[n] = zero[:3]
+    node_row = lax.broadcasted_iota(jnp.int32, (LANES, LANES), 0)
+
+    def step(moment, _):
+        drive = time_ref[moment]
+        inputs = input_ref[moment]
+        kick = jnp.zeros((LANES, 3 * LANES), jnp.float32)
+        for c in range(3):
+            chosen = jnp.where(node_row == node_ref[c : c + 1], inputs[c : c + 1], 0.0)
+            for _ in range(3):
+                part = chosen.astype(jnp.bfloat16)
+                kick = kick + jnp.dot(part, spread_ref[c], preferred_element_type=jnp.float32)
+                chosen = chosen - part.astype(jnp.float32)
+        for c in range(3):
+            kick_ref[c * LANES : (c + 1) * LANES] = kick[:, c * LANES : (c + 1) * LANES]
+        extra = partner_faces(lambda k: y_ref[k], side)
+        for n in range(NODES):
+            assembled = y_ref[n] if extra[n] is None else y_ref[n] + extra[n]
+            inverse = data_ref[1, n]
+            damp = data_ref[3, n]
+            x = x_ref[n]
+            h = h_ref[n]
+            arrived = kick_ref[pl.ds(n, 3, stride=LANES)]
+            dx = damp * x
+            advanced = 2.0 * x - h + inverse * (drive * data_ref[2, n] - assembled - dx + arrived)
+            h_ref[n] = x - inverse * dx
+            flat_ref[pl.ds(n, 3, stride=LANES)] = x
+            x_ref[n] = advanced
+        stiffness_lines(x_ref, data_ref.at[0], y_ref)
+        return 0
+
+    lax.fori_loop(0, STEPS, step, 0)
+    linked = jnp.where(
+        home_ref[...] == lax.broadcasted_iota(jnp.int32, (LANES, 2 * LANES), 0), 1.0, 0.0
+    ).astype(jnp.bfloat16)
+    alone = home_ref[...] < 0
+
+    def put(out_ref):
+        rest = flat_ref[0:LANES]
+        moved = jnp.zeros((LANES, 2 * LANES), jnp.float32)
+        for _ in range(3):
+            part = rest.astype(jnp.bfloat16)
+            moved = moved + jnp.dot(part, linked, preferred_element_type=jnp.float32)
+            rest = rest - part.astype(jnp.float32)
+        for g in range(2):
+            own = flat_ref[(g + 1) * LANES : (g + 2) * LANES]
+            cut = slice(g * LANES, (g + 1) * LANES)
+            merged = jnp.where(alone[:, cut], own, moved[:, cut])
+            out_ref[:, cut] = merged[:NODES]
+
+    put(before_ref)
+    for n in range(NODES):
+        flat_ref[pl.ds(n, 3, stride=LANES)] = x_ref[n]
+    put(now_ref)
+
+
+def fast_body(wave_speed, inverse_mass, source_field, source_time, face_links, coupling_links):
+    _, weight_np, _ = node_tables()
+    blocks = lax.axis_size("blk")
+    bits = blocks.bit_length() - 1
+    me = lax.axis_index("blk")
+    sec = lax.axis_index("sec")
+    is_box = sec == 0
+    columns = wave_speed.shape[-1]
+    records = face_links.shape[-1]
+    per_peer = records // 8
+    offsets = [0] + [1 << j for j in range(bits)]
+
+    live = coupling_links[:, : CAPC * blocks]
+    owner = live[2]
+    ordinal = jnp.arange(HALF)
+    rank = jnp.sum(
+        ((owner[:, None] == owner[None, :]) & (ordinal[None, :] < ordinal[:, None])).astype(jnp.int32),
+        axis=1,
+    )
+    slot = jnp.where(owner >= 0, owner * CAPC + rank, -1)
+    to_slot = (slot[:, None] == ordinal[None, :]).astype(jnp.float32)
+    named = (jnp.stack([live[0], live[1], live[3], live[4]]) + 1).astype(jnp.float32)
+    links = jnp.dot(named, to_slot, precision=EXACT)
+    everyone = lax.all_to_all(
+        jnp.broadcast_to(links[None], (blocks, 4, HALF)), "blk", 0, 0, tiled=True
+    )
+
+    face_element, face_side, face_peer = face_links[0, 0], face_links[0, 1], face_links[0, 2]
+    count = jnp.arange(records)
+    linked = face_peer != me
+    face_rank = jnp.sum(
+        ((face_peer[:, None] == face_peer[None, :]) & (count[None, :] < count[:, None])).astype(jnp.int32),
+        axis=1,
+    )
+    distance = jnp.bitwise_xor(face_peer, me)
+    bit = sum([j * (distance == 1 << j).astype(jnp.int32) for j in range(bits)])
+    face_slot = jnp.where(linked, bit * per_peer + face_rank, -1)
+    to_record = (face_slot[:, None] == ordinal[None, :]).astype(jnp.float32)
+    record = jnp.dot(
+        (jnp.stack([face_element, face_side]) + 1).astype(jnp.float32), to_record, precision=EXACT
+    )
+
+    own_nodes = (jnp.arange(128)[:, None] + 1).astype(jnp.float32) == links[1][None, :]
+    own_cols = links[0][:, None] == (jnp.arange(columns)[None, :] + 1).astype(jnp.float32)
+    points_at = jnp.dot(own_nodes.astype(jnp.float32), own_cols.astype(jnp.float32), precision=EXACT)
+    damping = jnp.where(is_box, PENALTY, 0.0) * points_at
+
+    def padded(field):
+        return jnp.concatenate([field, jnp.zeros((3, columns), jnp.float32)], axis=0)
+
+    fields = jnp.stack(
+        [
+            padded(jnp.asarray(weight_np) * wave_speed[0]),
+            padded(DT_SQUARED * inverse_mass[0]),
+            padded(source_field[0]),
+            damping,
+        ]
+    )
+    take_linked = (record[0][:, None] == (jnp.arange(columns)[None, :] + 1).astype(jnp.float32)).astype(
+        jnp.float32
+    )
+    mine = lax.dot_general(
+        take_linked, fields.reshape(512, columns), (((1,), (1,)), ((), ())), precision=EXACT
+    )
+    mine = mine.at[:, 125].set(record[0]).at[:, 126].set(record[1])
+    ghost = jnp.concatenate(
+        [
+            partner_2(mine[j * per_peer : (j + 1) * per_peer], "blk", j)
+            for j in range(bits)
+        ],
+        axis=0,
+    )
+    partner_record = ghost[:, 125:127].T
+    wide = jnp.concatenate([mine, ghost], axis=0).T.reshape(4, 128, 128)
+    home = jnp.concatenate([wide, fields], axis=2)
+
+    box_table = everyone[:, 0:2]
+    global_table = (
+        everyone[:, 2:4].reshape(blocks, 2, blocks, CAPC).transpose(2, 1, 0, 3).reshape(blocks, 2, HALF)
+    )
+    table = jnp.where(is_box, box_table, global_table)
+    peers = jnp.bitwise_xor(jnp.asarray(offsets, jnp.int32), me)
+    near = table[peers]
+    element_1 = near[:, 0].reshape(-1)
+    node_1 = near[:, 1].reshape(-1)
+    where_from = jnp.repeat(jnp.arange(bits + 1), HALF)
+    valid = node_1 > 0
+    key = jnp.where(valid, where_from * columns + element_1.astype(jnp.int32) - 1, -1)
+    within = jnp.arange((bits + 1) * HALF) % HALF
+    gid = within // CAPC * HALF + jnp.repeat(peers, HALF) * CAPC + within % CAPC
+
+    point_element = near[0, 0]
+    point_node = near[0, 1].astype(jnp.int32) - 1
+    of_column = (
+        (jnp.arange(columns)[:, None] + 1).astype(jnp.float32) == point_element[None, :]
+    ).astype(jnp.float32)
+    of_record = (
+        (record[0][:, None] == point_element[None, :]) & (point_element[None, :] > 0)
+    ).astype(jnp.float32)
+    own_part = jnp.dot(fields.reshape(512, columns), of_column, precision=EXACT)
+    partner_part = jnp.dot(ghost.T, of_record, precision=EXACT)
+    copies = jnp.concatenate([own_part, partner_part], axis=1).reshape(4, 128, 1, 128)[:, :NODES]
+    record_key = jnp.where(
+        partner_record[0] > 0,
+        (1 + jnp.arange(bits * per_peer) // per_peer) * columns + partner_record[0].astype(jnp.int32) - 1,
+        0,
+    )
+    facts = jnp.stack([record[1], partner_record[1], record_key.astype(jnp.float32)])
+    facts = jnp.dot(facts, of_record, precision=EXACT)
+    copy_side = jnp.concatenate([facts[0], facts[1]]).astype(jnp.int32) - 1
+    copy_side = jnp.broadcast_to(copy_side[None], (8, LANES))
+    copy_side = jnp.where(jnp.arange(8)[:, None] < 2, copy_side, -1)
+    ghost_key = jnp.where(facts[1] > 0, facts[2].astype(jnp.int32), -5)
+    own_key = jnp.where(point_element > 0, point_element.astype(jnp.int32) - 1, -5)
+    match = (key[:, None] == own_key[None, :]) | (key[:, None] == ghost_key[None, :])
+    matched = match.astype(jnp.float32)
+    lower = jnp.asarray(np.tril(np.ones((key.shape[0],) * 2, np.float32), -1))
+    place = jnp.dot(lower, matched, precision=EXACT)
+    picked = jnp.stack([match & (place == q) for q in range(SLOTS)], axis=1).astype(jnp.float32)
+    described = jnp.stack([node_1, gid.astype(jnp.float32), (where_from > 0).astype(jnp.float32)])
+    lists = jnp.dot(
+        described, picked.reshape(key.shape[0], SLOTS * HALF), precision=EXACT
+    ).reshape(3, SLOTS, HALF)
+    list_node = lists[0].astype(jnp.int32) - 1
+    on_partner = lists[2] > 0
+    wanted = jnp.concatenate(
+        [jnp.where(on_partner, -1, list_node), jnp.where(on_partner, list_node, -1)], axis=1
+    )
+    own_row = jnp.concatenate([point_node, jnp.full((HALF,), -1, jnp.int32)])[None]
+    wanted = jnp.concatenate([wanted, own_row, jnp.full((1, LANES), -1, jnp.int32)], axis=0)
+    too_long = jnp.max(jnp.sum(matched, axis=0)) > SLOTS
+    index_rows = jnp.concatenate(
+        [
+            lists[1].reshape(SLOTS // 2, LANES),
+            jnp.full((1, LANES), 1.0, jnp.float32) * too_long.astype(jnp.float32),
+        ],
+        axis=0,
+    )
+    unit = (
+        jnp.arange(NODES)[:, None]
+        == jnp.concatenate([point_node, jnp.full((HALF,), -1, jnp.int32)])[None, :]
+    ).astype(jnp.float32)[:, None, :]
+    late = (jnp.arange(STEPS) > 0).astype(jnp.float32)
+    box_f = is_box.astype(jnp.float32)
+    coef = jnp.stack(
+        [
+            source_time[0],
+            late,
+            jnp.where(late > 0, -1.0, box_f),
+            jnp.where(late > 0, 0.0, 1.0 - box_f),
+            jnp.full((STEPS,), 1.0, jnp.float32) * box_f,
+        ]
+    )
+    vmem = pl.BlockSpec(memory_space=pltpu.VMEM)
+    smem = pl.BlockSpec(memory_space=pltpu.SMEM)
+    full = pltpu.VMEM((NODES, 8, LANES), jnp.float32)
+    payload = pl.pallas_call(
+        response_kernel,
+        out_shape=jax.ShapeDtypeStruct((blocks, PAYLOAD, LANES), jnp.float32),
+        in_specs=[smem] + [vmem] * 5,
+        out_specs=vmem,
+        scratch_shapes=[full] * 7 + [pltpu.VMEM((STEPS, 8, LANES), jnp.float32)],
+    )(coef, copies, copy_side, unit, wanted, index_rows)
+
+    same_core = [[c + 2 * i for i in range(blocks)] for c in range(2)]
+    received = lax.all_to_all(
+        payload, ("sec", "blk"), 0, 0, axis_index_groups=same_core, tiled=True
+    )
+    sibling = partner_2(received, "blk", 0)
+    overflow = jnp.max(
+        jnp.maximum(received[:, FLAG_ROW, 0], sibling[:, FLAG_ROW, 0])
+    ) > 0
+
+    fill = 3 * LANES - key.shape[0]
+
+    def extend(values, rest):
+        return jnp.concatenate([values, jnp.full((fill,), rest, jnp.int32)])
+
+    at = jnp.zeros((8, LANES), jnp.int32).at[0:3].set(extend(gid, 0).reshape(3, LANES))
+    point_rows = extend(node_1.astype(jnp.int32) - 1, -1).reshape(3, LANES)
+    key_column = extend(key, -1)[:, None]
+    own_record_key = jnp.where(record[0] > 0, record[0].astype(jnp.int32) - 1, -3)
+    ghost_record_key = jnp.where(partner_record[0] > 0, record_key, -3)
+    lane_key = jnp.concatenate([own_record_key, ghost_record_key, jnp.arange(columns)])[None]
+    home_lane = jnp.dot(
+        (jnp.arange(HALF)[None] + 1).astype(jnp.float32), take_linked, precision=EXACT
+    ).astype(jnp.int32) - 1
+    home_side = jnp.full((3, LANES), -1, jnp.int32)
+    home_side = home_side.at[0].set(
+        jnp.concatenate([record[1], partner_record[1]]).astype(jnp.int32) - 1
+    )
+    home = home[:, :NODES].reshape(4, NODES, 3, LANES)
+    where_am_i = jnp.stack([sec, me % 2]).astype(jnp.int32)
+    three = pltpu.VMEM((NODES, 3, LANES), jnp.float32)
+
+    def quick(_):
+        return tuple(pl.pallas_call(
+            final_kernel,
+            out_shape=[jax.ShapeDtypeStruct((NODES, columns), jnp.float32)] * 2,
+            in_specs=[smem] * 2 + [vmem] * 9,
+            out_specs=[vmem] * 2,
+            scratch_shapes=[
+                pltpu.VMEM((2, blocks, PAYLOAD, LANES), jnp.float32),
+                pltpu.VMEM((3, LANES, 3 * LANES), jnp.bfloat16),
+                pltpu.VMEM((STEPS, 8, LANES), jnp.float32),
+                three,
+                three,
+                three,
+                pltpu.VMEM((3 * LANES, LANES), jnp.float32),
+                pltpu.VMEM((3 * LANES, LANES), jnp.float32),
+            ],
+        )(
+            where_am_i,
+            source_time[0],
+            received,
+            sibling,
+            home,
+            home_side,
+            at,
+            point_rows,
+            key_column,
+            lane_key,
+            home_lane,
+        ))
+
+    def slow(_):
+        now, before = general_body(
+            wave_speed, inverse_mass, source_field, source_time, face_links, coupling_links
+        )
+        return (now[0], before[0])
+
+    now, before = lax.cond(overflow, slow, quick, 0)
+    return (now[None], before[None])
+
+
+def body(*arguments):
+    wave_speed, _, _, _, face_links, coupling_links = arguments
+    fits = (
+        lax.axis_size("blk") == 16
+        and lax.axis_size("sec") == 2
+        and wave_speed.shape[1:] == (NODES, 2 * LANES)
+        and face_links.shape[-1] == LANES
+        and coupling_links.shape[-1] >= CAPC * 16
+    )
+    return fast_body(*arguments) if fits else general_body(*arguments)
 
 
 def solution(mesh):

time: 1420 us -> 112 us (0.08)
  other arithmetic: 1000 us -> 10 us
  local copies, waits for them, and re-layouts: 181 us -> 17.8 us
  starting transfers between devices: 102 us -> 20 us
  waiting for transfers between devices: 95.3 us -> 15.8 us
  Pallas kernels: 0 us -> 42.5 us
  matrix products: 23.9 us -> 3.18 us
    scatter-add x51 -> x0, other arithmetic: 511 us -> none  [the longest x12 361 us: body(): driving = driving.at[target_rows, target_cols].add(values)]
    select_n x86 -> x10, other arithmetic: 482 us -> 1.45 us  [the longest x1 0.7 us: fast_body(): slot = jnp.where(owner >= 0, owner * CAPC + rank, -1)]
    gather x108 -> x1, local copies, waits for them, and re-layouts: 160 us -> 0.57 us  [fast_body(): near = table[peers]]
    all_to_all x13 -> x2, waiting for transfers between devices: 67.6 us -> 11 us  [the longest x1 11 us: fast_body(): lax.all_to_all(payload, ('sec', 'blk'), 0, 0, axis_index_groups=same_core...]
    all_to_all x13 -> x2, starting transfers between devices: 61.4 us -> 14.1 us  [the longest x1 7.36 us: fast_body(): lax.all_to_all(jnp.broadcast_to(links[None], (blocks, 4, HALF)), 'blk', 0...]
    pallas_call x0 -> x2, Pallas kernels: none -> 42.5 us  [the longest x1 24.8 us: quick(): pl.pallas_call(final_kernel, out_shape=[jax.ShapeDtypeStruct((NODES, colu...]
    ppermute x60 -> x5, starting transfers between devices: 40.2 us -> 5.92 us  [partner_2(): lax.ppermute(value, axis, [(i, i ^ 1 << stride) for i in range(lax.axis_s...]
    ppermute x60 -> x5, waiting for transfers between devices: 27.7 us -> 4.82 us  [partner_2(): lax.ppermute(value, axis, [(i, i ^ 1 << stride) for i in range(lax.axis_s...]
  transfers between devices with their start and end apart: 73 -> 7, of which waited for: 37 -> 3; matrix products, arithmetic and copies ran while one was open for 6% -> 10% of each run, Pallas kernels for 0% -> 0%
where the time goes in v1:
time: 112 us
  Pallas kernels  42.5 us (38%)
  starting transfers between devices  20 us (18%)
  local copies, waits for them, and re-layouts  17.8 us (16%)
  waiting for transfers between devices  15.8 us (14%)
  other arithmetic  10 us (9%)
  matrix products  3.18 us (3%)
  between operations  2.35 us (2%)
    pallas_call x1, Pallas kernels, quick(): pl.pallas_call(final_kernel, out_shape=[jax.ShapeDtypeStruct((NODES, colu...  24.8 us
    pallas_call x1, Pallas kernels, fast_body(): pl.pallas_call(response_kernel, out_shape=jax.ShapeDtypeStruct((blocks, P...  17.8 us
    all_to_all x1, waiting for transfers between devices, fast_body(): lax.all_to_all(payload, ('sec', 'blk'), 0, 0, axis_index_groups=same_core...  11 us
    all_to_all x1, starting transfers between devices, fast_body(): lax.all_to_all(jnp.broadcast_to(links[None], (blocks, 4, HALF)), 'blk', 0...  7.36 us
    all_to_all x1, starting transfers between devices, fast_body(): lax.all_to_all(payload, ('sec', 'blk'), 0, 0, axis_index_groups=same_core...  6.76 us
    ppermute x5, starting transfers between devices, partner_2(): lax.ppermute(value, axis, [(i, i ^ 1 << stride) for i in range(lax.axis_s...  5.92 us
    unnamed x33, local copies, waits for them, and re-layouts  5.66 us
    ppermute x5, waiting for transfers between devices, partner_2(): lax.ppermute(value, axis, [(i, i ^ 1 << stride) for i in range(lax.axis_s...  4.82 us
  transfers between devices with their start and end apart: 7, of which 3 were waited for; matrix products, arithmetic and copies ran while one was open for 10% of the time, Pallas kernels for 0%

profile of v1, /device:TPU:0, one launch (start us, length us, event | category | flops | bytes accessed | tf_op | source)
XLA Modules:
  0.0 111.7 jit_solution(12063543588489501755)
XLA Ops:
  1.3 0.8 fusion.150
  2.3 0.7 compare_select_fusion.23
  3.2 0.7 reshape.1166
  3.9 7.4 %all-to-all-start.2 = ((f32[16,1,256]{2,1,0:T(1,128)}), f32[16,1,256]{2,1,0:T(1,128)S(1)}, u32[]{:S(2)}, u32[]{:S(2)}) async-start(f32[16,1,256]{2,1,0:T(1,128)} %reshape.1166), calls=%async_computation.2 | async-start | bytes 32768 | tf_op jit(solution)/shard_map/all_to_all | solution.py:546
  11.9 0.7 compare_reduce_fusion.1
  14.5 0.9 copy-done.4
  15.4 0.9 copy-done.3
  18.5 1.0 fusion.149
  19.9 2.6 %collective-permute-start.8 = (f32[16,512]{0,1:T(8,128)}, f32[16,512]{0,1:T(8,128)S(1)}, u32[]{:S(2)}, u32[]{:S(2)}) collective-permute-start(f32[16,512]{0,1:T(8,128)} %get-tuple-element.868), channel_id=1, source_target_pairs={{0,8},{1,9},{2,10},{3,11},{4,12},{5,13},{6,14},{7,15},{8,0},{9,1},... | collective-permute-start | bytes 98312 | tf_op jit(solution)/shard_map/ppermute | solution.py:18
  22.5 1.5 %collective-permute-start.7 = (f32[16,512]{0,1:T(8,128)S(1)}, f32[16,512]{0,1:T(8,128)S(1)}, u32[]{:S(2)}, u32[]{:S(2)}) collective-permute-start(f32[16,512]{0,1:T(8,128)S(1)} %get-tuple-element.869), channel_id=1, source_target_pairs={{0,4},{1,5},{2,6},{3,7},{4,0},{5,1},{6,2},{7,3},{8,12},{9,13},{10,... | collective-permute-start | bytes 98312 | tf_op jit(solution)/shard_map/ppermute | solution.py:18
  23.9 1.5 %collective-permute-start.6 = (f32[16,512]{0,1:T(8,128)S(1)}, f32[16,512]{0,1:T(8,128)S(1)}, u32[]{:S(2)}, u32[]{:S(2)}) collective-permute-start(f32[16,512]{0,1:T(8,128)S(1)} %get-tuple-element.870), channel_id=1, source_target_pairs={{0,2},{1,3},{2,0},{3,1},{4,6},{5,7},{6,4},{7,5},{8,10},{9,11},{10,... | collective-permute-start | bytes 98312 | tf_op jit(solution)/shard_map/ppermute | solution.py:18
  31.5 3.6 %collective-permute-done.8 = f32[16,512]{0,1:T(8,128)S(1)} collective-permute-done((f32[16,512]{0,1:T(8,128)}, f32[16,512]{0,1:T(8,128)S(1)}, u32[]{:S(2)}, u32[]{:S(2)}) %collective-permute-start.8) | collective-permute-done | bytes 32800 | tf_op jit(solution)/shard_map/ppermute | solution.py:18
  37.7 0.7 slice.454.data_ref
  41.7 17.8 %shard_map.140 = f32[16,40,128]{2,1,0:T(8,128)} custom-call(f32[5,12]{1,0:T(8,128)} %stack.68.coef_ref, f32[4,125,1,128]{3,2,1,0:T(1,128)} %slice.454.data_ref, s32[8,128]{1,0:T(8,128)} %broadcast_select_fusion.8.side_ref, f32[125,1,128]{2,1,0:T(1,128)} %compare_convert_fusion.1.start_ref, s32[8,128]{1,0:T(8,128)} %pad_add_fusion.2.list_ref, ...), custom_call_target="tpu_custom_call" | custom-call | tf_op jit(solution)/shard_map/pallas_call | solution.py:679
  59.5 6.8 %all-to-all-start.3 = ((f32[16,40,128]{2,1,0:T(8,128)}), f32[16,40,128]{2,1,0:T(8,128)S(1)}, u32[]{:S(2)}, u32[]{:S(2)}) async-start(f32[16,40,128]{2,1,0:T(8,128)} %shard_map.140), calls=%async_computation.3 | async-start | bytes 655360 | tf_op jit(solution)/shard_map/all_to_all | solution.py:688
  66.8 11.0 %all-to-all-done.3 = f32[16,40,128]{2,1,0:T(8,128)S(1)} async-done(((f32[16,40,128]{2,1,0:T(8,128)}), f32[16,40,128]{2,1,0:T(8,128)S(1)}, u32[]{:S(2)}, u32[]{:S(2)}) %all-to-all-start.3) | async-done | bytes 327712 | tf_op jit(solution)/shard_map/all_to_all | solution.py:688
  78.4 1.2 %collective-permute-done.9 = f32[16,40,128]{2,1,0:T(8,128)} collective-permute-done((f32[16,40,128]{2,1,0:T(8,128)S(1)}, f32[16,40,128]{2,1,0:T(8,128)}, u32[]{:S(2)}, u32[]{:S(2)}) %collective-permute-start.9) | collective-permute-done | bytes 327712 | tf_op jit(solution)/shard_map/ppermute | solution.py:18
  79.6 1.5 %fusion.73 = f32[]{:T(128)} fusion(f32[16,40,128]{2,1,0:T(8,128)} %collective-permute-done.9, f32[16,40,128]{2,1,0:T(8,128)S(1)} %all-to-all-done.3), kind=kLoop, calls=%fused_computation.183 | loop fusion | flops 31 | bytes 132 | tf_op jit(solution)/shard_map/reduce_max | solution.py:692
  82.3 29.4 %conditional.1 = (f32[1,125,256]{2,0,1:T(1,128)}, f32[1,125,256]{2,0,1:T(1,128)}) conditional(s32[]{:T(128)} %convert_element_type.239, (f32[1,12]{1,0:T(1,128)S(1)}, s32[2]{0:T(128)S(1)}, f32[16,40,128]{2,1,0:T(8,128)S(1)}, f32[16,40,128]{2,1,0:T(8,128)}, f32[4,125,3,128]{1,3,2,0:T(8,128)S(1)}, /*index=5*/s32[3,128]{1,0:T(4,128)S(1)}, ...), branch_computations={%region_7.8_spmd, %region_8.21_spmd} | conditional | flops 347599744 | bytes 8484523 | solution.py:754
  82.3 0.8 copy.121.key_ref
  83.2 1.3 %copy.120.data_ref = f32[4,125,3,128]{3,2,1,0:T(4,128)} copy(f32[4,125,3,128]{1,3,2,0:T(8,128)S(1)} %get-tuple-element.695) | data formatting | bytes 1536000 | tf_op jit(solution)/shard_map
  84.5 24.8 %branch_0_fun.1 = (f32[125,256]{1,0:T(8,128)}, f32[125,256]{1,0:T(8,128)}) custom-call(s32[2]{0:T(128)S(1)} %get-tuple-element.461.where_ref, f32[12]{0:T(128)S(1)} %bitcast.486, f32[16,40,128]{2,1,0:T(8,128)S(1)} %get-tuple-element.463.mine_ref, f32[16,40,128]{2,1,0:T(8,128)} %get-tuple-element.464.other_ref, f32[4,125,3,128]{3,2,1,0:T(4,128)} %copy.120.data_ref, ...), custom_call_target="tpu_custom_call" | custom-call | tf_op jit(solution)/shard_map/cond/branch_0_fun/pallas_call | solution.py:719
  109.3 1.7 %broadcast_in_dim.301 = f32[1,125,256]{2,0,1:T(1,128)} reshape(f32[125,256]{1,0:T(8,128)} %get-tuple-element.712) | data formatting | bytes 256000 | tf_op jit(solution)/shard_map/broadcast_in_dim | solution.py:755
  111.0 0.7 broadcast_in_dim.303
  (146 shorter events, 19.0 us)
Async XLA Ops:
  3.0 10.8 %copy-start.6 = (f32[1,125,256]{2,0,1:T(1,128)S(1)}, f32[1,125,256]{2,0,1:T(1,128)}, u32[]{:S(2)}) copy-start(f32[1,125,256]{2,0,1:T(1,128)} %param.25) | copy-start | bytes 384004
  3.9 23.9 %all-to-all-start.2 = ((f32[16,1,256]{2,1,0:T(1,128)}), f32[16,1,256]{2,1,0:T(1,128)S(1)}, u32[]{:S(2)}, u32[]{:S(2)}) async-start(f32[16,1,256]{2,1,0:T(1,128)} %reshape.1166), calls=%async_computation.2 | async-start | bytes 32768 | tf_op jit(solution)/shard_map/all_to_all | solution.py:546
  12.6 0.7 copy-start.12
  13.7 0.7 copy-start.14
  14.5 0.9 copy-start.4
  15.4 0.9 copy-start.3
  19.5 12.0 %collective-permute-start.5 = (f32[16,512]{0,1:T(8,128)}, f32[16,512]{0,1:T(8,128)S(1)}, u32[]{:S(2)}, u32[]{:S(2)}) collective-permute-start(f32[16,512]{0,1:T(8,128)} %get-tuple-element.867), channel_id=1, source_target_pairs={{0,1},{1,0},{2,3},{3,2},{4,5},{5,4},{6,7},{7,6},{8,9},{9,8},{10,11... | collective-permute-start | bytes 98312 | tf_op jit(solution)/shard_map/ppermute | solution.py:18
  19.9 15.2 %collective-permute-start.8 = (f32[16,512]{0,1:T(8,128)}, f32[16,512]{0,1:T(8,128)S(1)}, u32[]{:S(2)}, u32[]{:S(2)}) collective-permute-start(f32[16,512]{0,1:T(8,128)} %get-tuple-element.868), channel_id=1, source_target_pairs={{0,8},{1,9},{2,10},{3,11},{4,12},{5,13},{6,14},{7,15},{8,0},{9,1},... | collective-permute-start | bytes 98312 | tf_op jit(solution)/shard_map/ppermute | solution.py:18
  22.5 12.7 %collective-permute-start.7 = (f32[16,512]{0,1:T(8,128)S(1)}, f32[16,512]{0,1:T(8,128)S(1)}, u32[]{:S(2)}, u32[]{:S(2)}) collective-permute-start(f32[16,512]{0,1:T(8,128)S(1)} %get-tuple-element.869), channel_id=1, source_target_pairs={{0,4},{1,5},{2,6},{3,7},{4,0},{5,1},{6,2},{7,3},{8,12},{9,13},{10,... | collective-permute-start | bytes 98312 | tf_op jit(solution)/shard_map/ppermute | solution.py:18
  23.9 11.2 %collective-permute-start.6 = (f32[16,512]{0,1:T(8,128)S(1)}, f32[16,512]{0,1:T(8,128)S(1)}, u32[]{:S(2)}, u32[]{:S(2)}) collective-permute-start(f32[16,512]{0,1:T(8,128)S(1)} %get-tuple-element.870), channel_id=1, source_target_pairs={{0,2},{1,3},{2,0},{3,1},{4,6},{5,7},{6,4},{7,5},{8,10},{9,11},{10,... | collective-permute-start | bytes 98312 | tf_op jit(solution)/shard_map/ppermute | solution.py:18
  25.4 0.7 copy-start.15
  26.5 0.7 copy-start.13
  31.5 4.2 %copy-start.8 = (f32[320,320]{1,0:T(8,128)S(1)}, f32[320,320]{1,0:T(8,128)}, u32[]{:S(2)}) copy-start(f32[320,320]{1,0:T(8,128)} %constant.389.clone) | copy-start | bytes 1228804
  59.5 18.3 %all-to-all-start.3 = ((f32[16,40,128]{2,1,0:T(8,128)}), f32[16,40,128]{2,1,0:T(8,128)S(1)}, u32[]{:S(2)}, u32[]{:S(2)}) async-start(f32[16,40,128]{2,1,0:T(8,128)} %shard_map.140), calls=%async_computation.3 | async-start | bytes 655360 | tf_op jit(solution)/shard_map/all_to_all | solution.py:688
  77.8 1.8 %collective-permute-start.9 = (f32[16,40,128]{2,1,0:T(8,128)S(1)}, f32[16,40,128]{2,1,0:T(8,128)}, u32[]{:S(2)}, u32[]{:S(2)}) collective-permute-start(f32[16,40,128]{2,1,0:T(8,128)S(1)} %all-to-all-done.3), channel_id=1, source_target_pairs={{0,1},{1,0},{2,3},{3,2},{4,5},{5,4},{6,7},{7,6},{8,9},{9,8},{10,11... | collective-permute-start | bytes 983048 | tf_op jit(solution)/shard_map/ppermute | solution.py:18
  77.9 3.8 %copy-start = (f32[375,125]{1,0:T(8,128)S(1)}, f32[375,125]{1,0:T(8,128)}, u32[]{:S(2)}) copy-start(f32[375,125]{1,0:T(8,128)} %constant.390.clone) | copy-start | bytes 562504
  77.9 3.8 %copy-start.1 = (f32[125,150]{1,0:T(8,128)S(1)}, f32[125,150]{1,0:T(8,128)}, u32[]{:S(2)}) copy-start(f32[125,150]{1,0:T(8,128)} %constant.392.clone) | copy-start | bytes 225004
  77.9 3.8 %copy-start.2 = (f32[150,125]{1,0:T(8,128)S(1)}, f32[150,125]{1,0:T(8,128)}, u32[]{:S(2)}) copy-start(f32[150,125]{1,0:T(8,128)} %constant.391.clone) | copy-start | bytes 225004
  77.9 3.8 %copy-start.5 = (f32[1,125,256]{2,0,1:T(1,128)S(1)}, f32[1,125,256]{2,0,1:T(1,128)}, u32[]{:S(2)}) copy-start(f32[1,125,256]{2,0,1:T(1,128)} %param.26) | copy-start | bytes 384004
  77.9 3.8 %copy-start.7 = (f32[1,125,256]{2,0,1:T(1,128)S(1)}, f32[1,125,256]{2,0,1:T(1,128)}, u32[]{:S(2)}) copy-start(f32[1,125,256]{2,0,1:T(1,128)} %param.25) | copy-start | bytes 384004
  78.3 3.5 %copy-start.11 = (s32[5,512]{1,0:T(8,128)S(1)}, s32[5,512]{1,0:T(8,128)}, u32[]{:S(2)}) copy-start(s32[5,512]{1,0:T(8,128)} %param.30) | copy-start | bytes 30724
  81.7 0.7 copy-start.10
  109.3 1.7 %copy-start.9 = (f32[125,256]{1,0:T(8,128)S(1)}, f32[125,256]{1,0:T(8,128)}, u32[]{:S(2)}) copy-start(f32[125,256]{1,0:T(8,128)} %get-tuple-element.713) | copy-start | bytes 384004 | tf_op jit(solution)/shard_map/cond

commit v2 on v1

--- a/solution.py
+++ b/solution.py
@@ -284,14 +284,197 @@
     return extra
 
 
+def across(row_values):
+    return jnp.broadcast_to(row_values, (LANES, LANES)).T
+
+
+def rank_among(row_values):
+    down = lax.broadcasted_iota(jnp.int32, (LANES, LANES), 0)
+    right = lax.broadcasted_iota(jnp.int32, (LANES, LANES), 1)
+    same = (across(row_values) == row_values) & (down < right)
+    return jnp.sum(jnp.where(same, 1.0, 0.0), axis=0, keepdims=True)
+
+
+def one_hot(condition):
+    return jnp.where(condition, 1.0, 0.0).astype(jnp.bfloat16)
+
+
+def plain_dot(a, b):
+    return jnp.dot(a.astype(jnp.bfloat16), b, preferred_element_type=jnp.float32)
+
+
+def exact_pick(values, chosen, transposed=False):
+    total = None
+    rest = values
+    for _ in range(3):
+        part = rest.astype(jnp.bfloat16)
+        if transposed:
+            got = lax.dot_general(
+                chosen, part, (((1,), (1,)), ((), ())), preferred_element_type=jnp.float32
+            )
+        else:
+            got = jnp.dot(part, chosen, preferred_element_type=jnp.float32)
+        total = got if total is None else total + got
+        rest = rest - part.astype(jnp.float32)
+    return total
+
+
+def lane_row():
+    return lax.broadcasted_iota(jnp.int32, (1, LANES), 1)
+
+
+def pack_kernel(
+    where_ref,
+    wave_ref,
+    mass_ref,
+    source_ref,
+    weight_ref,
+    face_ref,
+    couple_ref,
+    links_ref,
+    m0_ref,
+    m1_ref,
+    m2_ref,
+    m3_ref,
+    count_ref,
+):
+    me = where_ref[1]
+    me_f = me.astype(jnp.float32)
+    is_box = where_ref[0] == 0
+    down = lax.broadcasted_iota(jnp.int32, (LANES, LANES), 0)
+    right = lax.broadcasted_iota(jnp.int32, (LANES, LANES), 1)
+    right_f = right.astype(jnp.float32)
+    lane = lane_row()
+
+    live = couple_ref[:, 0:LANES].astype(jnp.float32)
+    owner = jnp.where(lane < HALF, live[2:3], -1.0)
+    slot = jnp.where(owner >= 0.0, owner * CAPC + rank_among(owner), -1.0)
+    to_slot = one_hot(across(slot) == right_f)
+    named = jnp.concatenate([live[0:2], live[3:5], jnp.full((4, LANES), -1.0)], axis=0) + 1.0
+    links = plain_dot(named, to_slot)
+    for k in range(links_ref.shape[0]):
+        links_ref[k] = links
+
+    faces = face_ref[0]
+    peer = faces[2:3]
+    linked = peer != me
+    distance = peer ^ me
+    bit = jnp.zeros((1, LANES), jnp.float32)
+    for j in range(1, 4):
+        bit = bit + jnp.where(distance == 1 << j, float(j), 0.0)
+    face_slot = jnp.where(linked, bit * 16.0 + rank_among(peer.astype(jnp.float32)), -1.0)
+    to_record = one_hot(across(face_slot) == right_f)
+    facts = jnp.concatenate([faces[0:2].astype(jnp.float32) + 1.0, jnp.zeros((6, LANES))], axis=0)
+    record = plain_dot(facts, to_record)
+
+    node_one = lax.broadcasted_iota(jnp.int32, (LANES, LANES), 0).astype(jnp.float32) + 1.0
+    own_nodes = one_hot(node_one == links[1:2])
+    point_column = across(links[0:1])
+    record_column = across(record[0:1])
+    side_column = across(record[1:2])
+    counts = []
+    taken = []
+    for g in range(2):
+        column_one = right_f + float(g * LANES + 1)
+        counts.append(
+            jnp.dot(own_nodes, one_hot(point_column == column_one), preferred_element_type=jnp.float32)
+        )
+        taken.append(one_hot(record_column == column_one)[:HALF])
+    count = jnp.concatenate(counts, axis=1) * jnp.where(is_box, 1.0, 0.0)
+    count_ref[...] = count
+    take = jnp.concatenate(taken, axis=1)
+    pad = jnp.zeros((LANES - NODES, 2 * LANES), jnp.float32)
+    stiff = jnp.concatenate([weight_ref[...] * wave_ref[0], pad], axis=0)
+    mass = jnp.concatenate([DT_SQUARED * mass_ref[0], pad], axis=0)
+    source = jnp.concatenate([source_ref[0], pad], axis=0)
+    first = exact_pick(stiff, take, True)
+    first = jnp.where(right[:HALF] == 125, record_column[:HALF], first)
+    first = jnp.where(right[:HALF] == 126, side_column[:HALF], first)
+    parts = [
+        first,
+        exact_pick(mass, take, True),
+        exact_pick(source, take, True),
+        lax.dot_general(
+            take,
+            count.astype(jnp.bfloat16),
+            (((1,), (1,)), ((), ())),
+            preferred_element_type=jnp.float32,
+        ),
+    ]
+    for j, out in enumerate((m0_ref, m1_ref, m2_ref, m3_ref)):
+        for k in range(4):
+            out[:, k * LANES : (k + 1) * LANES] = parts[k][16 * j : 16 * j + 16]
+
+
+def point_tables(where_ref, every_ref):
+    me = where_ref[1]
+    is_box = where_ref[0] == 0
+    lane = lane_row()
+    low = lane < HALF
+    blocks = every_ref.shape[0]
+    down = lax.broadcasted_iota(jnp.int32, (blocks, LANES), 0)
+    right = lax.broadcasted_iota(jnp.int32, (blocks, LANES), 1)
+    mine = right // CAPC == down
+    tables = []
+    for offset in (0, 1, 2, 4, 8):
+        beta = me ^ offset
+        at = beta * CAPC + right % CAPC
+        rows = []
+        for f in range(2):
+            direct = every_ref[beta, f : f + 1, :]
+            column = every_ref[:, 2 + f, :]
+            picked = jnp.concatenate(
+                [
+                    jnp.take_along_axis(column[8 * h : 8 * h + 8], at[8 * h : 8 * h + 8], axis=1,
+                                        mode="promise_in_bounds")
+                    for h in range(blocks // 8)
+                ],
+                axis=0,
+            )
+            turned = jnp.sum(jnp.where(mine, picked, 0.0), axis=0, keepdims=True)
+            row = jnp.where(is_box, direct, turned)
+            rows.append(jnp.where(low, row, 0.0))
+        inputs = lane // CAPC * HALF + beta * CAPC + lane % CAPC
+        rows.append(jnp.where(low, inputs, 0).astype(jnp.float32))
+        tables.append(rows)
+    tables.append([jnp.zeros((1, LANES), jnp.float32)] * 3)
+    chunks = []
+    for c in range(3):
+        chunks.append(
+            [
+                jnp.where(low, tables[2 * c][f], pltpu.roll(tables[2 * c + 1][f], HALF, 1))
+                for f in range(3)
+            ]
+        )
+    keys = []
+    for c in range(3):
+        table = jnp.where(low, float(2 * c), float(2 * c + 1))
+        element, node, _ = chunks[c]
+        keys.append(jnp.where(node > 0.0, table * 256.0 + element - 1.0, -1.0))
+    return chunks, keys
+
+
 def response_kernel(
+    where_ref,
     coef_ref,
+    wave_ref,
+    mass_ref,
+    source_ref,
+    weight_ref,
+    count_ref,
+    m0_ref,
+    m1_ref,
+    m2_ref,
+    m3_ref,
+    g0_ref,
+    g1_ref,
+    g2_ref,
+    g3_ref,
+    every_ref,
+    out_ref,
+    pair_ref,
+    note_ref,
     data_ref,
-    side_ref,
-    start_ref,
-    list_ref,
-    index_ref,
-    out_ref,
     scale_ref,
     x_ref,
     h_ref,
@@ -301,37 +484,151 @@
     rec_ref,
     seen_ref,
 ):
+    down = lax.broadcasted_iota(jnp.int32, (LANES, LANES), 0)
+    right = lax.broadcasted_iota(jnp.int32, (LANES, LANES), 1)
+    right_f = right.astype(jnp.float32)
+    lane = lane_row()
+    lane_low = lane < HALF
+    lane_f = lane.astype(jnp.float32)
+
+    stacked = jnp.concatenate(
+        [r[...] for r in (m0_ref, m1_ref, m2_ref, m3_ref, g0_ref, g1_ref, g2_ref, g3_ref)], axis=0
+    )
+    pair = [stacked[:, k * LANES : (k + 1) * LANES].T for k in range(4)]
+    for k in range(4):
+        pair_ref[k] = pair[k]
+    pair_element = pair[0][125:126]
+    pair_side = pair[0][126:127]
+    own_column = jnp.broadcast_to(stacked[:HALF, 125:126], (HALF, LANES))
+    own_column = jnp.concatenate([own_column, own_column], axis=0)
+
+    chunks, keys = point_tables(where_ref, every_ref)
+    element, node, _ = chunks[0]
+    element_both = jnp.where(lane_low, element, pltpu.roll(element, HALF, 1))
+    node_low = jnp.where(lane_low, node, 0.0)
+    present = element_both > 0.0
+    same_half = (down < HALF) == (right < HALF)
+    of_record = (own_column == element_both) & present & same_half
+    facts_matrix = one_hot(of_record)
+    partner_matrix = one_hot(of_record & (down >= HALF))
+    table_row = jnp.where(lane_low, 0.0, (1 + (lane - HALF) // 16).astype(jnp.float32))
+    facts = plain_dot(
+        jnp.concatenate([pair_side, pair_element, table_row, jnp.zeros((5, LANES))], axis=0),
+        facts_matrix,
+    )
+    side_row = facts[0:1].astype(jnp.int32) - 1
+    partner = pltpu.roll(facts, HALF, 1)
+    ghost_key = jnp.where(partner[1:2] > 0.0, partner[2:3] * 256.0 + partner[1:2] - 1.0, -5.0)
+    own_key = jnp.where(element > 0.0, element - 1.0, -5.0)
+    own_key = jnp.where(lane_low, own_key, -5.0)
+    ghost_key = jnp.where(lane_low, ghost_key, -5.0)
+
+    match = [(across(keys[c]) == own_key) | (across(keys[c]) == ghost_key) for c in range(3)]
+    matched = [jnp.where(m, 1.0, 0.0) for m in match]
+    lower = one_hot(right < down)
+    before = jnp.zeros((1, LANES), jnp.float32)
+    lists = [jnp.zeros((8, LANES), jnp.float32)] * SLOTS
+    for c in range(3):
+        place = jnp.dot(lower, matched[c].astype(jnp.bfloat16), preferred_element_type=jnp.float32)
+        place = jnp.where(match[c], place + before, -1.0)
+        before = before + jnp.sum(matched[c], axis=0, keepdims=True)
+        _, node_c, gid_c = chunks[c]
+        gid_high = jnp.floor(gid_c * (1.0 / 256.0))
+        table_c = jnp.where(lane_low, float(2 * c), float(2 * c + 1))
+        described = jnp.concatenate(
+            [node_c, gid_high, gid_c - 256.0 * gid_high, table_c, jnp.zeros((4, LANES))], axis=0
+        )
+        for q in range(SLOTS):
+            lists[q] = lists[q] + plain_dot(described, one_hot(place == float(q)))
+    too_long = jnp.max(before) > float(SLOTS)
+    wanted_rows = []
+    gids = []
+    for q in range(SLOTS):
+        node_q = lists[q][0:1] - 1.0
+        there = lists[q][3:4] > 0.0
+        gids.append(lists[q][1:2] * 256.0 + lists[q][2:3])
+        wanted_rows.append(
+            jnp.where(
+                lane_low,
+                jnp.where(there, -1.0, node_q),
+                pltpu.roll(jnp.where(there, node_q, -1.0), HALF, 1),
+            )
+        )
+    own_node = jnp.where(lane_low, node - 1.0, -1.0)
+    wanted_rows.append(own_node)
+    wanted_rows.append(jnp.full((1, LANES), -1.0))
+    wanted = jnp.concatenate(wanted_rows, axis=0).astype(jnp.int32)
+
+    take = [
+        one_hot((down.astype(jnp.float32) + float(g * LANES + 1) == element_both) & (right < HALF))
+        for g in range(2)
+    ]
+    take = jnp.concatenate(take, axis=0)
+    own_fields = [
+        weight_ref[...] * wave_ref[0],
+        DT_SQUARED * mass_ref[0],
+        source_ref[0],
+        count_ref[...][:NODES],
+    ]
+    for k in range(4):
+        copy = exact_pick(own_fields[k], take) + exact_pick(pair[k], partner_matrix)[:NODES]
+        data_ref[k, 0:NODES] = PENALTY * copy if k == 3 else copy
+
+    home = []
+    for g in range(2):
+        hit = one_hot(own_column[:HALF] == right_f[:HALF] + float(g * LANES + 1))
+        home.append(
+            jnp.dot(
+                jnp.broadcast_to(lane_f[:, :HALF] + 1.0, (8, HALF)).astype(jnp.bfloat16),
+                hit,
+                preferred_element_type=jnp.float32,
+            )[0:1]
+            - 1.0
+        )
+    pair_key = jnp.where(pair_element > 0.0, table_row * 256.0 + pair_element - 1.0, -3.0)
+    notes = (
+        [chunks[c][2] for c in range(3)]
+        + [chunks[c][1] - 1.0 for c in range(3)]
+        + keys
+        + [pair_key, lane_f, lane_f + float(LANES)]
+        + [pair_side - 1.0]
+        + home
+        + [jnp.zeros((1, LANES), jnp.float32)]
+    )
+    note_ref[...] = jnp.concatenate(notes, axis=0)
+
     row = lax.broadcasted_iota(jnp.int32, (8, LANES), 0)
     low = lax.broadcasted_iota(jnp.int32, (8, LANES), 1) < HALF
     first = row == 0
-    side = side_ref[...]
-    wanted = list_ref[...]
+    side = jnp.where(row < 2, jnp.broadcast_to(side_row, (8, LANES)), -1)
     forced = row == SLOTS
     shape = (8, LANES)
-
-    def tile(ref, k, n):
-        return jnp.broadcast_to(ref[k, n], shape)
+    start_node = own_node.astype(jnp.int32)
+
+    def tile(k, n):
+        return jnp.broadcast_to(data_ref[k, n : n + 1], shape)
 
     for n in range(NODES):
-        x_ref[n] = jnp.where(row == 1, jnp.broadcast_to(start_ref[n], shape), 0.0)
+        x_ref[n] = jnp.where((row == 1) & (start_node == n), 1.0, 0.0)
         h_ref[n] = jnp.zeros(shape, jnp.float32)
         y_ref[n] = jnp.zeros(shape, jnp.float32)
-        scale_ref[n] = tile(data_ref, 0, n)
+        scale_ref[n] = tile(0, n)
+
+    is_box = jnp.where(where_ref[0] == 0, 1.0, 0.0)
 
     def step(moment, _):
         drive = coef_ref[0, moment]
-        keep = coef_ref[1, moment]
-        stiff = coef_ref[2, moment]
-        begin = coef_ref[3, moment]
-        is_box = coef_ref[4, 0]
+        keep = jnp.where(moment > 0, 1.0, 0.0)
+        stiff = jnp.where(moment > 0, -1.0, is_box)
+        begin = jnp.where(moment > 0, 0.0, 1.0 - is_box)
         for n in range(NODES):
             t_ref[n] = jnp.where(first, y_ref[n], x_ref[n])
         extra = partner_faces(lambda k: t_ref[k], side)
         for n in range(NODES):
             assembled = t_ref[n] if extra[n] is None else t_ref[n] + extra[n]
-            inverse = tile(data_ref, 1, n)
-            force = tile(data_ref, 2, n)
-            damp = tile(data_ref, 3, n)
+            inverse = tile(1, n)
+            force = tile(2, n)
+            damp = tile(3, n)
             x = x_ref[n]
             h = h_ref[n]
             advanced = 2.0 * x - h + inverse * (drive * force - assembled - damp * x)
@@ -340,8 +637,8 @@
         stiffness_lines(in_ref, scale_ref, y_ref)
         seen = jnp.zeros(shape, jnp.float32)
         for n in range(NODES):
-            inverse = tile(data_ref, 1, n)
-            damp = tile(data_ref, 3, n)
+            inverse = tile(1, n)
+            damp = tile(3, n)
             x = x_ref[n]
             h = h_ref[n]
             dx = damp * x
@@ -358,10 +655,9 @@
         return 0
 
     lax.fori_loop(0, STEPS, step, 0)
-    pair_low = lax.broadcasted_iota(jnp.int32, (1, LANES), 1) < HALF
     for k in range(FREE_ROWS):
         out_ref[0, k : k + 1] = jnp.where(
-            pair_low,
+            lane_low,
             seen_ref[2 * k][SLOTS : SLOTS + 1],
             seen_ref[2 * k + 1][SLOTS : SLOTS + 1],
         )
@@ -369,9 +665,12 @@
         for k in range(PAIRS):
             r = GAIN_ROW + q * PAIRS + k
             out_ref[0, r : r + 1] = jnp.where(
-                pair_low, seen_ref[2 * k][q : q + 1], seen_ref[2 * k + 1][q : q + 1]
+                lane_low, seen_ref[2 * k][q : q + 1], seen_ref[2 * k + 1][q : q + 1]
             )
-    out_ref[0, INDEX_ROW:PAYLOAD] = index_ref[...]
+    for q in range(0, SLOTS, 2):
+        r = INDEX_ROW + q // 2
+        out_ref[0, r : r + 1] = jnp.where(lane_low, gids[q], pltpu.roll(gids[q + 1], HALF, 1))
+    out_ref[0, FLAG_ROW : FLAG_ROW + 1] = jnp.full((1, LANES), jnp.where(too_long, 1.0, 0.0))
     for k in range(1, out_ref.shape[0]):
         out_ref[k] = out_ref[0]
 
@@ -392,18 +691,19 @@
     time_ref,
     mine_ref,
     other_ref,
-    data_ref,
-    side_ref,
-    at_ref,
-    node_ref,
-    key_ref,
-    lane_key_ref,
-    home_ref,
+    wave_ref,
+    mass_ref,
+    source_ref,
+    weight_ref,
+    count_ref,
+    pair_ref,
+    note_ref,
     now_ref,
     before_ref,
     both_ref,
     spread_ref,
     input_ref,
+    data_ref,
     x_ref,
     h_ref,
     y_ref,
@@ -411,7 +711,7 @@
     flat_ref,
 ):
     is_box = where_ref[0] == 0
-    parity = where_ref[1]
+    parity = where_ref[1] % 2
     both_ref[parity] = mine_ref[...]
     both_ref[1 - parity] = other_ref[...]
     low = lax.broadcasted_iota(jnp.int32, (8, LANES), 1) < HALF
@@ -427,7 +727,8 @@
                 turned = pltpu.roll(pair, HALF, 1)
                 index[s, p, 2 * k] = jnp.where(low, pair, turned)
                 index[s, p, 2 * k + 1] = jnp.where(low, turned, pair)
-    at = at_ref[...]
+    note = note_ref[...]
+    at = jnp.where(lax.broadcasted_iota(jnp.int32, (8, LANES), 0) < 3, note[0:8], 0.0).astype(jnp.int32)
     packed = {}
     pairs = {}
     last = {}
@@ -457,22 +758,39 @@
                         last[s, p, q] = got
     input_ref[0] = zero
     for c in range(3):
-        spread_ref[c] = jnp.where(
-            key_ref[c * LANES : (c + 1) * LANES] == lane_key_ref[...], 1.0, 0.0
-        ).astype(jnp.bfloat16)
-    side = side_ref[...]
+        point_key = across(note[6 + c : 7 + c])
+        for g in range(3):
+            spread_ref[c, :, g * LANES : (g + 1) * LANES] = one_hot(
+                point_key == note[9 + g : 10 + g]
+            )
+    group = lax.broadcasted_iota(jnp.int32, (3, LANES), 0)
+    side = jnp.where(group == 0, note[12:13].astype(jnp.int32), -1)
+    own_fields = [
+        weight_ref[...] * wave_ref[0],
+        DT_SQUARED * mass_ref[0],
+        source_ref[0],
+        count_ref[...][:NODES],
+    ]
+    for k in range(4):
+        flat_ref[0:LANES] = pair_ref[k]
+        flat_ref[LANES : LANES + NODES] = own_fields[k][:, :LANES]
+        flat_ref[2 * LANES : 2 * LANES + NODES] = own_fields[k][:, LANES:]
+        for n in range(NODES):
+            value = flat_ref[pl.ds(n, 3, stride=LANES)]
+            data_ref[k, n] = PENALTY * value if k == 3 else value
     for n in range(NODES):
         x_ref[n] = zero[:3]
         h_ref[n] = zero[:3]
         y_ref[n] = zero[:3]
+    point_node = note[3:6].astype(jnp.int32)
     node_row = lax.broadcasted_iota(jnp.int32, (LANES, LANES), 0)
 
     def step(moment, _):
-        drive = time_ref[moment]
+        drive = time_ref[0, moment]
         inputs = input_ref[moment]
         kick = jnp.zeros((LANES, 3 * LANES), jnp.float32)
         for c in range(3):
-            chosen = jnp.where(node_row == node_ref[c : c + 1], inputs[c : c + 1], 0.0)
+            chosen = jnp.where(node_row == point_node[c : c + 1], inputs[c : c + 1], 0.0)
             for _ in range(3):
                 part = chosen.astype(jnp.bfloat16)
                 kick = kick + jnp.dot(part, spread_ref[c], preferred_element_type=jnp.float32)
@@ -496,10 +814,11 @@
         return 0
 
     lax.fori_loop(0, STEPS, step, 0)
+    home = jnp.concatenate([note[13:14], note[14:15]], axis=1).astype(jnp.int32)
     linked = jnp.where(
-        home_ref[...] == lax.broadcasted_iota(jnp.int32, (LANES, 2 * LANES), 0), 1.0, 0.0
+        home == lax.broadcasted_iota(jnp.int32, (LANES, 2 * LANES), 0), 1.0, 0.0
     ).astype(jnp.bfloat16)
-    alone = home_ref[...] < 0
+    alone = home < 0
 
     def put(out_ref):
         rest = flat_ref[0:LANES]
@@ -512,7 +831,7 @@
             own = flat_ref[(g + 1) * LANES : (g + 2) * LANES]
             cut = slice(g * LANES, (g + 1) * LANES)
             merged = jnp.where(alone[:, cut], own, moved[:, cut])
-            out_ref[:, cut] = merged[:NODES]
+            out_ref[0, :, cut] = merged[:NODES]
 
     put(before_ref)
     for n in range(NODES):
@@ -522,167 +841,47 @@
 
 def fast_body(wave_speed, inverse_mass, source_field, source_time, face_links, coupling_links):
     _, weight_np, _ = node_tables()
+    weight = jnp.asarray(weight_np).reshape(NODES, 1)
     blocks = lax.axis_size("blk")
-    bits = blocks.bit_length() - 1
+    columns = wave_speed.shape[-1]
     me = lax.axis_index("blk")
-    sec = lax.axis_index("sec")
-    is_box = sec == 0
-    columns = wave_speed.shape[-1]
-    records = face_links.shape[-1]
-    per_peer = records // 8
-    offsets = [0] + [1 << j for j in range(bits)]
-
-    live = coupling_links[:, : CAPC * blocks]
-    owner = live[2]
-    ordinal = jnp.arange(HALF)
-    rank = jnp.sum(
-        ((owner[:, None] == owner[None, :]) & (ordinal[None, :] < ordinal[:, None])).astype(jnp.int32),
-        axis=1,
-    )
-    slot = jnp.where(owner >= 0, owner * CAPC + rank, -1)
-    to_slot = (slot[:, None] == ordinal[None, :]).astype(jnp.float32)
-    named = (jnp.stack([live[0], live[1], live[3], live[4]]) + 1).astype(jnp.float32)
-    links = jnp.dot(named, to_slot, precision=EXACT)
-    everyone = lax.all_to_all(
-        jnp.broadcast_to(links[None], (blocks, 4, HALF)), "blk", 0, 0, tiled=True
-    )
-
-    face_element, face_side, face_peer = face_links[0, 0], face_links[0, 1], face_links[0, 2]
-    count = jnp.arange(records)
-    linked = face_peer != me
-    face_rank = jnp.sum(
-        ((face_peer[:, None] == face_peer[None, :]) & (count[None, :] < count[:, None])).astype(jnp.int32),
-        axis=1,
-    )
-    distance = jnp.bitwise_xor(face_peer, me)
-    bit = sum([j * (distance == 1 << j).astype(jnp.int32) for j in range(bits)])
-    face_slot = jnp.where(linked, bit * per_peer + face_rank, -1)
-    to_record = (face_slot[:, None] == ordinal[None, :]).astype(jnp.float32)
-    record = jnp.dot(
-        (jnp.stack([face_element, face_side]) + 1).astype(jnp.float32), to_record, precision=EXACT
-    )
-
-    own_nodes = (jnp.arange(128)[:, None] + 1).astype(jnp.float32) == links[1][None, :]
-    own_cols = links[0][:, None] == (jnp.arange(columns)[None, :] + 1).astype(jnp.float32)
-    points_at = jnp.dot(own_nodes.astype(jnp.float32), own_cols.astype(jnp.float32), precision=EXACT)
-    damping = jnp.where(is_box, PENALTY, 0.0) * points_at
-
-    def padded(field):
-        return jnp.concatenate([field, jnp.zeros((3, columns), jnp.float32)], axis=0)
-
-    fields = jnp.stack(
-        [
-            padded(jnp.asarray(weight_np) * wave_speed[0]),
-            padded(DT_SQUARED * inverse_mass[0]),
-            padded(source_field[0]),
-            damping,
-        ]
-    )
-    take_linked = (record[0][:, None] == (jnp.arange(columns)[None, :] + 1).astype(jnp.float32)).astype(
-        jnp.float32
-    )
-    mine = lax.dot_general(
-        take_linked, fields.reshape(512, columns), (((1,), (1,)), ((), ())), precision=EXACT
-    )
-    mine = mine.at[:, 125].set(record[0]).at[:, 126].set(record[1])
-    ghost = jnp.concatenate(
-        [
-            partner_2(mine[j * per_peer : (j + 1) * per_peer], "blk", j)
-            for j in range(bits)
-        ],
-        axis=0,
-    )
-    partner_record = ghost[:, 125:127].T
-    wide = jnp.concatenate([mine, ghost], axis=0).T.reshape(4, 128, 128)
-    home = jnp.concatenate([wide, fields], axis=2)
-
-    box_table = everyone[:, 0:2]
-    global_table = (
-        everyone[:, 2:4].reshape(blocks, 2, blocks, CAPC).transpose(2, 1, 0, 3).reshape(blocks, 2, HALF)
-    )
-    table = jnp.where(is_box, box_table, global_table)
-    peers = jnp.bitwise_xor(jnp.asarray(offsets, jnp.int32), me)
-    near = table[peers]
-    element_1 = near[:, 0].reshape(-1)
-    node_1 = near[:, 1].reshape(-1)
-    where_from = jnp.repeat(jnp.arange(bits + 1), HALF)
-    valid = node_1 > 0
-    key = jnp.where(valid, where_from * columns + element_1.astype(jnp.int32) - 1, -1)
-    within = jnp.arange((bits + 1) * HALF) % HALF
-    gid = within // CAPC * HALF + jnp.repeat(peers, HALF) * CAPC + within % CAPC
-
-    point_element = near[0, 0]
-    point_node = near[0, 1].astype(jnp.int32) - 1
-    of_column = (
-        (jnp.arange(columns)[:, None] + 1).astype(jnp.float32) == point_element[None, :]
-    ).astype(jnp.float32)
-    of_record = (
-        (record[0][:, None] == point_element[None, :]) & (point_element[None, :] > 0)
-    ).astype(jnp.float32)
-    own_part = jnp.dot(fields.reshape(512, columns), of_column, precision=EXACT)
-    partner_part = jnp.dot(ghost.T, of_record, precision=EXACT)
-    copies = jnp.concatenate([own_part, partner_part], axis=1).reshape(4, 128, 1, 128)[:, :NODES]
-    record_key = jnp.where(
-        partner_record[0] > 0,
-        (1 + jnp.arange(bits * per_peer) // per_peer) * columns + partner_record[0].astype(jnp.int32) - 1,
-        0,
-    )
-    facts = jnp.stack([record[1], partner_record[1], record_key.astype(jnp.float32)])
-    facts = jnp.dot(facts, of_record, precision=EXACT)
-    copy_side = jnp.concatenate([facts[0], facts[1]]).astype(jnp.int32) - 1
-    copy_side = jnp.broadcast_to(copy_side[None], (8, LANES))
-    copy_side = jnp.where(jnp.arange(8)[:, None] < 2, copy_side, -1)
-    ghost_key = jnp.where(facts[1] > 0, facts[2].astype(jnp.int32), -5)
-    own_key = jnp.where(point_element > 0, point_element.astype(jnp.int32) - 1, -5)
-    match = (key[:, None] == own_key[None, :]) | (key[:, None] == ghost_key[None, :])
-    matched = match.astype(jnp.float32)
-    lower = jnp.asarray(np.tril(np.ones((key.shape[0],) * 2, np.float32), -1))
-    place = jnp.dot(lower, matched, precision=EXACT)
-    picked = jnp.stack([match & (place == q) for q in range(SLOTS)], axis=1).astype(jnp.float32)
-    described = jnp.stack([node_1, gid.astype(jnp.float32), (where_from > 0).astype(jnp.float32)])
-    lists = jnp.dot(
-        described, picked.reshape(key.shape[0], SLOTS * HALF), precision=EXACT
-    ).reshape(3, SLOTS, HALF)
-    list_node = lists[0].astype(jnp.int32) - 1
-    on_partner = lists[2] > 0
-    wanted = jnp.concatenate(
-        [jnp.where(on_partner, -1, list_node), jnp.where(on_partner, list_node, -1)], axis=1
-    )
-    own_row = jnp.concatenate([point_node, jnp.full((HALF,), -1, jnp.int32)])[None]
-    wanted = jnp.concatenate([wanted, own_row, jnp.full((1, LANES), -1, jnp.int32)], axis=0)
-    too_long = jnp.max(jnp.sum(matched, axis=0)) > SLOTS
-    index_rows = jnp.concatenate(
-        [
-            lists[1].reshape(SLOTS // 2, LANES),
-            jnp.full((1, LANES), 1.0, jnp.float32) * too_long.astype(jnp.float32),
-        ],
-        axis=0,
-    )
-    unit = (
-        jnp.arange(NODES)[:, None]
-        == jnp.concatenate([point_node, jnp.full((HALF,), -1, jnp.int32)])[None, :]
-    ).astype(jnp.float32)[:, None, :]
-    late = (jnp.arange(STEPS) > 0).astype(jnp.float32)
-    box_f = is_box.astype(jnp.float32)
-    coef = jnp.stack(
-        [
-            source_time[0],
-            late,
-            jnp.where(late > 0, -1.0, box_f),
-            jnp.where(late > 0, 0.0, 1.0 - box_f),
-            jnp.full((STEPS,), 1.0, jnp.float32) * box_f,
-        ]
-    )
+    place = jnp.stack([lax.axis_index("sec"), me]).astype(jnp.int32)
     vmem = pl.BlockSpec(memory_space=pltpu.VMEM)
     smem = pl.BlockSpec(memory_space=pltpu.SMEM)
+
+    def shape(*dims):
+        return jax.ShapeDtypeStruct(dims, jnp.float32)
+
+    links, m0, m1, m2, m3, count = pl.pallas_call(
+        pack_kernel,
+        out_shape=[shape(blocks, 8, LANES)] + [shape(16, 4 * LANES)] * 4 + [shape(LANES, columns)],
+        in_specs=[smem] + [vmem] * 6,
+        out_specs=[vmem] * 6,
+    )(place, wave_speed, inverse_mass, source_field, weight, face_links, coupling_links)
+    every = lax.all_to_all(links, "blk", 0, 0, tiled=True)
+    mine = [m0, m1, m2, m3]
+    ghost = [partner_2(part, "blk", j) for j, part in enumerate(mine)]
     full = pltpu.VMEM((NODES, 8, LANES), jnp.float32)
-    payload = pl.pallas_call(
+    payload, pair, note = pl.pallas_call(
         response_kernel,
-        out_shape=jax.ShapeDtypeStruct((blocks, PAYLOAD, LANES), jnp.float32),
-        in_specs=[smem] + [vmem] * 5,
-        out_specs=vmem,
-        scratch_shapes=[full] * 7 + [pltpu.VMEM((STEPS, 8, LANES), jnp.float32)],
-    )(coef, copies, copy_side, unit, wanted, index_rows)
+        out_shape=[shape(blocks, PAYLOAD, LANES), shape(4, LANES, LANES), shape(16, LANES)],
+        in_specs=[smem] * 2 + [vmem] * 14,
+        out_specs=[vmem] * 3,
+        scratch_shapes=[pltpu.VMEM((4, LANES, LANES), jnp.float32)]
+        + [full] * 7
+        + [pltpu.VMEM((STEPS, 8, LANES), jnp.float32)],
+    )(
+        place,
+        source_time,
+        wave_speed,
+        inverse_mass,
+        source_field,
+        weight,
+        count,
+        *mine,
+        *ghost,
+        every,
+    )
 
     same_core = [[c + 2 * i for i in range(blocks)] for c in range(2)]
     received = lax.all_to_all(
@@ -692,67 +891,47 @@
     overflow = jnp.max(
         jnp.maximum(received[:, FLAG_ROW, 0], sibling[:, FLAG_ROW, 0])
     ) > 0
-
-    fill = 3 * LANES - key.shape[0]
-
-    def extend(values, rest):
-        return jnp.concatenate([values, jnp.full((fill,), rest, jnp.int32)])
-
-    at = jnp.zeros((8, LANES), jnp.int32).at[0:3].set(extend(gid, 0).reshape(3, LANES))
-    point_rows = extend(node_1.astype(jnp.int32) - 1, -1).reshape(3, LANES)
-    key_column = extend(key, -1)[:, None]
-    own_record_key = jnp.where(record[0] > 0, record[0].astype(jnp.int32) - 1, -3)
-    ghost_record_key = jnp.where(partner_record[0] > 0, record_key, -3)
-    lane_key = jnp.concatenate([own_record_key, ghost_record_key, jnp.arange(columns)])[None]
-    home_lane = jnp.dot(
-        (jnp.arange(HALF)[None] + 1).astype(jnp.float32), take_linked, precision=EXACT
-    ).astype(jnp.int32) - 1
-    home_side = jnp.full((3, LANES), -1, jnp.int32)
-    home_side = home_side.at[0].set(
-        jnp.concatenate([record[1], partner_record[1]]).astype(jnp.int32) - 1
-    )
-    home = home[:, :NODES].reshape(4, NODES, 3, LANES)
-    where_am_i = jnp.stack([sec, me % 2]).astype(jnp.int32)
     three = pltpu.VMEM((NODES, 3, LANES), jnp.float32)
 
     def quick(_):
-        return tuple(pl.pallas_call(
-            final_kernel,
-            out_shape=[jax.ShapeDtypeStruct((NODES, columns), jnp.float32)] * 2,
-            in_specs=[smem] * 2 + [vmem] * 9,
-            out_specs=[vmem] * 2,
-            scratch_shapes=[
-                pltpu.VMEM((2, blocks, PAYLOAD, LANES), jnp.float32),
-                pltpu.VMEM((3, LANES, 3 * LANES), jnp.bfloat16),
-                pltpu.VMEM((STEPS, 8, LANES), jnp.float32),
-                three,
-                three,
-                three,
-                pltpu.VMEM((3 * LANES, LANES), jnp.float32),
-                pltpu.VMEM((3 * LANES, LANES), jnp.float32),
-            ],
-        )(
-            where_am_i,
-            source_time[0],
-            received,
-            sibling,
-            home,
-            home_side,
-            at,
-            point_rows,
-            key_column,
-            lane_key,
-            home_lane,
-        ))
+        return tuple(
+            pl.pallas_call(
+                final_kernel,
+                out_shape=[shape(1, NODES, columns)] * 2,
+                in_specs=[smem] * 2 + [vmem] * 9,
+                out_specs=[vmem] * 2,
+                scratch_shapes=[
+                    pltpu.VMEM((2, blocks, PAYLOAD, LANES), jnp.float32),
+                    pltpu.VMEM((3, LANES, 3 * LANES), jnp.bfloat16),
+                    pltpu.VMEM((STEPS, 8, LANES), jnp.float32),
+                    pltpu.VMEM((4, NODES, 3, LANES), jnp.float32),
+                    three,
+                    three,
+                    three,
+                    pltpu.VMEM((3 * LANES, LANES), jnp.float32),
+                    pltpu.VMEM((3 * LANES, LANES), jnp.float32),
+                ],
+            )(
+                place,
+                source_time,
+                received,
+                sibling,
+                wave_speed,
+                inverse_mass,
+                source_field,
+                weight,
+                count,
+                pair,
+                note,
+            )
+        )
 
     def slow(_):
-        now, before = general_body(
+        return general_body(
             wave_speed, inverse_mass, source_field, source_time, face_links, coupling_links
         )
-        return (now[0], before[0])
-
-    now, before = lax.cond(overflow, slow, quick, 0)
-    return (now[None], before[None])
+
+    return lax.cond(overflow, slow, quick, 0)
 
 
 def body(*arguments):

time: 112 us -> 92.1 us (0.82)
  blocking collectives: 0 us -> 14.7 us
  waiting for transfers between devices: 15.8 us -> 4.41 us
  other arithmetic: 10 us -> 0.69 us
  local copies, waits for them, and re-layouts: 17.8 us -> 9.68 us
  starting transfers between devices: 20 us -> 13.5 us
  Pallas kernels: 42.5 us -> 47.2 us
  matrix products: 3.18 us -> 0 us
    all_to_all x0 -> x1, blocking collectives: none -> 14.7 us  [fast_body(): lax.all_to_all(payload, ('sec', 'blk'), 0, 0, axis_index_groups=same_core...]
    all_to_all x2 -> x1, waiting for transfers between devices: 11 us -> 0.01 us  [fast_body(): every = lax.all_to_all(links, 'blk', 0, 0, tiled=True)]
    all_to_all x2 -> x1, starting transfers between devices: 14.1 us -> 7.5 us  [fast_body(): every = lax.all_to_all(links, 'blk', 0, 0, tiled=True)]
    pallas_call x2 -> x3, Pallas kernels: 42.5 us -> 47.2 us  [the longest x1 25.1 us: quick(): pl.pallas_call(final_kernel, out_shape=[shape(1, NODES, columns)] * 2, in...]
    dot_general x10 -> x0, matrix products: 3.18 us -> none  [the longest x1 0.53 us: fast_body(): partner_part = jnp.dot(ghost.T, of_record, precision=EXACT)]
    slice x10 -> x0, local copies, waits for them, and re-layouts: 2.92 us -> none  [the longest x1 0.99 us: fast_body(): mine[j * per_peer:(j + 1) * per_peer]]
    another operation x7 -> x1, other arithmetic: 2.91 us -> 0.07 us  [fast_body(): place = jnp.stack([lax.axis_index('sec'), me]).astype(jnp.int32)]
    broadcast_in_dim x8 -> x0, local copies, waits for them, and re-layouts: 2.51 us -> none  [the longest x2 2.42 us: fast_body(): return (now[None], before[None])]
  transfers between devices with their start and end apart: 7 -> 6, of which waited for: 3 -> 3; matrix products, arithmetic and copies ran while one was open for 10% -> 0% of each run, Pallas kernels for 0% -> 0%
where the time goes in v2:
time: 92.1 us; the launch traced here: 91.5 us
  Pallas kernels  47.2 us (51%)
  blocking collectives  14.7 us (16%)
  starting transfers between devices  13.5 us (15%)
  local copies, waits for them, and re-layouts  9.68 us (11%)
  waiting for transfers between devices  4.41 us (5%)
  between operations  1.38 us (1%)
    pallas_call x1, Pallas kernels, quick(): pl.pallas_call(final_kernel, out_shape=[shape(1, NODES, columns)] * 2, in...  25.1 us
    pallas_call x1, Pallas kernels, fast_body(): pl.pallas_call(response_kernel, out_shape=[shape(blocks, PAYLOAD, LANES),...  19.6 us
    all_to_all x1, blocking collectives, fast_body(): lax.all_to_all(payload, ('sec', 'blk'), 0, 0, axis_index_groups=same_core...  14.7 us
    all_to_all x1, starting transfers between devices, fast_body(): every = lax.all_to_all(links, 'blk', 0, 0, tiled=True)  7.5 us
    ppermute x5, starting transfers between devices, partner_2(): lax.ppermute(value, axis, [(i, i ^ 1 << stride) for i in range(lax.axis_s...  5.98 us
    unnamed x36, local copies, waits for them, and re-layouts  5.2 us
    ppermute x5, waiting for transfers between devices, partner_2(): lax.ppermute(value, axis, [(i, i ^ 1 << stride) for i in range(lax.axis_s...  4.4 us
    cond x2, local copies, waits for them, and re-layouts, fast_body(): return lax.cond(overflow, slow, quick, 0)  2.5 us
  transfers between devices with their start and end apart: 6, of which 3 were waited for; matrix products, arithmetic and copies ran while one was open for 0% of the time, Pallas kernels for 0%

profile of v2, /device:TPU:0, one launch (start us, length us, event | category | flops | bytes accessed | tf_op | source)
XLA Modules:
  0.0 91.5 jit_solution(13262843967729408896)
XLA Ops:
  0.6 0.7 copy-done.18
  1.3 0.6 copy.153.face_ref
  1.9 1.6 %copy.154.wave_ref = f32[1,125,256]{2,1,0:T(8,128)} copy(f32[1,125,256]{2,0,1:T(1,128)} %param.15) | data formatting | bytes 256000 | tf_op args[0]
  3.5 0.7 copy.155.mass_ref
  4.4 0.7 copy.156.source_ref
  5.3 2.5 %shard_map.129 = (f32[16,8,128]{2,1,0:T(8,128)}, f32[16,512]{1,0:T(8,128)}, f32[16,512]{1,0:T(8,128)}, f32[16,512]{1,0:T(8,128)}, f32[16,512]{1,0:T(8,128)}, /*index=5*/f32[128,256]{1,0:T(8,128)S(1)}) custom-call(s32[2]{0:T(128)S(1)} %pad_add_fusion.2.where_ref, f32[1,125,256]{2,1,0:T(8,128)} %copy.154.wave_ref, f32[1,125,256]{2,1,0:T(8,128)} %copy.155.mass_ref, ...), custom_call_target="tpu_custom_call" | custom-call | tf_op jit(solution)/shard_map/pallas_call | solution.py:855
  7.8 7.5 %all-to-all-start.2 = ((f32[16,8,128]{2,1,0:T(8,128)}), f32[16,8,128]{2,1,0:T(8,128)S(1)}, u32[]{:S(2)}, u32[]{:S(2)}) async-start(f32[16,8,128]{2,1,0:T(8,128)} %get-tuple-element.474), calls=%async_computation.2 | async-start | bytes 131072 | tf_op jit(solution)/shard_map/all_to_all | solution.py:861
  15.3 0.5 collective-permute-start.5
  15.8 1.7 %collective-permute-start.6 = (f32[16,512]{1,0:T(8,128)S(1)}, f32[16,512]{1,0:T(8,128)S(1)}, u32[]{:S(2)}, u32[]{:S(2)}) collective-permute-start(f32[16,512]{1,0:T(8,128)S(1)} %copy-done.11), channel_id=1, source_target_pairs={{0,2},{1,3},{2,0},{3,1},{4,6},{5,7},{6,4},{7,5},{8,10},{9,11},{10,... | collective-permute-start | bytes 98312 | tf_op jit(solution)/shard_map/ppermute | solution.py:18
  17.4 1.5 %collective-permute-start.7 = (f32[16,512]{1,0:T(8,128)S(1)}, f32[16,512]{1,0:T(8,128)S(1)}, u32[]{:S(2)}, u32[]{:S(2)}) collective-permute-start(f32[16,512]{1,0:T(8,128)S(1)} %copy-done.12), channel_id=1, source_target_pairs={{0,4},{1,5},{2,6},{3,7},{4,0},{5,1},{6,2},{7,3},{8,12},{9,13},{10,... | collective-permute-start | bytes 98312 | tf_op jit(solution)/shard_map/ppermute | solution.py:18
  18.9 2.4 %collective-permute-start.8 = (f32[16,512]{1,0:T(8,128)S(1)}, f32[16,512]{1,0:T(8,128)S(1)}, u32[]{:S(2)}, u32[]{:S(2)}) collective-permute-start(f32[16,512]{1,0:T(8,128)S(1)} %copy-done.13), channel_id=1, source_target_pairs={{0,8},{1,9},{2,10},{3,11},{4,12},{5,13},{6,14},{7,15},{8,0},{9,1},... | collective-permute-start | bytes 98312 | tf_op jit(solution)/shard_map/ppermute | solution.py:18
  21.5 2.6 %collective-permute-done.8.g3_ref = f32[16,512]{1,0:T(8,128)S(1)} collective-permute-done((f32[16,512]{1,0:T(8,128)S(1)}, f32[16,512]{1,0:T(8,128)S(1)}, u32[]{:S(2)}, u32[]{:S(2)}) %collective-permute-start.8) | collective-permute-done | bytes 32800 | tf_op jit(solution)/shard_map/ppermute | solution.py:18
  24.1 0.6 copy-done.17
  24.7 19.6 %shard_map.130 = (f32[16,40,128]{2,1,0:T(8,128)}, f32[4,128,128]{2,1,0:T(8,128)S(1)}, f32[16,128]{1,0:T(8,128)S(1)}) custom-call(s32[2]{0:T(128)S(1)} %pad_add_fusion.2.where_ref, f32[1,12]{1,0:T(1,128)S(1)} %copy-done.19, f32[1,125,256]{2,1,0:T(8,128)} %copy.154.wave_ref, f32[1,125,256]{2,1,0:T(8,128)} %copy.155.mass_ref, f32[1,125,256]{2,1,0:T(8,128)} %copy.156.source_ref, ...), custom_call_target="tpu_custom_call" | custom-call | tf_op jit(solution)/shard_map/pallas_call | solution.py:865
  44.4 14.7 %all_to_all.33 = f32[16,40,128]{2,1,0:T(8,128)S(1)} all-to-all(f32[16,40,128]{2,1,0:T(8,128)} %get-tuple-element.475), channel_id=1, replica_groups={{0,2,4,6,8,10,12,14,16,18,20,22,24,26,28,30},{1,3,5,7,9,11,13,15,17,19,..., dimensions={0} | all-to-all | bytes 655360 | tf_op jit(solution)/shard_map/all_to_all | solution.py:887
  59.0 1.6 %collective-permute-done.9 = f32[16,40,128]{2,1,0:T(8,128)S(1)} collective-permute-done((f32[16,40,128]{2,1,0:T(8,128)S(1)}, f32[16,40,128]{2,1,0:T(8,128)S(1)}, u32[]{:S(2)}, u32[]{:S(2)}) %collective-permute-start.9) | collective-permute-done | bytes 327712 | tf_op jit(solution)/shard_map/ppermute | solution.py:18
  60.7 0.6 fusion.32
  62.0 29.6 %conditional.1 = (f32[1,125,256]{2,0,1:T(1,128)}, f32[1,125,256]{2,0,1:T(1,128)}) conditional(s32[]{:T(128)} %convert_element_type.23, (s32[2]{0:T(128)S(1)}, f32[1,12]{1,0:T(1,128)S(1)}, f32[16,40,128]{2,1,0:T(8,128)S(1)}, f32[16,40,128]{2,1,0:T(8,128)S(1)}, f32[1,125,256]{2,0,1:T(1,128)S(1)}, /*index=5*/f32[1,125,256]{2,0,1:T(1,128)S(1)}, ...), branch_computations={%region_1.0_spmd, %region_2.15_spmd} | conditional | flops 347599744 | bytes 9835607 | solution.py:934
  62.0 0.7 copy.159.source_ref
  62.6 0.7 copy.158.mass_ref
  63.3 0.7 copy.157.wave_ref
  63.9 25.1 %branch_0_fun.1 = (f32[1,125,256]{2,1,0:T(8,128)}, f32[1,125,256]{2,1,0:T(8,128)}) custom-call(s32[2]{0:T(128)S(1)} %get-tuple-element.409.where_ref, f32[1,12]{1,0:T(1,128)S(1)} %get-tuple-element.410.time_ref, f32[16,40,128]{2,1,0:T(8,128)S(1)} %get-tuple-element.411.mine_ref, f32[16,40,128]{2,1,0:T(8,128)S(1)} %get-tuple-element.412.other_ref, ...), custom_call_target="tpu_custom_call" | custom-call | tf_op jit(solution)/shard_map/cond/branch_0_fun/pallas_call | solution.py:898
  89.0 1.7 %copy.168 = f32[1,125,256]{2,0,1:T(1,128)} copy(f32[1,125,256]{2,1,0:T(8,128)} %get-tuple-element.771) | data formatting | bytes 256000 | tf_op jit(solution)/shard_map/cond | solution.py:934
  90.8 0.8 copy.170
  (38 shorter events, 0.7 us)
Async XLA Ops:
  0.6 0.7 copy-start.18
  1.9 1.6 %copy-start.4 = (f32[1,125,256]{2,0,1:T(1,128)S(1)}, f32[1,125,256]{2,0,1:T(1,128)}, u32[]{:S(2)}) copy-start(f32[1,125,256]{2,0,1:T(1,128)} %param.16) | copy-start | bytes 384004
  3.5 1.0 %copy-start.5 = (f32[1,125,256]{2,0,1:T(1,128)S(1)}, f32[1,125,256]{2,0,1:T(1,128)}, u32[]{:S(2)}) copy-start(f32[1,125,256]{2,0,1:T(1,128)} %param.17) | copy-start | bytes 384004
  4.4 0.8 copy-start.6
  4.4 0.8 copy-start.9
  7.8 7.5 %copy-start.10 = (f32[16,512]{1,0:T(8,128)S(1)}, f32[16,512]{1,0:T(8,128)}, u32[]{:S(2)}) copy-start(f32[16,512]{1,0:T(8,128)} %get-tuple-element.470.m0_ref) | copy-start | bytes 98308
  7.8 8.0 %copy-start.11 = (f32[16,512]{1,0:T(8,128)S(1)}, f32[16,512]{1,0:T(8,128)}, u32[]{:S(2)}) copy-start(f32[16,512]{1,0:T(8,128)} %get-tuple-element.471.m1_ref) | copy-start | bytes 98308
  7.8 9.7 %copy-start.12 = (f32[16,512]{1,0:T(8,128)S(1)}, f32[16,512]{1,0:T(8,128)}, u32[]{:S(2)}) copy-start(f32[16,512]{1,0:T(8,128)} %get-tuple-element.472.m2_ref) | copy-start | bytes 98308
  7.8 11.2 %copy-start.13 = (f32[16,512]{1,0:T(8,128)S(1)}, f32[16,512]{1,0:T(8,128)}, u32[]{:S(2)}) copy-start(f32[16,512]{1,0:T(8,128)} %get-tuple-element.473.m3_ref) | copy-start | bytes 98308
  7.8 16.3 %all-to-all-start.2 = ((f32[16,8,128]{2,1,0:T(8,128)}), f32[16,8,128]{2,1,0:T(8,128)S(1)}, u32[]{:S(2)}, u32[]{:S(2)}) async-start(f32[16,8,128]{2,1,0:T(8,128)} %get-tuple-element.474), calls=%async_computation.2 | async-start | bytes 131072 | tf_op jit(solution)/shard_map/all_to_all | solution.py:861
  15.3 6.0 %collective-permute-start.5 = (f32[16,512]{1,0:T(8,128)S(1)}, f32[16,512]{1,0:T(8,128)S(1)}, u32[]{:S(2)}, u32[]{:S(2)}) collective-permute-start(f32[16,512]{1,0:T(8,128)S(1)} %copy-done.10), channel_id=1, source_target_pairs={{0,1},{1,0},{2,3},{3,2},{4,5},{5,4},{6,7},{7,6},{8,9},{9,8},{10,11... | collective-permute-start | bytes 98312 | tf_op jit(solution)/shard_map/ppermute | solution.py:18
  15.8 5.5 %collective-permute-start.6 = (f32[16,512]{1,0:T(8,128)S(1)}, f32[16,512]{1,0:T(8,128)S(1)}, u32[]{:S(2)}, u32[]{:S(2)}) collective-permute-start(f32[16,512]{1,0:T(8,128)S(1)} %copy-done.11), channel_id=1, source_target_pairs={{0,2},{1,3},{2,0},{3,1},{4,6},{5,7},{6,4},{7,5},{8,10},{9,11},{10,... | collective-permute-start | bytes 98312 | tf_op jit(solution)/shard_map/ppermute | solution.py:18
  17.4 4.0 %collective-permute-start.7 = (f32[16,512]{1,0:T(8,128)S(1)}, f32[16,512]{1,0:T(8,128)S(1)}, u32[]{:S(2)}, u32[]{:S(2)}) collective-permute-start(f32[16,512]{1,0:T(8,128)S(1)} %copy-done.12), channel_id=1, source_target_pairs={{0,4},{1,5},{2,6},{3,7},{4,0},{5,1},{6,2},{7,3},{8,12},{9,13},{10,... | collective-permute-start | bytes 98312 | tf_op jit(solution)/shard_map/ppermute | solution.py:18
  18.9 5.8 %copy-start.19 = (f32[1,12]{1,0:T(1,128)S(1)}, f32[1,12]{1,0:T(1,128)}, u32[]{:S(2)}) copy-start(f32[1,12]{1,0:T(1,128)} %coef_ref.1) | copy-start | bytes 148
  18.9 5.2 %collective-permute-start.8 = (f32[16,512]{1,0:T(8,128)S(1)}, f32[16,512]{1,0:T(8,128)S(1)}, u32[]{:S(2)}, u32[]{:S(2)}) collective-permute-start(f32[16,512]{1,0:T(8,128)S(1)} %copy-done.13), channel_id=1, source_target_pairs={{0,8},{1,9},{2,10},{3,11},{4,12},{5,13},{6,14},{7,15},{8,0},{9,1},... | collective-permute-start | bytes 98312 | tf_op jit(solution)/shard_map/ppermute | solution.py:18
  21.3 2.8 %copy-start.14 = (f32[16,512]{1,0:T(8,128)}, f32[16,512]{1,0:T(8,128)S(1)}, u32[]{:S(2)}) copy-start(f32[16,512]{1,0:T(8,128)S(1)} %collective-permute-done.5.g0_ref) | copy-start | bytes 98308
  21.3 2.8 %copy-start.15 = (f32[16,512]{1,0:T(8,128)}, f32[16,512]{1,0:T(8,128)S(1)}, u32[]{:S(2)}) copy-start(f32[16,512]{1,0:T(8,128)S(1)} %collective-permute-done.6.g1_ref) | copy-start | bytes 98308
  21.4 2.7 %copy-start.16 = (f32[16,512]{1,0:T(8,128)}, f32[16,512]{1,0:T(8,128)S(1)}, u32[]{:S(2)}) copy-start(f32[16,512]{1,0:T(8,128)S(1)} %collective-permute-done.7.g2_ref) | copy-start | bytes 98308
  24.1 0.6 copy-start.17
  24.1 0.6 copy-start.7
  44.4 17.6 %copy-start.3 = (f32[1,125,256]{2,0,1:T(1,128)S(1)}, f32[1,125,256]{2,0,1:T(1,128)}, u32[]{:S(2)}) copy-start(f32[1,125,256]{2,0,1:T(1,128)} %param.15) | copy-start | bytes 384004
  59.0 1.6 %collective-permute-start.9 = (f32[16,40,128]{2,1,0:T(8,128)S(1)}, f32[16,40,128]{2,1,0:T(8,128)S(1)}, u32[]{:S(2)}, u32[]{:S(2)}) collective-permute-start(f32[16,40,128]{2,1,0:T(8,128)S(1)} %all_to_all.33), channel_id=1, source_target_pairs={{0,1},{1,0},{2,3},{3,2},{4,5},{5,4},{6,7},{7,6},{8,9},{9,8},{10,11... | collective-permute-start | bytes 983048 | tf_op jit(solution)/shard_map/ppermute | solution.py:18
  89.0 1.7 %copy-start.8 = (f32[1,125,256]{2,1,0:T(8,128)S(1)}, f32[1,125,256]{2,1,0:T(8,128)}, u32[]{:S(2)}) copy-start(f32[1,125,256]{2,1,0:T(8,128)} %get-tuple-element.772) | copy-start | bytes 384004 | tf_op jit(solution)/shard_map/cond

commit v3 on v2

--- a/solution.py
+++ b/solution.py
@@ -236,52 +236,107 @@
     return out
 
 
-def stiffness_lines(x_ref, scale_ref, y_ref):
+def line_tiles():
+    row = lax.broadcasted_iota(jnp.int32, (8, LANES), 0)
+    tiles = []
+    for matrix in (line_matrix(), line_matrix().T):
+        columns = []
+        for j in range(5):
+            tile = jnp.zeros((8, LANES), jnp.float32)
+            for i in range(5):
+                tile = jnp.where(row == i, float(matrix[i, j]), tile)
+            columns.append(tile)
+        tiles.append(columns)
+    return tiles
+
+
+def tile_of(ref, bc, group=0, groups=1):
+    start = (bc * groups + group) * 8
+    return ref[start : start + 8, :]
+
+
+def set_tile(ref, value, bc, group=0, groups=1):
+    start = (bc * groups + group) * 8
+    ref[start : start + 8, :] = value
+
+
+def repeat_row(ref, row):
+    return jnp.broadcast_to(ref[row : row + 1, :], (8, LANES))
+
+
+def stiffness_tiles(x_ref, scale_ref, y_ref, grad_ref, groups, shared):
     forward = line_matrix()
     backward = forward.T.copy()
-
-    def along(index):
-        x = [x_ref[k] for k in index]
-        grads = apply_line(forward, x)
-        scaled = [g * scale_ref[k] for g, k in zip(grads, index)]
-        return apply_line(backward, scaled)
-
+    to_grad, to_node = line_tiles()
+
+    for g in range(groups):
+
+        def scale(bc):
+            return tile_of(scale_ref, bc) if shared else tile_of(scale_ref, bc, g, groups)
+
+        def along(index):
+            grads = apply_line(forward, [tile_of(x_ref, k, g, groups) for k in index])
+            return apply_line(backward, [v * scale(k) for v, k in zip(grads, index)])
+
+        for bc in range(25):
+            start = (bc * groups + g) * 8
+            total = to_grad[0] * repeat_row(x_ref, start)
+            for j in range(1, 5):
+                total = total + to_grad[j] * repeat_row(x_ref, start + j)
+            grad_ref[start : start + 8, :] = total * scale(bc)
+        total = [None] * 25
+        for c in range(5):
+            index = [5 * j + c for j in range(5)]
+            for k, value in zip(index, along(index)):
+                total[k] = value
+        for b in range(5):
+            index = [5 * b + j for j in range(5)]
+            for k, value in zip(index, along(index)):
+                total[k] = total[k] + value
+        for bc in range(25):
+            start = (bc * groups + g) * 8
+            value = total[bc]
+            for j in range(5):
+                value = value + to_node[j] * repeat_row(grad_ref, start + j)
+            set_tile(y_ref, value, bc, g, groups)
+
+
+def partner_faces(ref, face_ref, side, group=0, groups=1):
+    row = lax.broadcasted_iota(jnp.int32, (8, LANES), 0)
+    is_side = [side == q for q in range(6)]
+    on_a = (is_side[0] & (row == 0)) | (is_side[1] & (row == 4))
+    arrived = []
+    for t in range(5):
+        first = ref[pl.ds((t * groups + group) * 8, 8, stride=40 * groups), :]
+        last = ref[pl.ds((t * groups + group) * 8 + 4, 8, stride=40 * groups), :]
+        value = jnp.where(is_side[1], last, first)
+        value = jnp.where(is_side[2], tile_of(ref, t, group, groups), value)
+        value = jnp.where(is_side[3], tile_of(ref, 20 + t, group, groups), value)
+        value = jnp.where(is_side[4], tile_of(ref, 5 * t, group, groups), value)
+        value = jnp.where(is_side[5], tile_of(ref, 5 * t + 4, group, groups), value)
+        value = pltpu.roll(value, HALF, 1)
+        arrived.append(value)
+        set_tile(face_ref, value, t)
+    extra = []
     for b in range(5):
         for c in range(5):
-            index = [25 * j + 5 * b + c for j in range(5)]
-            for k, value in zip(index, along(index)):
-                y_ref[k] = value
-    for a in range(5):
-        total = [y_ref[25 * a + k] for k in range(25)]
-        for c in range(5):
-            local = [5 * j + c for j in range(5)]
-            for k, value in zip(local, along([25 * a + k for k in local])):
-                total[k] = total[k] + value
-        for b in range(5):
-            local = [5 * b + j for j in range(5)]
-            for k, value in zip(local, along([25 * a + k for k in local])):
-                total[k] = total[k] + value
-        for k in range(25):
-            y_ref[25 * a + k] = total[k]
-
-
-def partner_faces(load, side):
-    _, _, faces = node_tables()
-    masks = [side == q for q in range(6)]
-    arrived = []
-    for t in range(25):
-        value = jnp.zeros(side.shape, jnp.float32)
-        for q in range(6):
-            value = jnp.where(masks[q], load(int(faces[q, t])), value)
-        arrived.append(pltpu.roll(value, HALF, 1))
-    extra = [None] * NODES
-    for q in range(6):
-        for t in range(25):
-            node = int(faces[q, t])
-            before = extra[node]
-            zero = jnp.zeros(side.shape, jnp.float32) if before is None else before
-            extra[node] = jnp.where(masks[q], arrived[t], zero)
+            value = jnp.where(on_a, repeat_row(face_ref, 8 * c + b), 0.0)
+            if b == 0:
+                value = jnp.where(is_side[2], arrived[c], value)
+            if b == 4:
+                value = jnp.where(is_side[3], arrived[c], value)
+            if c == 0:
+                value = jnp.where(is_side[4], arrived[b], value)
+            if c == 4:
+                value = jnp.where(is_side[5], arrived[b], value)
+            extra.append(value)
     return extra
+
+
+def load_tiles(flat_ref, out_ref, factor=None, group=0, groups=1, start=0):
+    for bc in range(25):
+        value = flat_ref[pl.ds(start + bc, 8, stride=25), :]
+        set_tile(out_ref, value if factor is None else factor * value, bc, group, groups)
 
 
 def across(row_values):
@@ -355,7 +410,7 @@
     for k in range(links_ref.shape[0]):
         links_ref[k] = links
 
-    faces = face_ref[0]
+    faces = face_ref[:, 0, :]
     peer = faces[2:3]
     linked = peer != me
     distance = peer ^ me
@@ -384,9 +439,9 @@
     count_ref[...] = count
     take = jnp.concatenate(taken, axis=1)
     pad = jnp.zeros((LANES - NODES, 2 * LANES), jnp.float32)
-    stiff = jnp.concatenate([weight_ref[...] * wave_ref[0], pad], axis=0)
-    mass = jnp.concatenate([DT_SQUARED * mass_ref[0], pad], axis=0)
-    source = jnp.concatenate([source_ref[0], pad], axis=0)
+    stiff = jnp.concatenate([weight_ref[...] * wave_ref[:, 0, :], pad], axis=0)
+    mass = jnp.concatenate([DT_SQUARED * mass_ref[:, 0, :], pad], axis=0)
+    source = jnp.concatenate([source_ref[:, 0, :], pad], axis=0)
     first = exact_pick(stiff, take, True)
     first = jnp.where(right[:HALF] == 125, record_column[:HALF], first)
     first = jnp.where(right[:HALF] == 126, side_column[:HALF], first)
@@ -474,14 +529,19 @@
     out_ref,
     pair_ref,
     note_ref,
-    data_ref,
+    flat_ref,
     scale_ref,
-    x_ref,
-    h_ref,
+    inverse_ref,
+    force_ref,
+    damp_ref,
+    state_ref,
+    z_ref,
+    hc_ref,
+    hz_ref,
     y_ref,
-    t_ref,
-    in_ref,
-    rec_ref,
+    grad_ref,
+    face_ref,
+    code_ref,
     seen_ref,
 ):
     down = lax.broadcasted_iota(jnp.int32, (LANES, LANES), 0)
@@ -565,14 +625,17 @@
     ]
     take = jnp.concatenate(take, axis=0)
     own_fields = [
-        weight_ref[...] * wave_ref[0],
-        DT_SQUARED * mass_ref[0],
-        source_ref[0],
+        weight_ref[...] * wave_ref[:, 0, :],
+        DT_SQUARED * mass_ref[:, 0, :],
+        source_ref[:, 0, :],
         count_ref[...][:NODES],
     ]
-    for k in range(4):
-        copy = exact_pick(own_fields[k], take) + exact_pick(pair[k], partner_matrix)[:NODES]
-        data_ref[k, 0:NODES] = PENALTY * copy if k == 3 else copy
+    flat_ref[...] = jnp.zeros(flat_ref.shape, jnp.float32)
+    for k, out in enumerate((scale_ref, inverse_ref, force_ref, damp_ref)):
+        flat_ref[0:NODES] = (
+            exact_pick(own_fields[k], take) + exact_pick(pair[k], partner_matrix)[:NODES]
+        )
+        load_tiles(flat_ref, out, PENALTY if k == 3 else None)
 
     home = []
     for g in range(2):
@@ -598,21 +661,22 @@
     note_ref[...] = jnp.concatenate(notes, axis=0)
 
     row = lax.broadcasted_iota(jnp.int32, (8, LANES), 0)
-    low = lax.broadcasted_iota(jnp.int32, (8, LANES), 1) < HALF
-    first = row == 0
-    side = jnp.where(row < 2, jnp.broadcast_to(side_row, (8, LANES)), -1)
-    forced = row == SLOTS
-    shape = (8, LANES)
-    start_node = own_node.astype(jnp.int32)
-
-    def tile(k, n):
-        return jnp.broadcast_to(data_ref[k, n : n + 1], shape)
-
-    for n in range(NODES):
-        x_ref[n] = jnp.where((row == 1) & (start_node == n), 1.0, 0.0)
-        h_ref[n] = jnp.zeros(shape, jnp.float32)
-        y_ref[n] = jnp.zeros(shape, jnp.float32)
-        scale_ref[n] = tile(0, n)
+    side = jnp.broadcast_to(side_row, (8, LANES))
+    own_here = jnp.broadcast_to(own_node.astype(jnp.int32), (8, LANES))
+    zero = jnp.zeros((8, LANES), jnp.float32)
+    for q in range(SLOTS + 1):
+        node_q = jnp.broadcast_to(wanted[q : q + 1], (8, LANES))
+        code_ref[q] = jnp.where((node_q >= 0) & (node_q // 25 == row), node_q % 25, -1)
+    for bc in range(25):
+        set_tile(z_ref, jnp.where(own_here == 25 * row + bc, jnp.where(row < 5, 1.0, 0.0), 0.0), bc)
+        set_tile(hc_ref, zero, bc)
+        set_tile(hz_ref, zero, bc)
+        set_tile(state_ref, zero, bc, 0, 2)
+        set_tile(y_ref, zero, bc, 0, 2)
+    for bc in range(25, 40):
+        set_tile(z_ref, zero, bc)
+        set_tile(y_ref, zero, bc, 0, 2)
+        set_tile(y_ref, zero, bc, 1, 2)
 
     is_box = jnp.where(where_ref[0] == 0, 1.0, 0.0)
 
@@ -621,40 +685,47 @@
         keep = jnp.where(moment > 0, 1.0, 0.0)
         stiff = jnp.where(moment > 0, -1.0, is_box)
         begin = jnp.where(moment > 0, 0.0, 1.0 - is_box)
-        for n in range(NODES):
-            t_ref[n] = jnp.where(first, y_ref[n], x_ref[n])
-        extra = partner_faces(lambda k: t_ref[k], side)
-        for n in range(NODES):
-            assembled = t_ref[n] if extra[n] is None else t_ref[n] + extra[n]
-            inverse = tile(1, n)
-            force = tile(2, n)
-            damp = tile(3, n)
-            x = x_ref[n]
-            h = h_ref[n]
-            advanced = 2.0 * x - h + inverse * (drive * force - assembled - damp * x)
-            in_ref[n] = jnp.where(first, advanced, assembled)
-            rec_ref[n] = is_box * assembled + (1.0 - is_box) * (x - h)
-        stiffness_lines(in_ref, scale_ref, y_ref)
-        seen = jnp.zeros(shape, jnp.float32)
-        for n in range(NODES):
-            inverse = tile(1, n)
-            damp = tile(3, n)
-            x = x_ref[n]
-            h = h_ref[n]
-            dx = damp * x
-            adjoint = 2.0 * keep * x - h + inverse * (stiff * y_ref[n] - keep * dx + begin * x)
-            x_ref[n] = jnp.where(first, in_ref[n], adjoint)
-            h_ref[n] = keep * (x - inverse * dx) + begin * (inverse * x)
-            source = jnp.where(
-                forced,
-                jnp.broadcast_to(rec_ref[n][0:1], shape),
-                jnp.broadcast_to(adjoint[1:2], shape),
+        extra = partner_faces(y_ref, face_ref, side, 0, 2)
+        code = code_ref[SLOTS]
+        seen = zero
+        for bc in range(25):
+            assembled = tile_of(y_ref, bc, 0, 2) + extra[bc]
+            inverse = tile_of(inverse_ref, bc)
+            x = tile_of(state_ref, bc, 0, 2)
+            h = tile_of(hc_ref, bc)
+            dx = tile_of(damp_ref, bc) * x
+            advanced = 2.0 * x - h + inverse * (drive * tile_of(force_ref, bc) - assembled - dx)
+            set_tile(state_ref, advanced, bc, 0, 2)
+            set_tile(hc_ref, x - inverse * dx, bc)
+            noted = is_box * assembled + (1.0 - is_box) * (x - h)
+            seen = seen + jnp.where(code == bc, noted, 0.0)
+        seen_ref[moment, SLOTS : SLOTS + 1] = jnp.sum(seen, axis=0, keepdims=True)
+        extra = partner_faces(z_ref, face_ref, side)
+        for bc in range(25):
+            set_tile(state_ref, tile_of(z_ref, bc) + extra[bc], bc, 1, 2)
+        stiffness_tiles(state_ref, scale_ref, y_ref, grad_ref, 2, True)
+        codes = [code_ref[q] for q in range(SLOTS)]
+        seen = [zero] * SLOTS
+        for bc in range(25):
+            inverse = tile_of(inverse_ref, bc)
+            x = tile_of(z_ref, bc)
+            h = tile_of(hz_ref, bc)
+            dx = tile_of(damp_ref, bc) * x
+            adjoint = (2.0 * keep) * x - h + inverse * (
+                stiff * tile_of(y_ref, bc, 1, 2) - keep * dx + begin * x
             )
-            seen = seen + jnp.where(wanted == n, source, 0.0)
-        seen_ref[moment] = seen + pltpu.roll(seen, HALF, 1)
+            set_tile(z_ref, adjoint, bc)
+            set_tile(hz_ref, keep * (x - inverse * dx) + begin * (inverse * x), bc)
+            for q in range(SLOTS):
+                seen[q] = seen[q] + jnp.where(codes[q] == bc, adjoint, 0.0)
+        for q in range(SLOTS):
+            seen_ref[moment, q : q + 1] = jnp.sum(seen[q], axis=0, keepdims=True)
         return 0
 
     lax.fori_loop(0, STEPS, step, 0)
+    for n in range(STEPS):
+        rows = seen_ref[n]
+        seen_ref[n] = rows + pltpu.roll(rows, HALF, 1)
     for k in range(FREE_ROWS):
         out_ref[0, k : k + 1] = jnp.where(
             lane_low,
@@ -703,12 +774,17 @@
     both_ref,
     spread_ref,
     input_ref,
-    data_ref,
+    scale_ref,
+    inverse_ref,
+    force_ref,
+    damp_ref,
     x_ref,
+    old_ref,
     h_ref,
     y_ref,
+    grad_ref,
+    face_ref,
     kick_ref,
-    flat_ref,
 ):
     is_box = where_ref[0] == 0
     parity = where_ref[1] % 2
@@ -760,57 +836,65 @@
     for c in range(3):
         point_key = across(note[6 + c : 7 + c])
         for g in range(3):
-            spread_ref[c, :, g * LANES : (g + 1) * LANES] = one_hot(
-                point_key == note[9 + g : 10 + g]
-            )
-    group = lax.broadcasted_iota(jnp.int32, (3, LANES), 0)
-    side = jnp.where(group == 0, note[12:13].astype(jnp.int32), -1)
+            matrix = one_hot(point_key == note[9 + g : 10 + g])
+            spread_ref[c * LANES : (c + 1) * LANES, g * LANES : (g + 1) * LANES] = matrix
+            spread_ref[(c + 3) * LANES : (c + 4) * LANES, g * LANES : (g + 1) * LANES] = matrix
+    side = jnp.broadcast_to(note[12:13].astype(jnp.int32), (8, LANES))
     own_fields = [
-        weight_ref[...] * wave_ref[0],
-        DT_SQUARED * mass_ref[0],
-        source_ref[0],
+        weight_ref[...] * wave_ref[:, 0, :],
+        DT_SQUARED * mass_ref[:, 0, :],
+        source_ref[:, 0, :],
         count_ref[...][:NODES],
     ]
-    for k in range(4):
-        flat_ref[0:LANES] = pair_ref[k]
-        flat_ref[LANES : LANES + NODES] = own_fields[k][:, :LANES]
-        flat_ref[2 * LANES : 2 * LANES + NODES] = own_fields[k][:, LANES:]
-        for n in range(NODES):
-            value = flat_ref[pl.ds(n, 3, stride=LANES)]
-            data_ref[k, n] = PENALTY * value if k == 3 else value
-    for n in range(NODES):
-        x_ref[n] = zero[:3]
-        h_ref[n] = zero[:3]
-        y_ref[n] = zero[:3]
+    kick_ref[...] = jnp.zeros(kick_ref.shape, jnp.float32)
+    for k, out in enumerate((scale_ref, inverse_ref, force_ref, damp_ref)):
+        kick_ref[0:NODES] = pair_ref[k][:NODES]
+        kick_ref[200 : 200 + NODES] = own_fields[k][:, :LANES]
+        kick_ref[400 : 400 + NODES] = own_fields[k][:, LANES:]
+        for g in range(3):
+            load_tiles(kick_ref, out, PENALTY if k == 3 else None, g, 3, 200 * g)
+    for g in range(3):
+        for bc in range(40):
+            set_tile(y_ref, zero, bc, g, 3)
+        for bc in range(25):
+            set_tile(x_ref, zero, bc, g, 3)
+            set_tile(h_ref, zero, bc, g, 3)
     point_node = note[3:6].astype(jnp.int32)
     node_row = lax.broadcasted_iota(jnp.int32, (LANES, LANES), 0)
 
     def step(moment, _):
         drive = time_ref[0, moment]
         inputs = input_ref[moment]
-        kick = jnp.zeros((LANES, 3 * LANES), jnp.float32)
-        for c in range(3):
-            chosen = jnp.where(node_row == point_node[c : c + 1], inputs[c : c + 1], 0.0)
-            for _ in range(3):
-                part = chosen.astype(jnp.bfloat16)
-                kick = kick + jnp.dot(part, spread_ref[c], preferred_element_type=jnp.float32)
-                chosen = chosen - part.astype(jnp.float32)
-        for c in range(3):
-            kick_ref[c * LANES : (c + 1) * LANES] = kick[:, c * LANES : (c + 1) * LANES]
-        extra = partner_faces(lambda k: y_ref[k], side)
-        for n in range(NODES):
-            assembled = y_ref[n] if extra[n] is None else y_ref[n] + extra[n]
-            inverse = data_ref[1, n]
-            damp = data_ref[3, n]
-            x = x_ref[n]
-            h = h_ref[n]
-            arrived = kick_ref[pl.ds(n, 3, stride=LANES)]
-            dx = damp * x
-            advanced = 2.0 * x - h + inverse * (drive * data_ref[2, n] - assembled - dx + arrived)
-            h_ref[n] = x - inverse * dx
-            flat_ref[pl.ds(n, 3, stride=LANES)] = x
-            x_ref[n] = advanced
-        stiffness_lines(x_ref, data_ref.at[0], y_ref)
+        chosen = [
+            jnp.where(node_row == point_node[c : c + 1], inputs[c : c + 1], 0.0) for c in range(3)
+        ]
+        high = [part.astype(jnp.bfloat16) for part in chosen]
+        rest = [
+            (part - top.astype(jnp.float32)).astype(jnp.bfloat16) for part, top in zip(chosen, high)
+        ]
+        kick = jnp.dot(
+            jnp.concatenate(high + rest, axis=1), spread_ref[...], preferred_element_type=jnp.float32
+        )
+        for g in range(3):
+            kick_ref[200 * g : 200 * g + LANES] = kick[:, g * LANES : (g + 1) * LANES]
+        extra = partner_faces(y_ref, face_ref, side, 0, 3)
+        for g in range(3):
+            for bc in range(25):
+                assembled = tile_of(y_ref, bc, g, 3)
+                if g == 0:
+                    assembled = assembled + extra[bc]
+                inverse = tile_of(inverse_ref, bc, g, 3)
+                x = tile_of(x_ref, bc, g, 3)
+                h = tile_of(h_ref, bc, g, 3)
+                arrived = kick_ref[pl.ds(200 * g + bc, 8, stride=25), :]
+                dx = tile_of(damp_ref, bc, g, 3) * x
+                advanced = 2.0 * x - h + inverse * (
+                    drive * tile_of(force_ref, bc, g, 3) - assembled - dx + arrived
+                )
+                set_tile(h_ref, x - inverse * dx, bc, g, 3)
+                set_tile(old_ref, x, bc, g, 3)
+                set_tile(x_ref, advanced, bc, g, 3)
+        stiffness_tiles(x_ref, scale_ref, y_ref, grad_ref, 3, False)
         return 0
 
     lax.fori_loop(0, STEPS, step, 0)
@@ -820,28 +904,24 @@
     ).astype(jnp.bfloat16)
     alone = home < 0
 
-    def put(out_ref):
-        rest = flat_ref[0:LANES]
-        moved = jnp.zeros((LANES, 2 * LANES), jnp.float32)
-        for _ in range(3):
-            part = rest.astype(jnp.bfloat16)
-            moved = moved + jnp.dot(part, linked, preferred_element_type=jnp.float32)
-            rest = rest - part.astype(jnp.float32)
+    for tiles_ref, out_ref in ((old_ref, before_ref), (x_ref, now_ref)):
+        for g in range(3):
+            for bc in range(25):
+                kick_ref[pl.ds(200 * g + bc, 8, stride=25), :] = tile_of(tiles_ref, bc, g, 3)
+        moved = exact_pick(kick_ref[0:LANES], linked)
         for g in range(2):
-            own = flat_ref[(g + 1) * LANES : (g + 2) * LANES]
+            own = kick_ref[200 * (g + 1) : 200 * (g + 1) + LANES]
             cut = slice(g * LANES, (g + 1) * LANES)
-            merged = jnp.where(alone[:, cut], own, moved[:, cut])
-            out_ref[0, :, cut] = merged[:NODES]
-
-    put(before_ref)
-    for n in range(NODES):
-        flat_ref[pl.ds(n, 3, stride=LANES)] = x_ref[n]
-    put(now_ref)
+            out_ref[:, 0, cut] = jnp.where(alone[:, cut], own, moved[:, cut])[:NODES]
 
 
 def fast_body(wave_speed, inverse_mass, source_field, source_time, face_links, coupling_links):
     _, weight_np, _ = node_tables()
     weight = jnp.asarray(weight_np).reshape(NODES, 1)
+    wave, mass, source = [
+        jnp.transpose(field, (1, 0, 2)) for field in (wave_speed, inverse_mass, source_field)
+    ]
+    faces = jnp.transpose(face_links, (1, 0, 2))
     blocks = lax.axis_size("blk")
     columns = wave_speed.shape[-1]
     me = lax.axis_index("blk")
@@ -857,25 +937,28 @@
         out_shape=[shape(blocks, 8, LANES)] + [shape(16, 4 * LANES)] * 4 + [shape(LANES, columns)],
         in_specs=[smem] + [vmem] * 6,
         out_specs=[vmem] * 6,
-    )(place, wave_speed, inverse_mass, source_field, weight, face_links, coupling_links)
+    )(place, wave, mass, source, weight, faces, coupling_links)
     every = lax.all_to_all(links, "blk", 0, 0, tiled=True)
     mine = [m0, m1, m2, m3]
     ghost = [partner_2(part, "blk", j) for j, part in enumerate(mine)]
-    full = pltpu.VMEM((NODES, 8, LANES), jnp.float32)
+
+    def tiles(count):
+        return pltpu.VMEM((8 * count, LANES), jnp.float32)
+
     payload, pair, note = pl.pallas_call(
         response_kernel,
         out_shape=[shape(blocks, PAYLOAD, LANES), shape(4, LANES, LANES), shape(16, LANES)],
         in_specs=[smem] * 2 + [vmem] * 14,
         out_specs=[vmem] * 3,
-        scratch_shapes=[pltpu.VMEM((4, LANES, LANES), jnp.float32)]
-        + [full] * 7
-        + [pltpu.VMEM((STEPS, 8, LANES), jnp.float32)],
+        scratch_shapes=[tiles(25)] * 5
+        + [tiles(50), tiles(40), tiles(25), tiles(25), tiles(80), tiles(50), tiles(5)]
+        + [pltpu.VMEM((8, 8, LANES), jnp.int32), pltpu.VMEM((STEPS, 8, LANES), jnp.float32)],
     )(
         place,
         source_time,
-        wave_speed,
-        inverse_mass,
-        source_field,
+        wave,
+        mass,
+        source,
         weight,
         count,
         *mine,
@@ -891,34 +974,29 @@
     overflow = jnp.max(
         jnp.maximum(received[:, FLAG_ROW, 0], sibling[:, FLAG_ROW, 0])
     ) > 0
-    three = pltpu.VMEM((NODES, 3, LANES), jnp.float32)
 
     def quick(_):
         return tuple(
             pl.pallas_call(
                 final_kernel,
-                out_shape=[shape(1, NODES, columns)] * 2,
+                out_shape=[shape(NODES, 1, columns)] * 2,
                 in_specs=[smem] * 2 + [vmem] * 9,
                 out_specs=[vmem] * 2,
                 scratch_shapes=[
                     pltpu.VMEM((2, blocks, PAYLOAD, LANES), jnp.float32),
-                    pltpu.VMEM((3, LANES, 3 * LANES), jnp.bfloat16),
+                    pltpu.VMEM((6 * LANES, 3 * LANES), jnp.bfloat16),
                     pltpu.VMEM((STEPS, 8, LANES), jnp.float32),
-                    pltpu.VMEM((4, NODES, 3, LANES), jnp.float32),
-                    three,
-                    three,
-                    three,
-                    pltpu.VMEM((3 * LANES, LANES), jnp.float32),
-                    pltpu.VMEM((3 * LANES, LANES), jnp.float32),
-                ],
+                ]
+                + [tiles(75)] * 7
+                + [tiles(120), tiles(75), tiles(5), tiles(75)],
             )(
                 place,
                 source_time,
                 received,
                 sibling,
-                wave_speed,
-                inverse_mass,
-                source_field,
+                wave,
+                mass,
+                source,
                 weight,
                 count,
                 pair,
@@ -927,11 +1005,13 @@
         )
 
     def slow(_):
-        return general_body(
+        results = general_body(
             wave_speed, inverse_mass, source_field, source_time, face_links, coupling_links
         )
-
-    return lax.cond(overflow, slow, quick, 0)
+        return tuple(jnp.transpose(field, (1, 0, 2)) for field in results)
+
+    now, before = lax.cond(overflow, slow, quick, 0)
+    return (jnp.transpose(now, (1, 0, 2)), jnp.transpose(before, (1, 0, 2)))
 
 
 def body(*arguments):

time: 92.1 us -> 67.2 us (0.73)
  Pallas kernels: 47.2 us -> 30.8 us
  local copies, waits for them, and re-layouts: 9.68 us -> 1.32 us
    pallas_call x1, Pallas kernels: 19.6 us -> 11.4 us  [fast_body(): pl.pallas_call(response_kernel, out_shape=[shape(blocks, PAYLOAD, LANES),...]
    pallas_call x1, Pallas kernels: 25.1 us -> 16.9 us  [quick(): pl.pallas_call(final_kernel, out_shape=[shape(NODES, 1, columns)] * 2, in...]
    unnamed x36 -> x24, local copies, waits for them, and re-layouts: 5.2 us -> 1.32 us
    cond x4 -> x0, local copies, waits for them, and re-layouts: 2.51 us -> none  [the longest x2 2.5 us: fast_body(): return lax.cond(overflow, slow, quick, 0)]
    another operation x3 -> x0, local copies, waits for them, and re-layouts: 1.97 us -> none
where the time goes in v3:
time: 67.2 us; the launch traced here: 66.8 us
  Pallas kernels  30.8 us (46%)
  blocking collectives  14.5 us (22%)
  starting transfers between devices  13.4 us (20%)
  waiting for transfers between devices  4.62 us (7%)
  between operations  1.36 us (2%)
  local copies, waits for them, and re-layouts  1.32 us (2%)
  other arithmetic  0.69 us (1%)
    pallas_call x1, Pallas kernels, quick(): pl.pallas_call(final_kernel, out_shape=[shape(NODES, 1, columns)] * 2, in...  16.9 us
    all_to_all x1, blocking collectives, fast_body(): lax.all_to_all(payload, ('sec', 'blk'), 0, 0, axis_index_groups=same_core...  14.5 us
    pallas_call x1, Pallas kernels, fast_body(): pl.pallas_call(response_kernel, out_shape=[shape(blocks, PAYLOAD, LANES),...  11.4 us
    all_to_all x1, starting transfers between devices, fast_body(): every = lax.all_to_all(links, 'blk', 0, 0, tiled=True)  7.49 us
    ppermute x5, starting transfers between devices, partner_2(): lax.ppermute(value, axis, [(i, i ^ 1 << stride) for i in range(lax.axis_s...  5.92 us
    ppermute x5, waiting for transfers between devices, partner_2(): lax.ppermute(value, axis, [(i, i ^ 1 << stride) for i in range(lax.axis_s...  4.61 us
    pallas_call x1, Pallas kernels, fast_body(): pl.pallas_call(pack_kernel, out_shape=[shape(blocks, 8, LANES)] + [shape(...  2.52 us
  transfers between devices with their start and end apart: 6, of which 3 were waited for; matrix products, arithmetic and copies ran while one was open for 0% of the time, Pallas kernels for 0%

profile of v3, /device:TPU:0, one launch (start us, length us, event | category | flops | bytes accessed | tf_op | source)
XLA Modules:
  0.0 66.8 jit_solution(5164667742624825634)
XLA Ops:
  0.6 0.1 pad_add_fusion.2.where_ref
  0.7 0.6 copy-done.8
  1.3 0.1 copy-done.13
  1.4 2.5 %shard_map.129 = (f32[16,8,128]{2,1,0:T(8,128)}, f32[16,512]{1,0:T(8,128)}, f32[16,512]{1,0:T(8,128)}, f32[16,512]{1,0:T(8,128)}, f32[16,512]{1,0:T(8,128)}, /*index=5*/f32[128,256]{1,0:T(8,128)S(1)}) custom-call(s32[2]{0:T(128)S(1)} %pad_add_fusion.2.where_ref, f32[125,1,256]{2,1,0:T(1,128)} %bitcast.335, f32[125,1,256]{2,1,0:T(1,128)} %bitcast.338, ...), custom_call_target="tpu_custom_call" | custom-call | tf_op jit(solution)/shard_map/pallas_call | solution.py:935
  3.9 7.5 %all-to-all-start.2 = ((f32[16,8,128]{2,1,0:T(8,128)}), f32[16,8,128]{2,1,0:T(8,128)S(1)}, u32[]{:S(2)}, u32[]{:S(2)}) async-start(f32[16,8,128]{2,1,0:T(8,128)} %get-tuple-element.480), calls=%async_computation.2 | async-start | bytes 131072 | tf_op jit(solution)/shard_map/all_to_all | solution.py:941
  11.4 0.4 collective-permute-start.5
  11.8 1.7 %collective-permute-start.6 = (f32[16,512]{1,0:T(8,128)}, f32[16,512]{1,0:T(8,128)S(1)}, u32[]{:S(2)}, u32[]{:S(2)}) collective-permute-start(f32[16,512]{1,0:T(8,128)} %get-tuple-element.477.m1_ref), channel_id=1, source_target_pairs={{0,2},{1,3},{2,0},{3,1},{4,6},{5,7},{6,4},{7,5},{8,10},{9,11},{10,... | collective-permute-start | bytes 98312 | tf_op jit(solution)/shard_map/ppermute | solution.py:18
  13.5 1.5 %collective-permute-start.7 = (f32[16,512]{1,0:T(8,128)}, f32[16,512]{1,0:T(8,128)S(1)}, u32[]{:S(2)}, u32[]{:S(2)}) collective-permute-start(f32[16,512]{1,0:T(8,128)} %get-tuple-element.478.m2_ref), channel_id=1, source_target_pairs={{0,4},{1,5},{2,6},{3,7},{4,0},{5,1},{6,2},{7,3},{8,12},{9,13},{10,... | collective-permute-start | bytes 98312 | tf_op jit(solution)/shard_map/ppermute | solution.py:18
  15.0 2.4 %collective-permute-start.8 = (f32[16,512]{1,0:T(8,128)}, f32[16,512]{1,0:T(8,128)S(1)}, u32[]{:S(2)}, u32[]{:S(2)}) collective-permute-start(f32[16,512]{1,0:T(8,128)} %get-tuple-element.479.m3_ref), channel_id=1, source_target_pairs={{0,8},{1,9},{2,10},{3,11},{4,12},{5,13},{6,14},{7,15},{8,0},{9,1},... | collective-permute-start | bytes 98312 | tf_op jit(solution)/shard_map/ppermute | solution.py:18
  17.3 0.0 collective-permute-done.5.g0_ref
  17.4 0.0 collective-permute-done.6.g1_ref
  17.4 0.0 copy-start.10
  17.4 0.3 collective-permute-done.7.g2_ref
  17.6 2.7 %collective-permute-done.8.g3_ref = f32[16,512]{1,0:T(8,128)S(1)} collective-permute-done((f32[16,512]{1,0:T(8,128)}, f32[16,512]{1,0:T(8,128)S(1)}, u32[]{:S(2)}, u32[]{:S(2)}) %collective-permute-start.8) | collective-permute-done | bytes 32800 | tf_op jit(solution)/shard_map/ppermute | solution.py:18
  20.4 0.0 all-to-all-done.2.every_ref
  20.4 0.6 copy-done.12
  21.0 0.0 copy-done.7
  21.0 11.4 %shard_map.130 = (f32[16,40,128]{2,1,0:T(8,128)}, f32[4,128,128]{2,1,0:T(8,128)S(1)}, f32[16,128]{1,0:T(8,128)S(1)}) custom-call(s32[2]{0:T(128)S(1)} %pad_add_fusion.2.where_ref, f32[1,12]{1,0:T(1,128)S(1)} %copy-done.14, f32[125,1,256]{2,1,0:T(1,128)S(1)} %bitcast.336, f32[125,1,256]{2,1,0:T(1,128)S(1)} %bitcast.339, f32[125,1,256]{2,1,0:T(1,128)S(1)} %bitcast.342, ...), custom_call_target="tpu_custom_call" | custom-call | tf_op jit(solution)/shard_map/pallas_call | solution.py:948
  32.4 14.5 %all_to_all.33 = f32[16,40,128]{2,1,0:T(8,128)S(1)} all-to-all(f32[16,40,128]{2,1,0:T(8,128)} %get-tuple-element.481), channel_id=1, replica_groups={{0,2,4,6,8,10,12,14,16,18,20,22,24,26,28,30},{1,3,5,7,9,11,13,15,17,19,..., dimensions={0} | all-to-all | bytes 655360 | tf_op jit(solution)/shard_map/all_to_all | solution.py:970
  47.0 0.0 collective-permute-start.9
  47.0 1.6 %collective-permute-done.9 = f32[16,40,128]{2,1,0:T(8,128)S(1)} collective-permute-done((f32[16,40,128]{2,1,0:T(8,128)S(1)}, f32[16,40,128]{2,1,0:T(8,128)S(1)}, u32[]{:S(2)}, u32[]{:S(2)}) %collective-permute-start.9) | collective-permute-done | bytes 327712 | tf_op jit(solution)/shard_map/ppermute | solution.py:18
  48.6 0.6 fusion.32
  49.9 16.9 %conditional.1 = (f32[1,125,256]{2,0,1:T(1,128)}, f32[1,125,256]{2,0,1:T(1,128)}) conditional(s32[]{:T(128)} %convert_element_type.23, (s32[2]{0:T(128)S(1)}, f32[1,12]{1,0:T(1,128)S(1)}, f32[16,40,128]{2,1,0:T(8,128)S(1)}, f32[16,40,128]{2,1,0:T(8,128)S(1)}, f32[125,1,256]{2,1,0:T(1,128)S(1)}, /*index=5*/f32[125,1,256]{2,1,0:T(1,128)S(1)}, ...), branch_computations={%region_1.0_spmd, %region_2.15_spmd} | conditional | flops 347599744 | bytes 9835607 | solution.py:1013
  49.9 16.9 %branch_0_fun.1 = (f32[125,1,256]{2,1,0:T(1,128)}, f32[125,1,256]{2,1,0:T(1,128)}) custom-call(s32[2]{0:T(128)S(1)} %get-tuple-element.413.where_ref, f32[1,12]{1,0:T(1,128)S(1)} %get-tuple-element.414.time_ref, f32[16,40,128]{2,1,0:T(8,128)S(1)} %get-tuple-element.415.mine_ref, f32[16,40,128]{2,1,0:T(8,128)S(1)} %get-tuple-element.416.other_ref, ...), custom_call_target="tpu_custom_call" | custom-call | tf_op jit(solution)/shard_map/cond/branch_0_fun/pallas_call | solution.py:980
  (19 shorter events, 0.0 us)
Async XLA Ops:
  0.6 0.7 %copy-start.8 = (s32[5,512]{1,0:T(8,128)S(1)}, s32[5,512]{1,0:T(8,128)}, u32[]{:S(2)}) copy-start(s32[5,512]{1,0:T(8,128)} %couple_ref.1) | copy-start | bytes 30724
  0.7 0.7 %copy-start.13 = (s32[1,3,128]{2,0,1:T(1,128)S(1)}, s32[1,3,128]{2,0,1:T(1,128)}, u32[]{:S(2)}) copy-start(s32[1,3,128]{2,0,1:T(1,128)} %param.19) | copy-start | bytes 4612
  1.4 19.6 %copy-start.3 = (f32[1,125,256]{2,0,1:T(1,128)S(1)}, f32[1,125,256]{2,0,1:T(1,128)}, u32[]{:S(2)}) copy-start(f32[1,125,256]{2,0,1:T(1,128)} %param.16) | copy-start | bytes 384004
  1.4 19.6 %copy-start.4 = (f32[1,125,256]{2,0,1:T(1,128)S(1)}, f32[1,125,256]{2,0,1:T(1,128)}, u32[]{:S(2)}) copy-start(f32[1,125,256]{2,0,1:T(1,128)} %param.17) | copy-start | bytes 384004
  1.4 19.6 %copy-start.6 = (f32[125,1]{1,0:T(8,128)S(1)}, f32[125,1]{1,0:T(8,128)}, u32[]{:S(2)}) copy-start(f32[125,1]{1,0:T(8,128)} %constant.131.clone.weight_ref) | copy-start | bytes 1504
  3.9 17.1 %copy-start.2 = (f32[1,125,256]{2,0,1:T(1,128)S(1)}, f32[1,125,256]{2,0,1:T(1,128)}, u32[]{:S(2)}) copy-start(f32[1,125,256]{2,0,1:T(1,128)} %param.15) | copy-start | bytes 384004
  3.9 16.4 %all-to-all-start.2 = ((f32[16,8,128]{2,1,0:T(8,128)}), f32[16,8,128]{2,1,0:T(8,128)S(1)}, u32[]{:S(2)}, u32[]{:S(2)}) async-start(f32[16,8,128]{2,1,0:T(8,128)} %get-tuple-element.480), calls=%async_computation.2 | async-start | bytes 131072 | tf_op jit(solution)/shard_map/all_to_all | solution.py:941
  11.4 5.9 %collective-permute-start.5 = (f32[16,512]{1,0:T(8,128)}, f32[16,512]{1,0:T(8,128)S(1)}, u32[]{:S(2)}, u32[]{:S(2)}) collective-permute-start(f32[16,512]{1,0:T(8,128)} %get-tuple-element.476.m0_ref), channel_id=1, source_target_pairs={{0,1},{1,0},{2,3},{3,2},{4,5},{5,4},{6,7},{7,6},{8,9},{9,8},{10,11... | collective-permute-start | bytes 98312 | tf_op jit(solution)/shard_map/ppermute | solution.py:18
  11.8 5.5 %collective-permute-start.6 = (f32[16,512]{1,0:T(8,128)}, f32[16,512]{1,0:T(8,128)S(1)}, u32[]{:S(2)}, u32[]{:S(2)}) collective-permute-start(f32[16,512]{1,0:T(8,128)} %get-tuple-element.477.m1_ref), channel_id=1, source_target_pairs={{0,2},{1,3},{2,0},{3,1},{4,6},{5,7},{6,4},{7,5},{8,10},{9,11},{10,... | collective-permute-start | bytes 98312 | tf_op jit(solution)/shard_map/ppermute | solution.py:18
  13.5 4.1 %collective-permute-start.7 = (f32[16,512]{1,0:T(8,128)}, f32[16,512]{1,0:T(8,128)S(1)}, u32[]{:S(2)}, u32[]{:S(2)}) collective-permute-start(f32[16,512]{1,0:T(8,128)} %get-tuple-element.478.m2_ref), channel_id=1, source_target_pairs={{0,4},{1,5},{2,6},{3,7},{4,0},{5,1},{6,2},{7,3},{8,12},{9,13},{10,... | collective-permute-start | bytes 98312 | tf_op jit(solution)/shard_map/ppermute | solution.py:18
  15.0 6.0 %copy-start.14 = (f32[1,12]{1,0:T(1,128)S(1)}, f32[1,12]{1,0:T(1,128)}, u32[]{:S(2)}) copy-start(f32[1,12]{1,0:T(1,128)} %coef_ref.1) | copy-start | bytes 148
  15.0 5.4 %collective-permute-start.8 = (f32[16,512]{1,0:T(8,128)}, f32[16,512]{1,0:T(8,128)S(1)}, u32[]{:S(2)}, u32[]{:S(2)}) collective-permute-start(f32[16,512]{1,0:T(8,128)} %get-tuple-element.479.m3_ref), channel_id=1, source_target_pairs={{0,8},{1,9},{2,10},{3,11},{4,12},{5,13},{6,14},{7,15},{8,0},{9,1},... | collective-permute-start | bytes 98312 | tf_op jit(solution)/shard_map/ppermute | solution.py:18
  17.4 3.0 %copy-start.9 = (f32[16,512]{1,0:T(8,128)}, f32[16,512]{1,0:T(8,128)S(1)}, u32[]{:S(2)}) copy-start(f32[16,512]{1,0:T(8,128)S(1)} %collective-permute-done.5.g0_ref) | copy-start | bytes 98308
  17.4 3.0 %copy-start.10 = (f32[16,512]{1,0:T(8,128)}, f32[16,512]{1,0:T(8,128)S(1)}, u32[]{:S(2)}) copy-start(f32[16,512]{1,0:T(8,128)S(1)} %collective-permute-done.6.g1_ref) | copy-start | bytes 98308
  17.6 2.7 %copy-start.11 = (f32[16,512]{1,0:T(8,128)}, f32[16,512]{1,0:T(8,128)S(1)}, u32[]{:S(2)}) copy-start(f32[16,512]{1,0:T(8,128)S(1)} %collective-permute-done.7.g2_ref) | copy-start | bytes 98308
  20.4 0.6 copy-start.12
  20.4 0.6 copy-start.7
  47.0 1.6 %collective-permute-start.9 = (f32[16,40,128]{2,1,0:T(8,128)S(1)}, f32[16,40,128]{2,1,0:T(8,128)S(1)}, u32[]{:S(2)}, u32[]{:S(2)}) collective-permute-start(f32[16,40,128]{2,1,0:T(8,128)S(1)} %all_to_all.33), channel_id=1, source_target_pairs={{0,1},{1,0},{2,3},{3,2},{4,5},{5,4},{6,7},{7,6},{8,9},{9,8},{10,11... | collective-permute-start | bytes 983048 | tf_op jit(solution)/shard_map/ppermute | solution.py:18

commit v4 on v3

--- a/solution.py
+++ b/solution.py
@@ -191,14 +191,14 @@
 
 LANES = 128
 HALF = 64
-SLOTS = 6
+OTHERS = 5
 LAGS = 10
 PAIRS = LAGS // 2
 FREE_ROWS = STEPS // 2
 GAIN_ROW = FREE_ROWS
-INDEX_ROW = GAIN_ROW + SLOTS * PAIRS
-FLAG_ROW = INDEX_ROW + SLOTS // 2
-PAYLOAD = FLAG_ROW + 1
+EXTRA_ROW = GAIN_ROW + PAIRS
+INDEX_ROW = EXTRA_ROW + PAIRS
+PAYLOAD = INDEX_ROW + 1
 NODES = 125
 EXACT = lax.Precision.HIGHEST
 
@@ -507,6 +507,17 @@
         element, node, _ = chunks[c]
         keys.append(jnp.where(node > 0.0, table * 256.0 + element - 1.0, -1.0))
     return chunks, keys
+
+
+def gather_packed(packed, at):
+    rows = at // LANES
+    lanes = at % LANES
+    out = jnp.zeros(at.shape, jnp.float32)
+    for k in range(8):
+        source = jnp.broadcast_to(packed[k : k + 1], at.shape)
+        picked = jnp.take_along_axis(source, lanes, axis=1, mode="promise_in_bounds")
+        out = jnp.where(rows == k, picked, out)
+    return out
 
 
 def response_kernel(
@@ -584,10 +595,11 @@
     ghost_key = jnp.where(lane_low, ghost_key, -5.0)
 
     match = [(across(keys[c]) == own_key) | (across(keys[c]) == ghost_key) for c in range(3)]
+    match[0] = match[0] & (down != right)
     matched = [jnp.where(m, 1.0, 0.0) for m in match]
     lower = one_hot(right < down)
     before = jnp.zeros((1, LANES), jnp.float32)
-    lists = [jnp.zeros((8, LANES), jnp.float32)] * SLOTS
+    lists = [jnp.zeros((8, LANES), jnp.float32)] * OTHERS
     for c in range(3):
         place = jnp.dot(lower, matched[c].astype(jnp.bfloat16), preferred_element_type=jnp.float32)
         place = jnp.where(match[c], place + before, -1.0)
@@ -598,26 +610,41 @@
         described = jnp.concatenate(
             [node_c, gid_high, gid_c - 256.0 * gid_high, table_c, jnp.zeros((4, LANES))], axis=0
         )
-        for q in range(SLOTS):
+        for q in range(OTHERS):
             lists[q] = lists[q] + plain_dot(described, one_hot(place == float(q)))
-    too_long = jnp.max(before) > float(SLOTS)
-    wanted_rows = []
-    gids = []
-    for q in range(SLOTS):
+    own_node = jnp.where(lane_low, node - 1.0, -1.0)
+    wanted = [own_node]
+    gids = [jnp.zeros((1, LANES), jnp.float32)]
+    for q in range(OTHERS):
         node_q = lists[q][0:1] - 1.0
         there = lists[q][3:4] > 0.0
         gids.append(lists[q][1:2] * 256.0 + lists[q][2:3])
-        wanted_rows.append(
+        wanted.append(
             jnp.where(
                 lane_low,
                 jnp.where(there, -1.0, node_q),
                 pltpu.roll(jnp.where(there, node_q, -1.0), HALF, 1),
             )
         )
-    own_node = jnp.where(lane_low, node - 1.0, -1.0)
-    wanted_rows.append(own_node)
-    wanted_rows.append(jnp.full((1, LANES), -1.0))
-    wanted = jnp.concatenate(wanted_rows, axis=0).astype(jnp.int32)
+    gids.append(jnp.zeros((7 - OTHERS, LANES), jnp.float32))
+
+    length = jnp.minimum(before, 200.0)
+    start = plain_dot(jnp.broadcast_to(length, (8, LANES)), one_hot(down < right))[0:1]
+    too_long = (jnp.max(before) > float(OTHERS)) | (jnp.max(start + length) > float(HALF))
+    entry = right % HALF
+    entry_f = entry.astype(jnp.float32)
+    is_point = down < HALF
+    owner_of = jnp.sum(
+        jnp.where(is_point & (across(start + length) <= entry_f), 1.0, 0.0), axis=0, keepdims=True
+    )
+    begun = jnp.sum(
+        jnp.where(down.astype(jnp.float32) == owner_of, across(start), 0.0), axis=0, keepdims=True
+    )
+    used = owner_of < float(HALF)
+    which = jnp.clip(entry_f[0:1] - begun, 0.0, float(OTHERS - 1)) + 1.0
+    entry_at = jnp.where(used, which * float(LANES) + owner_of, 0.0).astype(jnp.int32)
+    entry_at = jnp.broadcast_to(entry_at, (8, LANES))
+    entry_gid = jnp.where(used, gather_packed(jnp.concatenate(gids, axis=0), entry_at)[0:1], 0.0)
 
     take = [
         one_hot((down.astype(jnp.float32) + float(g * LANES + 1) == element_both) & (right < HALF))
@@ -664,8 +691,8 @@
     side = jnp.broadcast_to(side_row, (8, LANES))
     own_here = jnp.broadcast_to(own_node.astype(jnp.int32), (8, LANES))
     zero = jnp.zeros((8, LANES), jnp.float32)
-    for q in range(SLOTS + 1):
-        node_q = jnp.broadcast_to(wanted[q : q + 1], (8, LANES))
+    for q in range(OTHERS + 1):
+        node_q = jnp.broadcast_to(wanted[q], (8, LANES)).astype(jnp.int32)
         code_ref[q] = jnp.where((node_q >= 0) & (node_q // 25 == row), node_q % 25, -1)
     for bc in range(25):
         set_tile(z_ref, jnp.where(own_here == 25 * row + bc, jnp.where(row < 5, 1.0, 0.0), 0.0), bc)
@@ -673,6 +700,8 @@
         set_tile(hz_ref, zero, bc)
         set_tile(state_ref, zero, bc, 0, 2)
         set_tile(y_ref, zero, bc, 0, 2)
+    for n in range(STEPS):
+        seen_ref[n] = zero
     for bc in range(25, 40):
         set_tile(z_ref, zero, bc)
         set_tile(y_ref, zero, bc, 0, 2)
@@ -680,32 +709,34 @@
 
     is_box = jnp.where(where_ref[0] == 0, 1.0, 0.0)
 
+    def note_free(moment, drive):
+        extra = partner_faces(y_ref, face_ref, side, 0, 2)
+        code = code_ref[0]
+        seen = zero
+        for bc in range(25):
+            assembled = tile_of(y_ref, bc, 0, 2) + extra[bc]
+            x = tile_of(state_ref, bc, 0, 2)
+            h = tile_of(hc_ref, bc)
+            seen = seen + jnp.where(code == bc, is_box * assembled + (1.0 - is_box) * (x - h), 0.0)
+            if drive is not None:
+                inverse = tile_of(inverse_ref, bc)
+                dx = tile_of(damp_ref, bc) * x
+                advanced = 2.0 * x - h + inverse * (drive * tile_of(force_ref, bc) - assembled - dx)
+                set_tile(state_ref, advanced, bc, 0, 2)
+                set_tile(hc_ref, x - inverse * dx, bc)
+        seen_ref[moment, 7:8] = jnp.sum(seen, axis=0, keepdims=True)
+
     def step(moment, _):
-        drive = coef_ref[0, moment]
         keep = jnp.where(moment > 0, 1.0, 0.0)
         stiff = jnp.where(moment > 0, -1.0, is_box)
         begin = jnp.where(moment > 0, 0.0, 1.0 - is_box)
-        extra = partner_faces(y_ref, face_ref, side, 0, 2)
-        code = code_ref[SLOTS]
-        seen = zero
-        for bc in range(25):
-            assembled = tile_of(y_ref, bc, 0, 2) + extra[bc]
-            inverse = tile_of(inverse_ref, bc)
-            x = tile_of(state_ref, bc, 0, 2)
-            h = tile_of(hc_ref, bc)
-            dx = tile_of(damp_ref, bc) * x
-            advanced = 2.0 * x - h + inverse * (drive * tile_of(force_ref, bc) - assembled - dx)
-            set_tile(state_ref, advanced, bc, 0, 2)
-            set_tile(hc_ref, x - inverse * dx, bc)
-            noted = is_box * assembled + (1.0 - is_box) * (x - h)
-            seen = seen + jnp.where(code == bc, noted, 0.0)
-        seen_ref[moment, SLOTS : SLOTS + 1] = jnp.sum(seen, axis=0, keepdims=True)
+        note_free(moment, coef_ref[0, moment])
         extra = partner_faces(z_ref, face_ref, side)
         for bc in range(25):
             set_tile(state_ref, tile_of(z_ref, bc) + extra[bc], bc, 1, 2)
         stiffness_tiles(state_ref, scale_ref, y_ref, grad_ref, 2, True)
-        codes = [code_ref[q] for q in range(SLOTS)]
-        seen = [zero] * SLOTS
+        codes = [code_ref[q] for q in range(OTHERS + 1)]
+        seen = [zero] * (OTHERS + 1)
         for bc in range(25):
             inverse = tile_of(inverse_ref, bc)
             x = tile_of(z_ref, bc)
@@ -716,45 +747,32 @@
             )
             set_tile(z_ref, adjoint, bc)
             set_tile(hz_ref, keep * (x - inverse * dx) + begin * (inverse * x), bc)
-            for q in range(SLOTS):
+            for q in range(OTHERS + 1):
                 seen[q] = seen[q] + jnp.where(codes[q] == bc, adjoint, 0.0)
-        for q in range(SLOTS):
+        for q in range(OTHERS + 1):
             seen_ref[moment, q : q + 1] = jnp.sum(seen[q], axis=0, keepdims=True)
         return 0
 
-    lax.fori_loop(0, STEPS, step, 0)
+    lax.fori_loop(0, STEPS - 1, step, 0)
+    note_free(STEPS - 1, None)
+    seen = []
+    extras = []
     for n in range(STEPS):
         rows = seen_ref[n]
-        seen_ref[n] = rows + pltpu.roll(rows, HALF, 1)
+        rows = rows + pltpu.roll(rows, HALF, 1)
+        seen.append(rows)
+        extras.append(jnp.where(used, gather_packed(rows, entry_at)[0:1], 0.0))
     for k in range(FREE_ROWS):
-        out_ref[0, k : k + 1] = jnp.where(
-            lane_low,
-            seen_ref[2 * k][SLOTS : SLOTS + 1],
-            seen_ref[2 * k + 1][SLOTS : SLOTS + 1],
-        )
-    for q in range(SLOTS):
-        for k in range(PAIRS):
-            r = GAIN_ROW + q * PAIRS + k
-            out_ref[0, r : r + 1] = jnp.where(
-                lane_low, seen_ref[2 * k][q : q + 1], seen_ref[2 * k + 1][q : q + 1]
-            )
-    for q in range(0, SLOTS, 2):
-        r = INDEX_ROW + q // 2
-        out_ref[0, r : r + 1] = jnp.where(lane_low, gids[q], pltpu.roll(gids[q + 1], HALF, 1))
-    out_ref[0, FLAG_ROW : FLAG_ROW + 1] = jnp.full((1, LANES), jnp.where(too_long, 1.0, 0.0))
+        out_ref[0, k : k + 1] = jnp.where(lane_low, seen[2 * k][7:8], seen[2 * k + 1][7:8])
+    for k in range(PAIRS):
+        r = GAIN_ROW + k
+        out_ref[0, r : r + 1] = jnp.where(lane_low, seen[2 * k][0:1], seen[2 * k + 1][0:1])
+        r = EXTRA_ROW + k
+        out_ref[0, r : r + 1] = jnp.where(lane_low, extras[2 * k], extras[2 * k + 1])
+    starts = jnp.where(lane == HALF, jnp.where(too_long, 1.0, 0.0), pltpu.roll(start, HALF, 1))
+    out_ref[0, INDEX_ROW : INDEX_ROW + 1] = jnp.where(lane_low, entry_gid, starts)
     for k in range(1, out_ref.shape[0]):
         out_ref[k] = out_ref[0]
-
-
-def gather_packed(packed, at):
-    rows = at // LANES
-    lanes = at % LANES
-    out = jnp.zeros(at.shape, jnp.float32)
-    for k in range(8):
-        source = jnp.broadcast_to(packed[k : k + 1], at.shape)
-        picked = jnp.take_along_axis(source, lanes, axis=1, mode="promise_in_bounds")
-        out = jnp.where(rows == k, picked, out)
-    return out
 
 
 def final_kernel(
@@ -795,16 +813,19 @@
     def rows(section, core, r):
         return both_ref[core, section * 8 : section * 8 + 8, r, :]
 
+    row = lax.broadcasted_iota(jnp.int32, (8, LANES), 0)
+    point = lax.broadcasted_iota(jnp.int32, (8, LANES), 1) % HALF
     index = {}
     for s in range(2):
         for p in range(2):
-            for k in range(SLOTS // 2):
-                pair = rows(s, p, INDEX_ROW + k).astype(jnp.int32)
-                turned = pltpu.roll(pair, HALF, 1)
-                index[s, p, 2 * k] = jnp.where(low, pair, turned)
-                index[s, p, 2 * k + 1] = jnp.where(low, turned, pair)
+            pair = rows(s, p, INDEX_ROW).astype(jnp.int32)
+            turned = pltpu.roll(pair, HALF, 1)
+            start = jnp.where(point == 0, 0, jnp.where(low, turned, pair))
+            stop = jnp.where(point == HALF - 1, HALF, pltpu.roll(start, LANES - 1, 1))
+            own = point // CAPC * HALF + (2 * row + p) * CAPC + point % CAPC
+            index[s, p] = (own, jnp.where(low, pair, turned), start, stop)
     note = note_ref[...]
-    at = jnp.where(lax.broadcasted_iota(jnp.int32, (8, LANES), 0) < 3, note[0:8], 0.0).astype(jnp.int32)
+    at = jnp.where(row < 3, note[0:8], 0.0).astype(jnp.int32)
     packed = {}
     pairs = {}
     last = {}
@@ -815,12 +836,22 @@
             for p in range(2):
                 free = rows(s, p, n // 2)
                 total = jnp.where(low, free, 0.0) if n % 2 == 0 else jnp.where(low, 0.0, free)
-                for q in range(SLOTS):
-                    for k in range(PAIRS):
-                        m = n - 2 * k - 1
-                        if m >= 1:
-                            total = total + rows(s, p, GAIN_ROW + q * PAIRS + k) * pairs[s, p, q, m]
-                value[s, p] = total + pltpu.roll(total, HALF, 1)
+                more = zero
+                for k in range(PAIRS):
+                    m = n - 2 * k - 1
+                    if m >= 1:
+                        total = total + rows(s, p, GAIN_ROW + k) * pairs[s, p, 0, m]
+                        more = more + rows(s, p, EXTRA_ROW + k) * pairs[s, p, 1, m]
+                total = total + pltpu.roll(total, HALF, 1)
+                if n > 1:
+                    more = more + pltpu.roll(more, HALF, 1)
+                    _, _, start, stop = index[s, p]
+                    for q in range(OTHERS):
+                        got = jnp.take_along_axis(
+                            more, jnp.minimum(start + q, HALF - 1), axis=1, mode="promise_in_bounds"
+                        )
+                        total = total + jnp.where(start + q < stop, got, 0.0)
+                value[s, p] = total
         for s in range(2):
             packed[s] = jnp.where(low, value[s, 0], value[s, 1])
         packed[1] = PENALTY * packed[1]
@@ -828,11 +859,10 @@
         if n < STEPS - 1:
             for s in range(2):
                 for p in range(2):
-                    for q in range(SLOTS):
-                        got = gather_packed(packed[1 - s], index[s, p, q])
+                    for q in range(2):
+                        got = gather_packed(packed[1 - s], index[s, p][q])
                         pairs[s, p, q, n] = jnp.where(low, got, last.get((s, p, q), zero))
                         last[s, p, q] = got
-    input_ref[0] = zero
     for c in range(3):
         point_key = across(note[6 + c : 7 + c])
         for g in range(3):
@@ -854,16 +884,18 @@
         for g in range(3):
             load_tiles(kick_ref, out, PENALTY if k == 3 else None, g, 3, 200 * g)
     for g in range(3):
-        for bc in range(40):
+        for bc in range(25, 40):
             set_tile(y_ref, zero, bc, g, 3)
         for bc in range(25):
-            set_tile(x_ref, zero, bc, g, 3)
+            first = time_ref[0, 0] * tile_of(force_ref, bc, g, 3)
+            set_tile(x_ref, tile_of(inverse_ref, bc, g, 3) * first, bc, g, 3)
             set_tile(h_ref, zero, bc, g, 3)
     point_node = note[3:6].astype(jnp.int32)
     node_row = lax.broadcasted_iota(jnp.int32, (LANES, LANES), 0)
 
     def step(moment, _):
         drive = time_ref[0, moment]
+        stiffness_tiles(x_ref, scale_ref, y_ref, grad_ref, 3, False)
         inputs = input_ref[moment]
         chosen = [
             jnp.where(node_row == point_node[c : c + 1], inputs[c : c + 1], 0.0) for c in range(3)
@@ -894,10 +926,9 @@
                 set_tile(h_ref, x - inverse * dx, bc, g, 3)
                 set_tile(old_ref, x, bc, g, 3)
                 set_tile(x_ref, advanced, bc, g, 3)
-        stiffness_tiles(x_ref, scale_ref, y_ref, grad_ref, 3, False)
         return 0
 
-    lax.fori_loop(0, STEPS, step, 0)
+    lax.fori_loop(1, STEPS, step, 0)
     home = jnp.concatenate([note[13:14], note[14:15]], axis=1).astype(jnp.int32)
     linked = jnp.where(
         home == lax.broadcasted_iota(jnp.int32, (LANES, 2 * LANES), 0), 1.0, 0.0
@@ -928,6 +959,7 @@
     place = jnp.stack([lax.axis_index("sec"), me]).astype(jnp.int32)
     vmem = pl.BlockSpec(memory_space=pltpu.VMEM)
     smem = pl.BlockSpec(memory_space=pltpu.SMEM)
+    params = pltpu.CompilerParams(vmem_limit_bytes=16 << 20)
 
     def shape(*dims):
         return jax.ShapeDtypeStruct(dims, jnp.float32)
@@ -937,10 +969,11 @@
         out_shape=[shape(blocks, 8, LANES)] + [shape(16, 4 * LANES)] * 4 + [shape(LANES, columns)],
         in_specs=[smem] + [vmem] * 6,
         out_specs=[vmem] * 6,
+        compiler_params=params,
     )(place, wave, mass, source, weight, faces, coupling_links)
-    every = lax.all_to_all(links, "blk", 0, 0, tiled=True)
     mine = [m0, m1, m2, m3]
     ghost = [partner_2(part, "blk", j) for j, part in enumerate(mine)]
+    every = lax.all_to_all(links, "blk", 0, 0, tiled=True)
 
     def tiles(count):
         return pltpu.VMEM((8 * count, LANES), jnp.float32)
@@ -950,6 +983,7 @@
         out_shape=[shape(blocks, PAYLOAD, LANES), shape(4, LANES, LANES), shape(16, LANES)],
         in_specs=[smem] * 2 + [vmem] * 14,
         out_specs=[vmem] * 3,
+        compiler_params=params,
         scratch_shapes=[tiles(25)] * 5
         + [tiles(50), tiles(40), tiles(25), tiles(25), tiles(80), tiles(50), tiles(5)]
         + [pltpu.VMEM((8, 8, LANES), jnp.int32), pltpu.VMEM((STEPS, 8, LANES), jnp.float32)],
@@ -972,7 +1006,7 @@
     )
     sibling = partner_2(received, "blk", 0)
     overflow = jnp.max(
-        jnp.maximum(received[:, FLAG_ROW, 0], sibling[:, FLAG_ROW, 0])
+        jnp.maximum(received[:, INDEX_ROW, HALF], sibling[:, INDEX_ROW, HALF])
     ) > 0
 
     def quick(_):
@@ -982,6 +1016,7 @@
                 out_shape=[shape(NODES, 1, columns)] * 2,
                 in_specs=[smem] * 2 + [vmem] * 9,
                 out_specs=[vmem] * 2,
+                compiler_params=params,
                 scratch_shapes=[
                     pltpu.VMEM((2, blocks, PAYLOAD, LANES), jnp.float32),
                     pltpu.VMEM((6 * LANES, 3 * LANES), jnp.bfloat16),

time: 67.2 us -> 57.8 us (0.86)
  Pallas kernels: 30.8 us -> 24.7 us
  blocking collectives: 14.5 us -> 12.3 us
    pallas_call x1, Pallas kernels: 16.9 us -> 12.8 us  [quick(): pl.pallas_call(final_kernel, out_shape=[shape(NODES, 1, columns)] * 2, in...]
    all_to_all x1, blocking collectives: 14.5 us -> 12.3 us  [fast_body(): lax.all_to_all(payload, ('sec', 'blk'), 0, 0, axis_index_groups=same_core...]
    pallas_call x1, Pallas kernels: 11.4 us -> 9.79 us  [fast_body(): pl.pallas_call(response_kernel, out_shape=[shape(blocks, PAYLOAD, LANES),...]
where the time goes in v4:
time: 57.8 us; the launch traced here: 57.5 us
  Pallas kernels  24.7 us (43%)
  starting transfers between devices  13.4 us (23%)
  blocking collectives  12.3 us (21%)
  waiting for transfers between devices  4.24 us (7%)
  between operations  1.35 us (2%)
  other arithmetic  0.78 us (1%)
  local copies, waits for them, and re-layouts  0.7 us (1%)
    pallas_call x1, Pallas kernels, quick(): pl.pallas_call(final_kernel, out_shape=[shape(NODES, 1, columns)] * 2, in...  12.8 us
    all_to_all x1, blocking collectives, fast_body(): lax.all_to_all(payload, ('sec', 'blk'), 0, 0, axis_index_groups=same_core...  12.3 us
    pallas_call x1, Pallas kernels, fast_body(): pl.pallas_call(response_kernel, out_shape=[shape(blocks, PAYLOAD, LANES),...  9.79 us
    all_to_all x1, starting transfers between devices, fast_body(): every = lax.all_to_all(links, 'blk', 0, 0, tiled=True)  7.49 us
    ppermute x5, starting transfers between devices, partner_2(): lax.ppermute(value, axis, [(i, i ^ 1 << stride) for i in range(lax.axis_s...  5.92 us
    ppermute x5, waiting for transfers between devices, partner_2(): lax.ppermute(value, axis, [(i, i ^ 1 << stride) for i in range(lax.axis_s...  4.23 us
    pallas_call x1, Pallas kernels, fast_body(): pl.pallas_call(pack_kernel, out_shape=[shape(blocks, 8, LANES)] + [shape(...  2.05 us
  transfers between devices with their start and end apart: 6, of which 3 were waited for; matrix products, arithmetic and copies ran while one was open for 0% of the time, Pallas kernels for 0%

profile of v4, /device:TPU:0, one launch (start us, length us, event | category | flops | bytes accessed | tf_op | source)
XLA Modules:
  0.0 57.5 jit_solution(8182711181435641539)
XLA Ops:
  0.6 0.0 copy-start.7
  0.6 0.1 pad_add_fusion.2.where_ref
  0.7 0.6 %copy-done.7 = s32[5,512]{1,0:T(8,128)S(1)} copy-done((s32[5,512]{1,0:T(8,128)S(1)}, s32[5,512]{1,0:T(8,128)}, u32[]{:S(2)}) %copy-start.7) | copy-done | bytes 10264
  1.3 0.1 copy-done.8
  1.4 2.0 %shard_map.129 = (f32[16,8,128]{2,1,0:T(8,128)}, f32[16,512]{1,0:T(8,128)S(1)}, f32[16,512]{1,0:T(8,128)S(1)}, f32[16,512]{1,0:T(8,128)S(1)}, f32[16,512]{1,0:T(8,128)S(1)}, /*index=5*/f32[128,256]{1,0:T(8,128)S(1)}) custom-call(s32[2]{0:T(128)S(1)} %pad_add_fusion.2.where_ref, f32[125,1,256]{2,1,0:T(1,128)} %bitcast.335, f32[125,1,256]{2,1,0:T(1,128)} %bitcast.338, ...), custom_call_target="tpu_custom_call" | custom-call | tf_op jit(solution)/shard_map/pallas_call | solution.py:967
  3.5 7.5 %all-to-all-start.2 = ((f32[16,8,128]{2,1,0:T(8,128)}), f32[16,8,128]{2,1,0:T(8,128)S(1)}, u32[]{:S(2)}, u32[]{:S(2)}) async-start(f32[16,8,128]{2,1,0:T(8,128)} %get-tuple-element.480), calls=%async_computation.2 | async-start | bytes 131072 | tf_op jit(solution)/shard_map/all_to_all | solution.py:976
  11.0 0.4 collective-permute-start.5
  11.4 1.7 %collective-permute-start.6 = (f32[16,512]{1,0:T(8,128)S(1)}, f32[16,512]{1,0:T(8,128)S(1)}, u32[]{:S(2)}, u32[]{:S(2)}) collective-permute-start(f32[16,512]{1,0:T(8,128)S(1)} %get-tuple-element.477.m1_ref), channel_id=1, source_target_pairs={{0,2},{1,3},{2,0},{3,1},{4,6},{5,7},{6,4},{7,5},{8,10},{9,11},{10,... | collective-permute-start | bytes 98312 | tf_op jit(solution)/shard_map/ppermute | solution.py:18
  13.0 1.5 %collective-permute-start.7 = (f32[16,512]{1,0:T(8,128)S(1)}, f32[16,512]{1,0:T(8,128)S(1)}, u32[]{:S(2)}, u32[]{:S(2)}) collective-permute-start(f32[16,512]{1,0:T(8,128)S(1)} %get-tuple-element.478.m2_ref), channel_id=1, source_target_pairs={{0,4},{1,5},{2,6},{3,7},{4,0},{5,1},{6,2},{7,3},{8,12},{9,13},{10,... | collective-permute-start | bytes 98312 | tf_op jit(solution)/shard_map/ppermute | solution.py:18
  14.5 2.4 %collective-permute-start.8 = (f32[16,512]{1,0:T(8,128)S(1)}, f32[16,512]{1,0:T(8,128)S(1)}, u32[]{:S(2)}, u32[]{:S(2)}) collective-permute-start(f32[16,512]{1,0:T(8,128)S(1)} %get-tuple-element.479.m3_ref), channel_id=1, source_target_pairs={{0,8},{1,9},{2,10},{3,11},{4,12},{5,13},{6,14},{7,15},{8,0},{9,1},... | collective-permute-start | bytes 98312 | tf_op jit(solution)/shard_map/ppermute | solution.py:18
  16.9 0.0 collective-permute-done.5.g0_ref
  16.9 0.0 collective-permute-done.6.g1_ref
  16.9 0.2 collective-permute-done.7.g2_ref
  17.0 2.6 %collective-permute-done.8.g3_ref = f32[16,512]{1,0:T(8,128)S(1)} collective-permute-done((f32[16,512]{1,0:T(8,128)S(1)}, f32[16,512]{1,0:T(8,128)S(1)}, u32[]{:S(2)}, u32[]{:S(2)}) %collective-permute-start.8) | collective-permute-done | bytes 32800 | tf_op jit(solution)/shard_map/ppermute | solution.py:18
  19.7 0.0 all-to-all-done.2.every_ref
  19.7 0.0 copy-done.3
  19.7 0.0 copy-done.4
  19.7 9.8 %shard_map.130 = (f32[16,17,128]{2,1,0:T(8,128)S(1)}, f32[4,128,128]{2,1,0:T(8,128)S(1)}, f32[16,128]{1,0:T(8,128)S(1)}) custom-call(s32[2]{0:T(128)S(1)} %pad_add_fusion.2.where_ref, f32[1,12]{1,0:T(1,128)S(1)} %copy-done.9, f32[125,1,256]{2,1,0:T(1,128)S(1)} %bitcast.336, f32[125,1,256]{2,1,0:T(1,128)S(1)} %bitcast.339, f32[125,1,256]{2,1,0:T(1,128)S(1)} %bitcast.342, ...), custom_call_target="tpu_custom_call" | custom-call | tf_op jit(solution)/shard_map/pallas_call | solution.py:981
  29.5 12.3 %all_to_all.33 = f32[16,17,128]{2,1,0:T(8,128)S(1)} all-to-all(f32[16,17,128]{2,1,0:T(8,128)S(1)} %get-tuple-element.481), channel_id=1, replica_groups={{0,2,4,6,8,10,12,14,16,18,20,22,24,26,28,30},{1,3,5,7,9,11,13,15,17,19,..., dimensions={0} | all-to-all | bytes 278528 | tf_op jit(solution)/shard_map/all_to_all | solution.py:1004
  41.8 0.0 collective-permute-start.9
  41.8 1.4 %collective-permute-done.9 = f32[16,17,128]{2,1,0:T(8,128)S(1)} collective-permute-done((f32[16,17,128]{2,1,0:T(8,128)S(1)}, f32[16,17,128]{2,1,0:T(8,128)S(1)}, u32[]{:S(2)}, u32[]{:S(2)}) %collective-permute-start.9) | collective-permute-done | bytes 139296 | tf_op jit(solution)/shard_map/ppermute | solution.py:18
  43.3 0.7 %fusion.32 = f32[]{:T(128)} fusion(f32[16,17,128]{2,1,0:T(8,128)S(1)} %collective-permute-done.9, f32[16,17,128]{2,1,0:T(8,128)S(1)} %all_to_all.33), kind=kLoop, calls=%fused_computation.102 | loop fusion | flops 31 | bytes 132 | tf_op jit(solution)/shard_map/reduce_max | solution.py:1008
  44.6 12.9 %conditional.1 = (f32[1,125,256]{2,0,1:T(1,128)}, f32[1,125,256]{2,0,1:T(1,128)}) conditional(s32[]{:T(128)} %convert_element_type.23, (s32[2]{0:T(128)S(1)}, f32[1,12]{1,0:T(1,128)S(1)}, f32[16,17,128]{2,1,0:T(8,128)S(1)}, f32[16,17,128]{2,1,0:T(8,128)S(1)}, f32[125,1,256]{2,1,0:T(1,128)S(1)}, /*index=5*/f32[125,1,256]{2,1,0:T(1,128)S(1)}, ...), branch_computations={%region_1.0_spmd, %region_2.15_spmd} | conditional | flops 347599744 | bytes 9835607 | solution.py:1048
  44.6 12.8 %branch_0_fun.1 = (f32[125,1,256]{2,1,0:T(1,128)}, f32[125,1,256]{2,1,0:T(1,128)}) custom-call(s32[2]{0:T(128)S(1)} %get-tuple-element.413.where_ref, f32[1,12]{1,0:T(1,128)S(1)} %get-tuple-element.414.time_ref, f32[16,17,128]{2,1,0:T(8,128)S(1)} %get-tuple-element.415.mine_ref, f32[16,17,128]{2,1,0:T(8,128)S(1)} %get-tuple-element.416.other_ref, ...), custom_call_target="tpu_custom_call" | custom-call | tf_op jit(solution)/shard_map/cond/branch_0_fun/pallas_call | solution.py:1014
  (9 shorter events, 0.0 us)
Async XLA Ops:
  0.6 0.7 %copy-start.7 = (s32[5,512]{1,0:T(8,128)S(1)}, s32[5,512]{1,0:T(8,128)}, u32[]{:S(2)}) copy-start(s32[5,512]{1,0:T(8,128)} %couple_ref.1) | copy-start | bytes 30724
  0.7 0.7 %copy-start.8 = (s32[1,3,128]{2,0,1:T(1,128)S(1)}, s32[1,3,128]{2,0,1:T(1,128)}, u32[]{:S(2)}) copy-start(s32[1,3,128]{2,0,1:T(1,128)} %param.19) | copy-start | bytes 4612
  1.4 18.3 %copy-start.3 = (f32[1,125,256]{2,0,1:T(1,128)S(1)}, f32[1,125,256]{2,0,1:T(1,128)}, u32[]{:S(2)}) copy-start(f32[1,125,256]{2,0,1:T(1,128)} %param.16) | copy-start | bytes 384004
  1.4 18.3 %copy-start.4 = (f32[1,125,256]{2,0,1:T(1,128)S(1)}, f32[1,125,256]{2,0,1:T(1,128)}, u32[]{:S(2)}) copy-start(f32[1,125,256]{2,0,1:T(1,128)} %param.17) | copy-start | bytes 384004
  1.4 18.3 %copy-start.6 = (f32[125,1]{1,0:T(8,128)S(1)}, f32[125,1]{1,0:T(8,128)}, u32[]{:S(2)}) copy-start(f32[125,1]{1,0:T(8,128)} %constant.131.clone.weight_ref) | copy-start | bytes 1504
  3.5 16.2 %copy-start.2 = (f32[1,125,256]{2,0,1:T(1,128)S(1)}, f32[1,125,256]{2,0,1:T(1,128)}, u32[]{:S(2)}) copy-start(f32[1,125,256]{2,0,1:T(1,128)} %param.15) | copy-start | bytes 384004
  3.5 16.2 %all-to-all-start.2 = ((f32[16,8,128]{2,1,0:T(8,128)}), f32[16,8,128]{2,1,0:T(8,128)S(1)}, u32[]{:S(2)}, u32[]{:S(2)}) async-start(f32[16,8,128]{2,1,0:T(8,128)} %get-tuple-element.480), calls=%async_computation.2 | async-start | bytes 131072 | tf_op jit(solution)/shard_map/all_to_all | solution.py:976
  11.0 5.9 %collective-permute-start.5 = (f32[16,512]{1,0:T(8,128)S(1)}, f32[16,512]{1,0:T(8,128)S(1)}, u32[]{:S(2)}, u32[]{:S(2)}) collective-permute-start(f32[16,512]{1,0:T(8,128)S(1)} %get-tuple-element.476.m0_ref), channel_id=1, source_target_pairs={{0,1},{1,0},{2,3},{3,2},{4,5},{5,4},{6,7},{7,6},{8,9},{9,8},{10,11... | collective-permute-start | bytes 98312 | tf_op jit(solution)/shard_map/ppermute | solution.py:18
  11.4 5.5 %collective-permute-start.6 = (f32[16,512]{1,0:T(8,128)S(1)}, f32[16,512]{1,0:T(8,128)S(1)}, u32[]{:S(2)}, u32[]{:S(2)}) collective-permute-start(f32[16,512]{1,0:T(8,128)S(1)} %get-tuple-element.477.m1_ref), channel_id=1, source_target_pairs={{0,2},{1,3},{2,0},{3,1},{4,6},{5,7},{6,4},{7,5},{8,10},{9,11},{10,... | collective-permute-start | bytes 98312 | tf_op jit(solution)/shard_map/ppermute | solution.py:18
  13.0 4.0 %collective-permute-start.7 = (f32[16,512]{1,0:T(8,128)S(1)}, f32[16,512]{1,0:T(8,128)S(1)}, u32[]{:S(2)}, u32[]{:S(2)}) collective-permute-start(f32[16,512]{1,0:T(8,128)S(1)} %get-tuple-element.478.m2_ref), channel_id=1, source_target_pairs={{0,4},{1,5},{2,6},{3,7},{4,0},{5,1},{6,2},{7,3},{8,12},{9,13},{10,... | collective-permute-start | bytes 98312 | tf_op jit(solution)/shard_map/ppermute | solution.py:18
  14.5 5.2 %copy-start.9 = (f32[1,12]{1,0:T(1,128)S(1)}, f32[1,12]{1,0:T(1,128)}, u32[]{:S(2)}) copy-start(f32[1,12]{1,0:T(1,128)} %coef_ref.1) | copy-start | bytes 148
  14.5 5.2 %collective-permute-start.8 = (f32[16,512]{1,0:T(8,128)S(1)}, f32[16,512]{1,0:T(8,128)S(1)}, u32[]{:S(2)}, u32[]{:S(2)}) collective-permute-start(f32[16,512]{1,0:T(8,128)S(1)} %get-tuple-element.479.m3_ref), channel_id=1, source_target_pairs={{0,8},{1,9},{2,10},{3,11},{4,12},{5,13},{6,14},{7,15},{8,0},{9,1},... | collective-permute-start | bytes 98312 | tf_op jit(solution)/shard_map/ppermute | solution.py:18
  41.8 1.4 %collective-permute-start.9 = (f32[16,17,128]{2,1,0:T(8,128)S(1)}, f32[16,17,128]{2,1,0:T(8,128)S(1)}, u32[]{:S(2)}, u32[]{:S(2)}) collective-permute-start(f32[16,17,128]{2,1,0:T(8,128)S(1)} %all_to_all.33), channel_id=1, source_target_pairs={{0,1},{1,0},{2,3},{3,2},{4,5},{5,4},{6,7},{7,6},{8,9},{9,8},{10,11... | collective-permute-start | bytes 417800 | tf_op jit(solution)/shard_map/ppermute | solution.py:18

commit v5 on v4

--- a/solution.py
+++ b/solution.py
@@ -333,10 +333,16 @@
     return extra
 
 
-def load_tiles(flat_ref, out_ref, factor=None, group=0, groups=1, start=0):
+def load_tiles(flat_ref, out_ref, group=0, groups=1, start=0):
     for bc in range(25):
-        value = flat_ref[pl.ds(start + bc, 8, stride=25), :]
-        set_tile(out_ref, value if factor is None else factor * value, bc, group, groups)
+        set_tile(out_ref, flat_ref[pl.ds(start + bc, 8, stride=25), :], bc, group, groups)
+
+
+def fold_tiles(inverse_ref, force_ref, keep_ref, count):
+    for k in range(count):
+        inverse = tile_of(inverse_ref, k)
+        set_tile(force_ref, inverse * tile_of(force_ref, k), k)
+        set_tile(keep_ref, 2.0 - inverse * (PENALTY * tile_of(keep_ref, k)), k)
 
 
 def across(row_values):
@@ -544,7 +550,7 @@
     scale_ref,
     inverse_ref,
     force_ref,
-    damp_ref,
+    keep_ref,
     state_ref,
     z_ref,
     hc_ref,
@@ -658,11 +664,12 @@
         count_ref[...][:NODES],
     ]
     flat_ref[...] = jnp.zeros(flat_ref.shape, jnp.float32)
-    for k, out in enumerate((scale_ref, inverse_ref, force_ref, damp_ref)):
+    for k, out in enumerate((scale_ref, inverse_ref, force_ref, keep_ref)):
         flat_ref[0:NODES] = (
             exact_pick(own_fields[k], take) + exact_pick(pair[k], partner_matrix)[:NODES]
         )
-        load_tiles(flat_ref, out, PENALTY if k == 3 else None)
+        load_tiles(flat_ref, out)
+    fold_tiles(inverse_ref, force_ref, keep_ref, 25)
 
     home = []
     for g in range(2):
@@ -699,7 +706,6 @@
         set_tile(hc_ref, zero, bc)
         set_tile(hz_ref, zero, bc)
         set_tile(state_ref, zero, bc, 0, 2)
-        set_tile(y_ref, zero, bc, 0, 2)
     for n in range(STEPS):
         seen_ref[n] = zero
     for bc in range(25, 40):
@@ -707,7 +713,7 @@
         set_tile(y_ref, zero, bc, 0, 2)
         set_tile(y_ref, zero, bc, 1, 2)
 
-    is_box = jnp.where(where_ref[0] == 0, 1.0, 0.0)
+    is_box = where_ref[0] == 0
 
     def note_free(moment, drive):
         extra = partner_faces(y_ref, face_ref, side, 0, 2)
@@ -717,20 +723,17 @@
             assembled = tile_of(y_ref, bc, 0, 2) + extra[bc]
             x = tile_of(state_ref, bc, 0, 2)
             h = tile_of(hc_ref, bc)
-            seen = seen + jnp.where(code == bc, is_box * assembled + (1.0 - is_box) * (x - h), 0.0)
+            seen = seen + jnp.where(code == bc, jnp.where(is_box, assembled, x - h), 0.0)
             if drive is not None:
-                inverse = tile_of(inverse_ref, bc)
-                dx = tile_of(damp_ref, bc) * x
-                advanced = 2.0 * x - h + inverse * (drive * tile_of(force_ref, bc) - assembled - dx)
-                set_tile(state_ref, advanced, bc, 0, 2)
-                set_tile(hc_ref, x - inverse * dx, bc)
+                kept = tile_of(keep_ref, bc) * x
+                pushed = drive * tile_of(force_ref, bc)
+                set_tile(
+                    state_ref, kept - h + pushed - tile_of(inverse_ref, bc) * assembled, bc, 0, 2
+                )
+                set_tile(hc_ref, kept - x, bc)
         seen_ref[moment, 7:8] = jnp.sum(seen, axis=0, keepdims=True)
 
-    def step(moment, _):
-        keep = jnp.where(moment > 0, 1.0, 0.0)
-        stiff = jnp.where(moment > 0, -1.0, is_box)
-        begin = jnp.where(moment > 0, 0.0, 1.0 - is_box)
-        note_free(moment, coef_ref[0, moment])
+    def step(moment, begin):
         extra = partner_faces(z_ref, face_ref, side)
         for bc in range(25):
             set_tile(state_ref, tile_of(z_ref, bc) + extra[bc], bc, 1, 2)
@@ -738,22 +741,31 @@
         codes = [code_ref[q] for q in range(OTHERS + 1)]
         seen = [zero] * (OTHERS + 1)
         for bc in range(25):
-            inverse = tile_of(inverse_ref, bc)
             x = tile_of(z_ref, bc)
-            h = tile_of(hz_ref, bc)
-            dx = tile_of(damp_ref, bc) * x
-            adjoint = (2.0 * keep) * x - h + inverse * (
-                stiff * tile_of(y_ref, bc, 1, 2) - keep * dx + begin * x
-            )
+            pushed = tile_of(inverse_ref, bc) * tile_of(y_ref, bc, 1, 2)
+            if begin:
+                at_once = tile_of(inverse_ref, bc) * x
+                adjoint = jnp.where(is_box, pushed, at_once)
+                set_tile(hz_ref, jnp.where(is_box, 0.0, at_once), bc)
+            else:
+                kept = tile_of(keep_ref, bc) * x
+                adjoint = kept - tile_of(hz_ref, bc) - pushed
+                set_tile(hz_ref, kept - x, bc)
             set_tile(z_ref, adjoint, bc)
-            set_tile(hz_ref, keep * (x - inverse * dx) + begin * (inverse * x), bc)
             for q in range(OTHERS + 1):
                 seen[q] = seen[q] + jnp.where(codes[q] == bc, adjoint, 0.0)
         for q in range(OTHERS + 1):
             seen_ref[moment, q : q + 1] = jnp.sum(seen[q], axis=0, keepdims=True)
+
+    def free_and_adjoint(moment, _):
+        note_free(moment, coef_ref[0, moment])
+        step(moment, False)
         return 0
 
-    lax.fori_loop(0, STEPS - 1, step, 0)
+    for bc in range(25):
+        set_tile(state_ref, coef_ref[0, 0] * tile_of(force_ref, bc), bc, 0, 2)
+    step(0, True)
+    lax.fori_loop(1, STEPS - 1, free_and_adjoint, 0)
     note_free(STEPS - 1, None)
     seen = []
     extras = []
@@ -763,14 +775,14 @@
         seen.append(rows)
         extras.append(jnp.where(used, gather_packed(rows, entry_at)[0:1], 0.0))
     for k in range(FREE_ROWS):
-        out_ref[0, k : k + 1] = jnp.where(lane_low, seen[2 * k][7:8], seen[2 * k + 1][7:8])
+        out_ref[0, :, k * LANES : (k + 1) * LANES] = jnp.where(lane_low, seen[2 * k][7:8], seen[2 * k + 1][7:8])
     for k in range(PAIRS):
         r = GAIN_ROW + k
-        out_ref[0, r : r + 1] = jnp.where(lane_low, seen[2 * k][0:1], seen[2 * k + 1][0:1])
+        out_ref[0, :, r * LANES : (r + 1) * LANES] = jnp.where(lane_low, seen[2 * k][0:1], seen[2 * k + 1][0:1])
         r = EXTRA_ROW + k
-        out_ref[0, r : r + 1] = jnp.where(lane_low, extras[2 * k], extras[2 * k + 1])
+        out_ref[0, :, r * LANES : (r + 1) * LANES] = jnp.where(lane_low, extras[2 * k], extras[2 * k + 1])
     starts = jnp.where(lane == HALF, jnp.where(too_long, 1.0, 0.0), pltpu.roll(start, HALF, 1))
-    out_ref[0, INDEX_ROW : INDEX_ROW + 1] = jnp.where(lane_low, entry_gid, starts)
+    out_ref[0, :, INDEX_ROW * LANES : PAYLOAD * LANES] = jnp.where(lane_low, entry_gid, starts)
     for k in range(1, out_ref.shape[0]):
         out_ref[k] = out_ref[0]
 
@@ -795,7 +807,7 @@
     scale_ref,
     inverse_ref,
     force_ref,
-    damp_ref,
+    keep_ref,
     x_ref,
     old_ref,
     h_ref,
@@ -803,15 +815,18 @@
     grad_ref,
     face_ref,
     kick_ref,
+    node_ref,
 ):
     is_box = where_ref[0] == 0
     parity = where_ref[1] % 2
-    both_ref[parity] = mine_ref[...]
-    both_ref[1 - parity] = other_ref[...]
+    for core, source in ((parity, mine_ref), (1 - parity, other_ref)):
+        for s in range(2):
+            for r in range(PAYLOAD):
+                both_ref[core, s, r] = source[8 * s : 8 * s + 8, 0, r * LANES : (r + 1) * LANES]
     low = lax.broadcasted_iota(jnp.int32, (8, LANES), 1) < HALF
 
     def rows(section, core, r):
-        return both_ref[core, section * 8 : section * 8 + 8, r, :]
+        return both_ref[core, section, r]
 
     row = lax.broadcasted_iota(jnp.int32, (8, LANES), 0)
     point = lax.broadcasted_iota(jnp.int32, (8, LANES), 1) % HALF
@@ -877,55 +892,53 @@
         count_ref[...][:NODES],
     ]
     kick_ref[...] = jnp.zeros(kick_ref.shape, jnp.float32)
-    for k, out in enumerate((scale_ref, inverse_ref, force_ref, damp_ref)):
+    for k, out in enumerate((scale_ref, inverse_ref, force_ref, keep_ref)):
         kick_ref[0:NODES] = pair_ref[k][:NODES]
         kick_ref[200 : 200 + NODES] = own_fields[k][:, :LANES]
         kick_ref[400 : 400 + NODES] = own_fields[k][:, LANES:]
         for g in range(3):
-            load_tiles(kick_ref, out, PENALTY if k == 3 else None, g, 3, 200 * g)
+            load_tiles(kick_ref, out, g, 3, 200 * g)
+    fold_tiles(inverse_ref, force_ref, keep_ref, 75)
     for g in range(3):
         for bc in range(25, 40):
             set_tile(y_ref, zero, bc, g, 3)
         for bc in range(25):
-            first = time_ref[0, 0] * tile_of(force_ref, bc, g, 3)
-            set_tile(x_ref, tile_of(inverse_ref, bc, g, 3) * first, bc, g, 3)
+            set_tile(x_ref, time_ref[0, 0] * tile_of(force_ref, bc, g, 3), bc, g, 3)
             set_tile(h_ref, zero, bc, g, 3)
+    node_row = lax.broadcasted_iota(jnp.int32, (LANES, LANES), 0)
     point_node = note[3:6].astype(jnp.int32)
-    node_row = lax.broadcasted_iota(jnp.int32, (LANES, LANES), 0)
+    for c in range(3):
+        node_ref[:, c * LANES : (c + 1) * LANES] = one_hot(node_row == point_node[c : c + 1])
 
     def step(moment, _):
         drive = time_ref[0, moment]
         stiffness_tiles(x_ref, scale_ref, y_ref, grad_ref, 3, False)
         inputs = input_ref[moment]
-        chosen = [
-            jnp.where(node_row == point_node[c : c + 1], inputs[c : c + 1], 0.0) for c in range(3)
-        ]
-        high = [part.astype(jnp.bfloat16) for part in chosen]
-        rest = [
-            (part - top.astype(jnp.float32)).astype(jnp.bfloat16) for part, top in zip(chosen, high)
+        high = inputs.astype(jnp.bfloat16)
+        rest = (inputs - high.astype(jnp.float32)).astype(jnp.bfloat16)
+        parts = [
+            node_ref[:, c * LANES : (c + 1) * LANES] * part[c : c + 1]
+            for part in (high, rest)
+            for c in range(3)
         ]
         kick = jnp.dot(
-            jnp.concatenate(high + rest, axis=1), spread_ref[...], preferred_element_type=jnp.float32
+            jnp.concatenate(parts, axis=1), spread_ref[...], preferred_element_type=jnp.float32
         )
         for g in range(3):
             kick_ref[200 * g : 200 * g + LANES] = kick[:, g * LANES : (g + 1) * LANES]
         extra = partner_faces(y_ref, face_ref, side, 0, 3)
         for g in range(3):
             for bc in range(25):
-                assembled = tile_of(y_ref, bc, g, 3)
+                net = kick_ref[pl.ds(200 * g + bc, 8, stride=25), :] - tile_of(y_ref, bc, g, 3)
                 if g == 0:
-                    assembled = assembled + extra[bc]
-                inverse = tile_of(inverse_ref, bc, g, 3)
+                    net = net - extra[bc]
                 x = tile_of(x_ref, bc, g, 3)
-                h = tile_of(h_ref, bc, g, 3)
-                arrived = kick_ref[pl.ds(200 * g + bc, 8, stride=25), :]
-                dx = tile_of(damp_ref, bc, g, 3) * x
-                advanced = 2.0 * x - h + inverse * (
-                    drive * tile_of(force_ref, bc, g, 3) - assembled - dx + arrived
-                )
-                set_tile(h_ref, x - inverse * dx, bc, g, 3)
+                kept = tile_of(keep_ref, bc, g, 3) * x
+                pushed = drive * tile_of(force_ref, bc, g, 3)
+                advanced = kept - tile_of(h_ref, bc, g, 3) + pushed
+                set_tile(x_ref, advanced + tile_of(inverse_ref, bc, g, 3) * net, bc, g, 3)
+                set_tile(h_ref, kept - x, bc, g, 3)
                 set_tile(old_ref, x, bc, g, 3)
-                set_tile(x_ref, advanced, bc, g, 3)
         return 0
 
     lax.fori_loop(1, STEPS, step, 0)
@@ -980,7 +993,7 @@
 
     payload, pair, note = pl.pallas_call(
         response_kernel,
-        out_shape=[shape(blocks, PAYLOAD, LANES), shape(4, LANES, LANES), shape(16, LANES)],
+        out_shape=[shape(blocks, 1, PAYLOAD * LANES), shape(4, LANES, LANES), shape(16, LANES)],
         in_specs=[smem] * 2 + [vmem] * 14,
         out_specs=[vmem] * 3,
         compiler_params=params,
@@ -1005,8 +1018,9 @@
         payload, ("sec", "blk"), 0, 0, axis_index_groups=same_core, tiled=True
     )
     sibling = partner_2(received, "blk", 0)
+    flag = INDEX_ROW * LANES + HALF
     overflow = jnp.max(
-        jnp.maximum(received[:, INDEX_ROW, HALF], sibling[:, INDEX_ROW, HALF])
+        jnp.maximum(received[:, 0, flag], sibling[:, 0, flag])
     ) > 0
 
     def quick(_):
@@ -1018,12 +1032,13 @@
                 out_specs=[vmem] * 2,
                 compiler_params=params,
                 scratch_shapes=[
-                    pltpu.VMEM((2, blocks, PAYLOAD, LANES), jnp.float32),
+                    pltpu.VMEM((2, 2, PAYLOAD, 8, LANES), jnp.float32),
                     pltpu.VMEM((6 * LANES, 3 * LANES), jnp.bfloat16),
                     pltpu.VMEM((STEPS, 8, LANES), jnp.float32),
                 ]
                 + [tiles(75)] * 7
-                + [tiles(120), tiles(75), tiles(5), tiles(75)],
+                + [tiles(120), tiles(75), tiles(5), tiles(75)]
+                + [pltpu.VMEM((LANES, 3 * LANES), jnp.bfloat16)],
             )(
                 place,
                 source_time,

time: 57.8 us -> 56.5 us (0.978)
  Pallas kernels: 24.7 us -> 23.7 us
    pallas_call x1, Pallas kernels: 9.79 us -> 9.07 us  [fast_body(): pl.pallas_call(response_kernel, out_shape=[shape(blocks, 1, PAYLOAD * LAN...]
where the time goes in v5:
time: 56.5 us; the launch traced here: 56.1 us
  Pallas kernels  23.7 us (42%)
  starting transfers between devices  13.4 us (24%)
  blocking collectives  12.1 us (21%)
  waiting for transfers between devices  4.15 us (7%)
  between operations  1.35 us (2%)
  other arithmetic  0.78 us (1%)
  local copies, waits for them, and re-layouts  0.7 us (1%)
    pallas_call x1, Pallas kernels, quick(): pl.pallas_call(final_kernel, out_shape=[shape(NODES, 1, columns)] * 2, in...  12.6 us
    all_to_all x1, blocking collectives, fast_body(): lax.all_to_all(payload, ('sec', 'blk'), 0, 0, axis_index_groups=same_core...  12.1 us
    pallas_call x1, Pallas kernels, fast_body(): pl.pallas_call(response_kernel, out_shape=[shape(blocks, 1, PAYLOAD * LAN...  9.07 us
    all_to_all x1, starting transfers between devices, fast_body(): every = lax.all_to_all(links, 'blk', 0, 0, tiled=True)  7.49 us
    ppermute x5, starting transfers between devices, partner_2(): lax.ppermute(value, axis, [(i, i ^ 1 << stride) for i in range(lax.axis_s...  5.92 us
    ppermute x5, waiting for transfers between devices, partner_2(): lax.ppermute(value, axis, [(i, i ^ 1 << stride) for i in range(lax.axis_s...  4.15 us
    pallas_call x1, Pallas kernels, fast_body(): pl.pallas_call(pack_kernel, out_shape=[shape(blocks, 8, LANES)] + [shape(...  2.05 us
  transfers between devices with their start and end apart: 6, of which 3 were waited for; matrix products, arithmetic and copies ran while one was open for 0% of the time, Pallas kernels for 0%

profile of v5, /device:TPU:0, one launch (start us, length us, event | category | flops | bytes accessed | tf_op | source)
XLA Modules:
  0.0 56.1 jit_solution(10047649613958503637)
XLA Ops:
  0.6 0.1 pad_add_fusion.2.where_ref
  0.7 0.6 %copy-done.7 = s32[5,512]{1,0:T(8,128)S(1)} copy-done((s32[5,512]{1,0:T(8,128)S(1)}, s32[5,512]{1,0:T(8,128)}, u32[]{:S(2)}) %copy-start.7) | copy-done | bytes 10264
  1.3 0.1 copy-done.8
  1.4 2.0 %shard_map.129 = (f32[16,8,128]{2,1,0:T(8,128)}, f32[16,512]{1,0:T(8,128)S(1)}, f32[16,512]{1,0:T(8,128)S(1)}, f32[16,512]{1,0:T(8,128)S(1)}, f32[16,512]{1,0:T(8,128)S(1)}, /*index=5*/f32[128,256]{1,0:T(8,128)S(1)}) custom-call(s32[2]{0:T(128)S(1)} %pad_add_fusion.2.where_ref, f32[125,1,256]{2,1,0:T(1,128)} %bitcast.335, f32[125,1,256]{2,1,0:T(1,128)} %bitcast.338, ...), custom_call_target="tpu_custom_call" | custom-call | tf_op jit(solution)/shard_map/pallas_call | solution.py:980
  3.5 7.5 %all-to-all-start.2 = ((f32[16,8,128]{2,1,0:T(8,128)}), f32[16,8,128]{2,1,0:T(8,128)S(1)}, u32[]{:S(2)}, u32[]{:S(2)}) async-start(f32[16,8,128]{2,1,0:T(8,128)} %get-tuple-element.480), calls=%async_computation.2 | async-start | bytes 131072 | tf_op jit(solution)/shard_map/all_to_all | solution.py:989
  11.0 0.4 collective-permute-start.5
  11.4 1.7 %collective-permute-start.6 = (f32[16,512]{1,0:T(8,128)S(1)}, f32[16,512]{1,0:T(8,128)S(1)}, u32[]{:S(2)}, u32[]{:S(2)}) collective-permute-start(f32[16,512]{1,0:T(8,128)S(1)} %get-tuple-element.477.m1_ref), channel_id=1, source_target_pairs={{0,2},{1,3},{2,0},{3,1},{4,6},{5,7},{6,4},{7,5},{8,10},{9,11},{10,... | collective-permute-start | bytes 98312 | tf_op jit(solution)/shard_map/ppermute | solution.py:18
  13.0 1.5 %collective-permute-start.7 = (f32[16,512]{1,0:T(8,128)S(1)}, f32[16,512]{1,0:T(8,128)S(1)}, u32[]{:S(2)}, u32[]{:S(2)}) collective-permute-start(f32[16,512]{1,0:T(8,128)S(1)} %get-tuple-element.478.m2_ref), channel_id=1, source_target_pairs={{0,4},{1,5},{2,6},{3,7},{4,0},{5,1},{6,2},{7,3},{8,12},{9,13},{10,... | collective-permute-start | bytes 98312 | tf_op jit(solution)/shard_map/ppermute | solution.py:18
  14.5 2.4 %collective-permute-start.8 = (f32[16,512]{1,0:T(8,128)S(1)}, f32[16,512]{1,0:T(8,128)S(1)}, u32[]{:S(2)}, u32[]{:S(2)}) collective-permute-start(f32[16,512]{1,0:T(8,128)S(1)} %get-tuple-element.479.m3_ref), channel_id=1, source_target_pairs={{0,8},{1,9},{2,10},{3,11},{4,12},{5,13},{6,14},{7,15},{8,0},{9,1},... | collective-permute-start | bytes 98312 | tf_op jit(solution)/shard_map/ppermute | solution.py:18
  16.9 0.0 collective-permute-done.5.g0_ref
  16.9 0.0 collective-permute-done.6.g1_ref
  16.9 0.2 collective-permute-done.7.g2_ref
  17.0 2.6 %collective-permute-done.8.g3_ref = f32[16,512]{1,0:T(8,128)S(1)} collective-permute-done((f32[16,512]{1,0:T(8,128)S(1)}, f32[16,512]{1,0:T(8,128)S(1)}, u32[]{:S(2)}, u32[]{:S(2)}) %collective-permute-start.8) | collective-permute-done | bytes 32800 | tf_op jit(solution)/shard_map/ppermute | solution.py:18
  19.7 0.0 all-to-all-done.2.every_ref
  19.7 0.0 copy-done.6
  19.7 0.0 copy-done.2
  19.7 0.0 copy-done.9
  19.7 9.1 %shard_map.130 = (f32[16,1,2176]{2,1,0:T(1,128)S(1)}, f32[4,128,128]{2,1,0:T(8,128)S(1)}, f32[16,128]{1,0:T(8,128)S(1)}) custom-call(s32[2]{0:T(128)S(1)} %pad_add_fusion.2.where_ref, f32[1,12]{1,0:T(1,128)S(1)} %copy-done.9, f32[125,1,256]{2,1,0:T(1,128)S(1)} %bitcast.336, f32[125,1,256]{2,1,0:T(1,128)S(1)} %bitcast.339, f32[125,1,256]{2,1,0:T(1,128)S(1)} %bitcast.342, ...), custom_call_target="tpu_custom_call" | custom-call | tf_op jit(solution)/shard_map/pallas_call | solution.py:994
  28.8 12.1 %all_to_all.33 = f32[16,1,2176]{2,1,0:T(1,128)S(1)} all-to-all(f32[16,1,2176]{2,1,0:T(1,128)S(1)} %get-tuple-element.481), channel_id=1, replica_groups={{0,2,4,6,8,10,12,14,16,18,20,22,24,26,28,30},{1,3,5,7,9,11,13,15,17,19,..., dimensions={0} | all-to-all | bytes 278528 | tf_op jit(solution)/shard_map/all_to_all | solution.py:1017
  40.9 0.0 collective-permute-start.9
  40.9 1.4 %collective-permute-done.9 = f32[16,1,2176]{2,1,0:T(1,128)S(1)} collective-permute-done((f32[16,1,2176]{2,1,0:T(1,128)S(1)}, f32[16,1,2176]{2,1,0:T(1,128)S(1)}, u32[]{:S(2)}, u32[]{:S(2)}) %collective-permute-start.9) | collective-permute-done | bytes 139296 | tf_op jit(solution)/shard_map/ppermute | solution.py:18
  42.2 0.7 %fusion.32 = f32[]{:T(128)} fusion(f32[16,1,2176]{2,1,0:T(1,128)S(1)} %collective-permute-done.9, f32[16,1,2176]{2,1,0:T(1,128)S(1)} %all_to_all.33), kind=kLoop, calls=%fused_computation.102 | loop fusion | flops 31 | bytes 132 | tf_op jit(solution)/shard_map/reduce_max | solution.py:1022
  43.6 12.6 %conditional.1 = (f32[1,125,256]{2,0,1:T(1,128)}, f32[1,125,256]{2,0,1:T(1,128)}) conditional(s32[]{:T(128)} %convert_element_type.23, (s32[2]{0:T(128)S(1)}, f32[1,12]{1,0:T(1,128)S(1)}, f32[16,1,2176]{2,1,0:T(1,128)S(1)}, f32[16,1,2176]{2,1,0:T(1,128)S(1)}, f32[125,1,256]{2,1,0:T(1,128)S(1)}, /*index=5*/f32[125,1,256]{2,1,0:T(1,128)S(1)}, ...), branch_computations={%region_1.0_spmd, %region_2.15_spmd} | conditional | flops 347599744 | bytes 9835607 | solution.py:1063
  43.6 12.6 %branch_0_fun.1 = (f32[125,1,256]{2,1,0:T(1,128)}, f32[125,1,256]{2,1,0:T(1,128)}) custom-call(s32[2]{0:T(128)S(1)} %get-tuple-element.413.where_ref, f32[1,12]{1,0:T(1,128)S(1)} %get-tuple-element.414.time_ref, f32[16,1,2176]{2,1,0:T(1,128)S(1)} %get-tuple-element.415.mine_ref, f32[16,1,2176]{2,1,0:T(1,128)S(1)} %get-tuple-element.416.other_ref, ...), custom_call_target="tpu_custom_call" | custom-call | tf_op jit(solution)/shard_map/cond/branch_0_fun/pallas_call | solution.py:1028
  (9 shorter events, 0.0 us)
Async XLA Ops:
  0.6 0.7 %copy-start.7 = (s32[5,512]{1,0:T(8,128)S(1)}, s32[5,512]{1,0:T(8,128)}, u32[]{:S(2)}) copy-start(s32[5,512]{1,0:T(8,128)} %couple_ref.1) | copy-start | bytes 30724
  0.7 0.7 %copy-start.8 = (s32[1,3,128]{2,0,1:T(1,128)S(1)}, s32[1,3,128]{2,0,1:T(1,128)}, u32[]{:S(2)}) copy-start(s32[1,3,128]{2,0,1:T(1,128)} %param.19) | copy-start | bytes 4612
  1.4 18.3 %copy-start.3 = (f32[1,125,256]{2,0,1:T(1,128)S(1)}, f32[1,125,256]{2,0,1:T(1,128)}, u32[]{:S(2)}) copy-start(f32[1,125,256]{2,0,1:T(1,128)} %param.16) | copy-start | bytes 384004
  1.4 18.3 %copy-start.4 = (f32[1,125,256]{2,0,1:T(1,128)S(1)}, f32[1,125,256]{2,0,1:T(1,128)}, u32[]{:S(2)}) copy-start(f32[1,125,256]{2,0,1:T(1,128)} %param.17) | copy-start | bytes 384004
  1.4 18.3 %copy-start.6 = (f32[125,1]{1,0:T(8,128)S(1)}, f32[125,1]{1,0:T(8,128)}, u32[]{:S(2)}) copy-start(f32[125,1]{1,0:T(8,128)} %constant.131.clone.weight_ref) | copy-start | bytes 1504
  3.5 16.2 %copy-start.2 = (f32[1,125,256]{2,0,1:T(1,128)S(1)}, f32[1,125,256]{2,0,1:T(1,128)}, u32[]{:S(2)}) copy-start(f32[1,125,256]{2,0,1:T(1,128)} %param.15) | copy-start | bytes 384004
  3.5 16.2 %all-to-all-start.2 = ((f32[16,8,128]{2,1,0:T(8,128)}), f32[16,8,128]{2,1,0:T(8,128)S(1)}, u32[]{:S(2)}, u32[]{:S(2)}) async-start(f32[16,8,128]{2,1,0:T(8,128)} %get-tuple-element.480), calls=%async_computation.2 | async-start | bytes 131072 | tf_op jit(solution)/shard_map/all_to_all | solution.py:989
  11.0 5.9 %collective-permute-start.5 = (f32[16,512]{1,0:T(8,128)S(1)}, f32[16,512]{1,0:T(8,128)S(1)}, u32[]{:S(2)}, u32[]{:S(2)}) collective-permute-start(f32[16,512]{1,0:T(8,128)S(1)} %get-tuple-element.476.m0_ref), channel_id=1, source_target_pairs={{0,1},{1,0},{2,3},{3,2},{4,5},{5,4},{6,7},{7,6},{8,9},{9,8},{10,11... | collective-permute-start | bytes 98312 | tf_op jit(solution)/shard_map/ppermute | solution.py:18
  11.4 5.5 %collective-permute-start.6 = (f32[16,512]{1,0:T(8,128)S(1)}, f32[16,512]{1,0:T(8,128)S(1)}, u32[]{:S(2)}, u32[]{:S(2)}) collective-permute-start(f32[16,512]{1,0:T(8,128)S(1)} %get-tuple-element.477.m1_ref), channel_id=1, source_target_pairs={{0,2},{1,3},{2,0},{3,1},{4,6},{5,7},{6,4},{7,5},{8,10},{9,11},{10,... | collective-permute-start | bytes 98312 | tf_op jit(solution)/shard_map/ppermute | solution.py:18
  13.0 4.0 %collective-permute-start.7 = (f32[16,512]{1,0:T(8,128)S(1)}, f32[16,512]{1,0:T(8,128)S(1)}, u32[]{:S(2)}, u32[]{:S(2)}) collective-permute-start(f32[16,512]{1,0:T(8,128)S(1)} %get-tuple-element.478.m2_ref), channel_id=1, source_target_pairs={{0,4},{1,5},{2,6},{3,7},{4,0},{5,1},{6,2},{7,3},{8,12},{9,13},{10,... | collective-permute-start | bytes 98312 | tf_op jit(solution)/shard_map/ppermute | solution.py:18
  14.5 5.2 %copy-start.9 = (f32[1,12]{1,0:T(1,128)S(1)}, f32[1,12]{1,0:T(1,128)}, u32[]{:S(2)}) copy-start(f32[1,12]{1,0:T(1,128)} %coef_ref.1) | copy-start | bytes 148
  14.5 5.2 %collective-permute-start.8 = (f32[16,512]{1,0:T(8,128)S(1)}, f32[16,512]{1,0:T(8,128)S(1)}, u32[]{:S(2)}, u32[]{:S(2)}) collective-permute-start(f32[16,512]{1,0:T(8,128)S(1)} %get-tuple-element.479.m3_ref), channel_id=1, source_target_pairs={{0,8},{1,9},{2,10},{3,11},{4,12},{5,13},{6,14},{7,15},{8,0},{9,1},... | collective-permute-start | bytes 98312 | tf_op jit(solution)/shard_map/ppermute | solution.py:18
  40.9 1.4 %collective-permute-start.9 = (f32[16,1,2176]{2,1,0:T(1,128)S(1)}, f32[16,1,2176]{2,1,0:T(1,128)S(1)}, u32[]{:S(2)}, u32[]{:S(2)}) collective-permute-start(f32[16,1,2176]{2,1,0:T(1,128)S(1)} %all_to_all.33), channel_id=1, source_target_pairs={{0,1},{1,0},{2,3},{3,2},{4,5},{5,4},{6,7},{7,6},{8,9},{9,8},{10,11... | collective-permute-start | bytes 417800 | tf_op jit(solution)/shard_map/ppermute | solution.py:18

commit v6 on v5

--- a/solution.py
+++ b/solution.py
@@ -264,7 +264,7 @@
     return jnp.broadcast_to(ref[row : row + 1, :], (8, LANES))
 
 
-def stiffness_tiles(x_ref, scale_ref, y_ref, grad_ref, groups, shared):
+def stiffness_tiles(x_ref, scale_of, y_ref, grad_ref, groups):
     forward = line_matrix()
     backward = forward.T.copy()
     to_grad, to_node = line_tiles()
@@ -272,7 +272,7 @@
     for g in range(groups):
 
         def scale(bc):
-            return tile_of(scale_ref, bc) if shared else tile_of(scale_ref, bc, g, groups)
+            return scale_of(bc, g)
 
         def along(index):
             grads = apply_line(forward, [tile_of(x_ref, k, g, groups) for k in index])
@@ -526,14 +526,56 @@
     return out
 
 
-def response_kernel(
+def point_kernel(
     where_ref,
-    coef_ref,
     wave_ref,
     mass_ref,
     source_ref,
     weight_ref,
     count_ref,
+    every_ref,
+    table_ref,
+    copy_ref,
+    scale_ref,
+    inverse_ref,
+    force_ref,
+    keep_ref,
+    flat_ref,
+):
+    chunks, keys = point_tables(where_ref, every_ref)
+    rows = [chunks[c][f] for c in range(3) for f in range(3)] + keys
+    table_ref[...] = jnp.concatenate(rows + [jnp.zeros((4, LANES), jnp.float32)], axis=0)
+    down = lax.broadcasted_iota(jnp.int32, (LANES, LANES), 0)
+    right = lax.broadcasted_iota(jnp.int32, (LANES, LANES), 1)
+    element = chunks[0][0]
+    element_both = jnp.where(lane_row() < HALF, element, pltpu.roll(element, HALF, 1))
+    take = [
+        one_hot((down.astype(jnp.float32) + float(g * LANES + 1) == element_both) & (right < HALF))
+        for g in range(2)
+    ]
+    take = jnp.concatenate(take, axis=0)
+    own_fields = [
+        weight_ref[...] * wave_ref[:, 0, :],
+        DT_SQUARED * mass_ref[:, 0, :],
+        source_ref[:, 0, :],
+        count_ref[...][:NODES],
+    ]
+    flat_ref[...] = jnp.zeros(flat_ref.shape, jnp.float32)
+    copy_ref[...] = jnp.zeros(copy_ref.shape, jnp.float32)
+    for k, out in enumerate((scale_ref, inverse_ref, force_ref, keep_ref)):
+        pick = plain_dot if k == 3 else exact_pick
+        copy_ref[k, 0:NODES] = pick(own_fields[k], take)
+        for g in range(2):
+            flat_ref[200 * g : 200 * g + NODES] = own_fields[k][:, g * LANES : (g + 1) * LANES]
+            load_tiles(flat_ref, out, g, 2, 200 * g)
+    fold_tiles(inverse_ref, force_ref, keep_ref, 50)
+
+
+def response_kernel(
+    where_ref,
+    coef_ref,
+    table_ref,
+    copy_ref,
     m0_ref,
     m1_ref,
     m2_ref,
@@ -542,7 +584,6 @@
     g1_ref,
     g2_ref,
     g3_ref,
-    every_ref,
     out_ref,
     pair_ref,
     note_ref,
@@ -579,7 +620,8 @@
     own_column = jnp.broadcast_to(stacked[:HALF, 125:126], (HALF, LANES))
     own_column = jnp.concatenate([own_column, own_column], axis=0)
 
-    chunks, keys = point_tables(where_ref, every_ref)
+    chunks = [[table_ref[3 * c + f : 3 * c + f + 1] for f in range(3)] for c in range(3)]
+    keys = [table_ref[9 + c : 10 + c] for c in range(3)]
     element, node, _ = chunks[0]
     element_both = jnp.where(lane_low, element, pltpu.roll(element, HALF, 1))
     node_low = jnp.where(lane_low, node, 0.0)
@@ -652,22 +694,10 @@
     entry_at = jnp.broadcast_to(entry_at, (8, LANES))
     entry_gid = jnp.where(used, gather_packed(jnp.concatenate(gids, axis=0), entry_at)[0:1], 0.0)
 
-    take = [
-        one_hot((down.astype(jnp.float32) + float(g * LANES + 1) == element_both) & (right < HALF))
-        for g in range(2)
-    ]
-    take = jnp.concatenate(take, axis=0)
-    own_fields = [
-        weight_ref[...] * wave_ref[:, 0, :],
-        DT_SQUARED * mass_ref[:, 0, :],
-        source_ref[:, 0, :],
-        count_ref[...][:NODES],
-    ]
     flat_ref[...] = jnp.zeros(flat_ref.shape, jnp.float32)
     for k, out in enumerate((scale_ref, inverse_ref, force_ref, keep_ref)):
-        flat_ref[0:NODES] = (
-            exact_pick(own_fields[k], take) + exact_pick(pair[k], partner_matrix)[:NODES]
-        )
+        pick = plain_dot if k == 3 else exact_pick
+        flat_ref[0:NODES] = (copy_ref[k] + pick(pair[k], partner_matrix))[:NODES]
         load_tiles(flat_ref, out)
     fold_tiles(inverse_ref, force_ref, keep_ref, 25)
 
@@ -737,7 +767,7 @@
         extra = partner_faces(z_ref, face_ref, side)
         for bc in range(25):
             set_tile(state_ref, tile_of(z_ref, bc) + extra[bc], bc, 1, 2)
-        stiffness_tiles(state_ref, scale_ref, y_ref, grad_ref, 2, True)
+        stiffness_tiles(state_ref, lambda bc, g: tile_of(scale_ref, bc), y_ref, grad_ref, 2)
         codes = [code_ref[q] for q in range(OTHERS + 1)]
         seen = [zero] * (OTHERS + 1)
         for bc in range(25):
@@ -792,11 +822,10 @@
     time_ref,
     mine_ref,
     other_ref,
-    wave_ref,
-    mass_ref,
-    source_ref,
-    weight_ref,
-    count_ref,
+    own_scale_ref,
+    own_inverse_ref,
+    own_force_ref,
+    own_keep_ref,
     pair_ref,
     note_ref,
     now_ref,
@@ -885,25 +914,24 @@
             spread_ref[c * LANES : (c + 1) * LANES, g * LANES : (g + 1) * LANES] = matrix
             spread_ref[(c + 3) * LANES : (c + 4) * LANES, g * LANES : (g + 1) * LANES] = matrix
     side = jnp.broadcast_to(note[12:13].astype(jnp.int32), (8, LANES))
-    own_fields = [
-        weight_ref[...] * wave_ref[:, 0, :],
-        DT_SQUARED * mass_ref[:, 0, :],
-        source_ref[:, 0, :],
-        count_ref[...][:NODES],
-    ]
     kick_ref[...] = jnp.zeros(kick_ref.shape, jnp.float32)
     for k, out in enumerate((scale_ref, inverse_ref, force_ref, keep_ref)):
         kick_ref[0:NODES] = pair_ref[k][:NODES]
-        kick_ref[200 : 200 + NODES] = own_fields[k][:, :LANES]
-        kick_ref[400 : 400 + NODES] = own_fields[k][:, LANES:]
-        for g in range(3):
-            load_tiles(kick_ref, out, g, 3, 200 * g)
-    fold_tiles(inverse_ref, force_ref, keep_ref, 75)
+        load_tiles(kick_ref, out)
+    fold_tiles(inverse_ref, force_ref, keep_ref, 25)
+
+    def choose(linked_ref, own_ref):
+        return lambda bc, g: tile_of(linked_ref, bc) if g == 0 else tile_of(own_ref, bc, g - 1, 2)
+
+    scale_of = choose(scale_ref, own_scale_ref)
+    inverse_of = choose(inverse_ref, own_inverse_ref)
+    force_of = choose(force_ref, own_force_ref)
+    keep_of = choose(keep_ref, own_keep_ref)
     for g in range(3):
         for bc in range(25, 40):
             set_tile(y_ref, zero, bc, g, 3)
         for bc in range(25):
-            set_tile(x_ref, time_ref[0, 0] * tile_of(force_ref, bc, g, 3), bc, g, 3)
+            set_tile(x_ref, time_ref[0, 0] * force_of(bc, g), bc, g, 3)
             set_tile(h_ref, zero, bc, g, 3)
     node_row = lax.broadcasted_iota(jnp.int32, (LANES, LANES), 0)
     point_node = note[3:6].astype(jnp.int32)
@@ -912,7 +940,7 @@
 
     def step(moment, _):
         drive = time_ref[0, moment]
-        stiffness_tiles(x_ref, scale_ref, y_ref, grad_ref, 3, False)
+        stiffness_tiles(x_ref, scale_of, y_ref, grad_ref, 3)
         inputs = input_ref[moment]
         high = inputs.astype(jnp.bfloat16)
         rest = (inputs - high.astype(jnp.float32)).astype(jnp.bfloat16)
@@ -933,10 +961,10 @@
                 if g == 0:
                     net = net - extra[bc]
                 x = tile_of(x_ref, bc, g, 3)
-                kept = tile_of(keep_ref, bc, g, 3) * x
-                pushed = drive * tile_of(force_ref, bc, g, 3)
+                kept = keep_of(bc, g) * x
+                pushed = drive * force_of(bc, g)
                 advanced = kept - tile_of(h_ref, bc, g, 3) + pushed
-                set_tile(x_ref, advanced + tile_of(inverse_ref, bc, g, 3) * net, bc, g, 3)
+                set_tile(x_ref, advanced + inverse_of(bc, g) * net, bc, g, 3)
                 set_tile(h_ref, kept - x, bc, g, 3)
                 set_tile(old_ref, x, bc, g, 3)
         return 0
@@ -991,10 +1019,18 @@
     def tiles(count):
         return pltpu.VMEM((8 * count, LANES), jnp.float32)
 
+    table, copies, *own_tiles = pl.pallas_call(
+        point_kernel,
+        out_shape=[shape(16, LANES), shape(4, LANES, LANES)] + [shape(400, LANES)] * 4,
+        in_specs=[smem] + [vmem] * 6,
+        out_specs=[vmem] * 6,
+        scratch_shapes=[tiles(50)],
+        compiler_params=params,
+    )(place, wave, mass, source, weight, count, every)
     payload, pair, note = pl.pallas_call(
         response_kernel,
         out_shape=[shape(blocks, 1, PAYLOAD * LANES), shape(4, LANES, LANES), shape(16, LANES)],
-        in_specs=[smem] * 2 + [vmem] * 14,
+        in_specs=[smem] * 2 + [vmem] * 10,
         out_specs=[vmem] * 3,
         compiler_params=params,
         scratch_shapes=[tiles(25)] * 5
@@ -1003,14 +1039,10 @@
     )(
         place,
         source_time,
-        wave,
-        mass,
-        source,
-        weight,
-        count,
+        table,
+        copies,
         *mine,
         *ghost,
-        every,
     )
 
     same_core = [[c + 2 * i for i in range(blocks)] for c in range(2)]
@@ -1028,7 +1060,7 @@
             pl.pallas_call(
                 final_kernel,
                 out_shape=[shape(NODES, 1, columns)] * 2,
-                in_specs=[smem] * 2 + [vmem] * 9,
+                in_specs=[smem] * 2 + [vmem] * 8,
                 out_specs=[vmem] * 2,
                 compiler_params=params,
                 scratch_shapes=[
@@ -1036,7 +1068,8 @@
                     pltpu.VMEM((6 * LANES, 3 * LANES), jnp.bfloat16),
                     pltpu.VMEM((STEPS, 8, LANES), jnp.float32),
                 ]
-                + [tiles(75)] * 7
+                + [tiles(25)] * 4
+                + [tiles(75)] * 3
                 + [tiles(120), tiles(75), tiles(5), tiles(75)]
                 + [pltpu.VMEM((LANES, 3 * LANES), jnp.bfloat16)],
             )(
@@ -1044,11 +1077,7 @@
                 source_time,
                 received,
                 sibling,
-                wave,
-                mass,
-                source,
-                weight,
-                count,
+                *own_tiles,
                 pair,
                 note,
             )

time: 56.5 us -> 55.5 us (0.982)
  waiting for transfers between devices: 4.15 us -> 2.68 us
  blocking collectives: 12.1 us -> 10.9 us
  Pallas kernels: 23.7 us -> 24.6 us
  local copies, waits for them, and re-layouts: 0.7 us -> 1.35 us
    ppermute x5, waiting for transfers between devices: 4.15 us -> 1.37 us  [partner_2(): lax.ppermute(value, axis, [(i, i ^ 1 << stride) for i in range(lax.axis_s...]
    pallas_call x0 -> x1, Pallas kernels: none -> 2.54 us  [fast_body(): pl.pallas_call(point_kernel, out_shape=[shape(16, LANES), shape(4, LANES,...]
    pallas_call x1, Pallas kernels: 9.07 us -> 7.39 us  [fast_body(): pl.pallas_call(response_kernel, out_shape=[shape(blocks, 1, PAYLOAD * LAN...]
    all_to_all x1, waiting for transfers between devices: 0.01 us -> 1.32 us  [fast_body(): every = lax.all_to_all(links, 'blk', 0, 0, tiled=True)]
    all_to_all x1, blocking collectives: 12.1 us -> 10.9 us  [fast_body(): lax.all_to_all(payload, ('sec', 'blk'), 0, 0, axis_index_groups=same_core...]
    unnamed x14, local copies, waits for them, and re-layouts: 0.7 us -> 1.35 us
  transfers between devices with their start and end apart: 6 -> 6, of which waited for: 3 -> 2; matrix products, arithmetic and copies ran while one was open for 0% -> 0% of each run, Pallas kernels for 0% -> 5%
where the time goes in v6:
time: 55.5 us; the launch traced here: 55.1 us
  Pallas kernels  24.6 us (44%)
  starting transfers between devices  13.4 us (24%)
  blocking collectives  10.9 us (20%)
  waiting for transfers between devices  2.68 us (5%)
  between operations  1.37 us (2%)
  local copies, waits for them, and re-layouts  1.35 us (2%)
  other arithmetic  0.78 us (1%)
    pallas_call x1, Pallas kernels, quick(): pl.pallas_call(final_kernel, out_shape=[shape(NODES, 1, columns)] * 2, in...  12.6 us
    all_to_all x1, blocking collectives, fast_body(): lax.all_to_all(payload, ('sec', 'blk'), 0, 0, axis_index_groups=same_core...  10.9 us
    all_to_all x1, starting transfers between devices, fast_body(): every = lax.all_to_all(links, 'blk', 0, 0, tiled=True)  7.49 us
    pallas_call x1, Pallas kernels, fast_body(): pl.pallas_call(response_kernel, out_shape=[shape(blocks, 1, PAYLOAD * LAN...  7.39 us
    ppermute x5, starting transfers between devices, partner_2(): lax.ppermute(value, axis, [(i, i ^ 1 << stride) for i in range(lax.axis_s...  5.92 us
    pallas_call x1, Pallas kernels, fast_body(): pl.pallas_call(point_kernel, out_shape=[shape(16, LANES), shape(4, LANES,...  2.54 us
    pallas_call x1, Pallas kernels, fast_body(): pl.pallas_call(pack_kernel, out_shape=[shape(blocks, 8, LANES)] + [shape(...  2.05 us
    ppermute x5, waiting for transfers between devices, partner_2(): lax.ppermute(value, axis, [(i, i ^ 1 << stride) for i in range(lax.axis_s...  1.37 us
  transfers between devices with their start and end apart: 6, of which 2 were waited for; matrix products, arithmetic and copies ran while one was open for 0% of the time, Pallas kernels for 5%

profile of v6, /device:TPU:0, one launch (start us, length us, event | category | flops | bytes accessed | tf_op | source)
XLA Modules:
  0.0 55.1 jit_solution(2214605969660125287)
XLA Ops:
  0.6 0.1 pad_add_fusion.2.where_ref
  0.7 0.6 %copy-done.7 = s32[5,512]{1,0:T(8,128)S(1)} copy-done((s32[5,512]{1,0:T(8,128)S(1)}, s32[5,512]{1,0:T(8,128)}, u32[]{:S(2)}) %copy-start.7) | copy-done | bytes 10264
  1.3 0.1 copy-done.8
  1.4 2.0 %shard_map.129 = (f32[16,8,128]{2,1,0:T(8,128)}, f32[16,512]{1,0:T(8,128)S(1)}, f32[16,512]{1,0:T(8,128)S(1)}, f32[16,512]{1,0:T(8,128)S(1)}, f32[16,512]{1,0:T(8,128)S(1)}, /*index=5*/f32[128,256]{1,0:T(8,128)S(1)}) custom-call(s32[2]{0:T(128)S(1)} %pad_add_fusion.2.where_ref, f32[125,1,256]{2,1,0:T(1,128)} %bitcast.335, f32[125,1,256]{2,1,0:T(1,128)} %bitcast.337, ...), custom_call_target="tpu_custom_call" | custom-call | tf_op jit(solution)/shard_map/pallas_call | solution.py:1008
  3.5 7.5 %all-to-all-start.2 = ((f32[16,8,128]{2,1,0:T(8,128)}), f32[16,8,128]{2,1,0:T(8,128)S(1)}, u32[]{:S(2)}, u32[]{:S(2)}) async-start(f32[16,8,128]{2,1,0:T(8,128)} %get-tuple-element.479), calls=%async_computation.2 | async-start | bytes 131072 | tf_op jit(solution)/shard_map/all_to_all | solution.py:1017
  11.0 0.4 collective-permute-start.5
  11.4 1.7 %collective-permute-start.6 = (f32[16,512]{1,0:T(8,128)S(1)}, f32[16,512]{1,0:T(8,128)S(1)}, u32[]{:S(2)}, u32[]{:S(2)}) collective-permute-start(f32[16,512]{1,0:T(8,128)S(1)} %get-tuple-element.483.m1_ref), channel_id=1, source_target_pairs={{0,2},{1,3},{2,0},{3,1},{4,6},{5,7},{6,4},{7,5},{8,10},{9,11},{10,... | collective-permute-start | bytes 98312 | tf_op jit(solution)/shard_map/ppermute | solution.py:18
  13.0 1.5 %collective-permute-start.7 = (f32[16,512]{1,0:T(8,128)S(1)}, f32[16,512]{1,0:T(8,128)S(1)}, u32[]{:S(2)}, u32[]{:S(2)}) collective-permute-start(f32[16,512]{1,0:T(8,128)S(1)} %get-tuple-element.484.m2_ref), channel_id=1, source_target_pairs={{0,4},{1,5},{2,6},{3,7},{4,0},{5,1},{6,2},{7,3},{8,12},{9,13},{10,... | collective-permute-start | bytes 98312 | tf_op jit(solution)/shard_map/ppermute | solution.py:18
  14.5 2.4 %collective-permute-start.8 = (f32[16,512]{1,0:T(8,128)S(1)}, f32[16,512]{1,0:T(8,128)S(1)}, u32[]{:S(2)}, u32[]{:S(2)}) collective-permute-start(f32[16,512]{1,0:T(8,128)S(1)} %get-tuple-element.485.m3_ref), channel_id=1, source_target_pairs={{0,8},{1,9},{2,10},{3,11},{4,12},{5,13},{6,14},{7,15},{8,0},{9,1},... | collective-permute-start | bytes 98312 | tf_op jit(solution)/shard_map/ppermute | solution.py:18
  16.9 1.3 %all-to-all-done.2.every_ref = f32[16,8,128]{2,1,0:T(8,128)S(1)} async-done(((f32[16,8,128]{2,1,0:T(8,128)}), f32[16,8,128]{2,1,0:T(8,128)S(1)}, u32[]{:S(2)}, u32[]{:S(2)}) %all-to-all-start.2) | async-done | bytes 65568 | tf_op jit(solution)/shard_map/all_to_all | solution.py:1017
  18.2 2.5 %shard_map.130 = (f32[16,128]{1,0:T(8,128)S(1)}, f32[4,128,128]{2,1,0:T(8,128)S(1)}, f32[400,128]{1,0:T(8,128)S(1)}, f32[400,128]{1,0:T(8,128)S(1)}, f32[400,128]{1,0:T(8,128)S(1)}, /*index=5*/f32[400,128]{1,0:T(8,128)S(1)}) custom-call(s32[2]{0:T(128)S(1)} %pad_add_fusion.2.where_ref, f32[125,1,256]{2,1,0:T(1,128)S(1)} %bitcast.336, ...), custom_call_target="tpu_custom_call" | custom-call | tf_op jit(solution)/shard_map/pallas_call | solution.py:1022
  20.8 0.0 collective-permute-done.5.g0_ref
  20.8 0.0 collective-permute-done.6.g1_ref
  20.8 0.0 collective-permute-done.7.g2_ref
  20.8 0.0 collective-permute-done.8.g3_ref
  20.8 0.0 copy-start.9
  20.8 0.6 %copy-done.9 = f32[1,12]{1,0:T(1,128)S(1)} copy-done((f32[1,12]{1,0:T(1,128)S(1)}, f32[1,12]{1,0:T(1,128)}, u32[]{:S(2)}) %copy-start.9) | copy-done | bytes 72
  21.5 7.4 %shard_map.131 = (f32[16,1,2176]{2,1,0:T(1,128)S(1)}, f32[4,128,128]{2,1,0:T(8,128)S(1)}, f32[16,128]{1,0:T(8,128)S(1)}) custom-call(s32[2]{0:T(128)S(1)} %pad_add_fusion.2.where_ref, f32[1,12]{1,0:T(1,128)S(1)} %copy-done.9, f32[16,128]{1,0:T(8,128)S(1)} %get-tuple-element.480.table_ref, f32[4,128,128]{2,1,0:T(8,128)S(1)} %get-tuple-element.481.copy_ref, ...), custom_call_target="tpu_custom_call" | custom-call | tf_op jit(solution)/shard_map/pallas_call | solution.py:1030
  28.9 10.9 %all_to_all.33 = f32[16,1,2176]{2,1,0:T(1,128)S(1)} all-to-all(f32[16,1,2176]{2,1,0:T(1,128)S(1)} %get-tuple-element.486), channel_id=1, replica_groups={{0,2,4,6,8,10,12,14,16,18,20,22,24,26,28,30},{1,3,5,7,9,11,13,15,17,19,..., dimensions={0} | all-to-all | bytes 278528 | tf_op jit(solution)/shard_map/all_to_all | solution.py:1049
  39.8 0.0 collective-permute-start.9
  39.8 1.4 %collective-permute-done.9 = f32[16,1,2176]{2,1,0:T(1,128)S(1)} collective-permute-done((f32[16,1,2176]{2,1,0:T(1,128)S(1)}, f32[16,1,2176]{2,1,0:T(1,128)S(1)}, u32[]{:S(2)}, u32[]{:S(2)}) %collective-permute-start.9) | collective-permute-done | bytes 139296 | tf_op jit(solution)/shard_map/ppermute | solution.py:18
  41.1 0.7 %fusion.32 = f32[]{:T(128)} fusion(f32[16,1,2176]{2,1,0:T(1,128)S(1)} %collective-permute-done.9, f32[16,1,2176]{2,1,0:T(1,128)S(1)} %all_to_all.33), kind=kLoop, calls=%fused_computation.102 | loop fusion | flops 31 | bytes 132 | tf_op jit(solution)/shard_map/reduce_max | solution.py:1054
  42.5 12.6 %conditional.1 = (f32[1,125,256]{2,0,1:T(1,128)}, f32[1,125,256]{2,0,1:T(1,128)}) conditional(s32[]{:T(128)} %convert_element_type.23, (s32[2]{0:T(128)S(1)}, f32[1,12]{1,0:T(1,128)S(1)}, f32[16,1,2176]{2,1,0:T(1,128)S(1)}, f32[16,1,2176]{2,1,0:T(1,128)S(1)}, f32[400,128]{1,0:T(8,128)S(1)}, /*index=5*/f32[400,128]{1,0:T(8,128)S(1)}, ...), branch_computations={%region_1.0_spmd, %region_2.15_spmd} | conditional | flops 347599744 | bytes 9835607 | solution.py:1092
  42.5 12.6 %branch_0_fun.1 = (f32[125,1,256]{2,1,0:T(1,128)}, f32[125,1,256]{2,1,0:T(1,128)}) custom-call(s32[2]{0:T(128)S(1)} %get-tuple-element.411.where_ref, f32[1,12]{1,0:T(1,128)S(1)} %get-tuple-element.412.time_ref, f32[16,1,2176]{2,1,0:T(1,128)S(1)} %get-tuple-element.413.mine_ref, f32[16,1,2176]{2,1,0:T(1,128)S(1)} %get-tuple-element.414.other_ref, ...), custom_call_target="tpu_custom_call" | custom-call | tf_op jit(solution)/shard_map/cond/branch_0_fun/pallas_call | solution.py:1060
  (10 shorter events, 0.0 us)
Async XLA Ops:
  0.6 0.7 %copy-start.7 = (s32[5,512]{1,0:T(8,128)S(1)}, s32[5,512]{1,0:T(8,128)}, u32[]{:S(2)}) copy-start(s32[5,512]{1,0:T(8,128)} %couple_ref.1) | copy-start | bytes 30724
  0.7 0.7 %copy-start.8 = (s32[1,3,128]{2,0,1:T(1,128)S(1)}, s32[1,3,128]{2,0,1:T(1,128)}, u32[]{:S(2)}) copy-start(s32[1,3,128]{2,0,1:T(1,128)} %param.19) | copy-start | bytes 4612
  1.4 16.8 %copy-start.4 = (f32[1,125,256]{2,0,1:T(1,128)S(1)}, f32[1,125,256]{2,0,1:T(1,128)}, u32[]{:S(2)}) copy-start(f32[1,125,256]{2,0,1:T(1,128)} %param.16) | copy-start | bytes 384004
  1.4 16.8 %copy-start.5 = (f32[1,125,256]{2,0,1:T(1,128)S(1)}, f32[1,125,256]{2,0,1:T(1,128)}, u32[]{:S(2)}) copy-start(f32[1,125,256]{2,0,1:T(1,128)} %param.17) | copy-start | bytes 384004
  1.4 16.8 %copy-start.6 = (f32[125,1]{1,0:T(8,128)S(1)}, f32[125,1]{1,0:T(8,128)}, u32[]{:S(2)}) copy-start(f32[125,1]{1,0:T(8,128)} %constant.131.clone.weight_ref) | copy-start | bytes 1504
  3.5 14.8 %copy-start.3 = (f32[1,125,256]{2,0,1:T(1,128)S(1)}, f32[1,125,256]{2,0,1:T(1,128)}, u32[]{:S(2)}) copy-start(f32[1,125,256]{2,0,1:T(1,128)} %param.15) | copy-start | bytes 384004
  3.5 14.7 %all-to-all-start.2 = ((f32[16,8,128]{2,1,0:T(8,128)}), f32[16,8,128]{2,1,0:T(8,128)S(1)}, u32[]{:S(2)}, u32[]{:S(2)}) async-start(f32[16,8,128]{2,1,0:T(8,128)} %get-tuple-element.479), calls=%async_computation.2 | async-start | bytes 131072 | tf_op jit(solution)/shard_map/all_to_all | solution.py:1017
  11.0 9.8 %collective-permute-start.5 = (f32[16,512]{1,0:T(8,128)S(1)}, f32[16,512]{1,0:T(8,128)S(1)}, u32[]{:S(2)}, u32[]{:S(2)}) collective-permute-start(f32[16,512]{1,0:T(8,128)S(1)} %get-tuple-element.482.m0_ref), channel_id=1, source_target_pairs={{0,1},{1,0},{2,3},{3,2},{4,5},{5,4},{6,7},{7,6},{8,9},{9,8},{10,11... | collective-permute-start | bytes 98312 | tf_op jit(solution)/shard_map/ppermute | solution.py:18
  11.4 9.4 %collective-permute-start.6 = (f32[16,512]{1,0:T(8,128)S(1)}, f32[16,512]{1,0:T(8,128)S(1)}, u32[]{:S(2)}, u32[]{:S(2)}) collective-permute-start(f32[16,512]{1,0:T(8,128)S(1)} %get-tuple-element.483.m1_ref), channel_id=1, source_target_pairs={{0,2},{1,3},{2,0},{3,1},{4,6},{5,7},{6,4},{7,5},{8,10},{9,11},{10,... | collective-permute-start | bytes 98312 | tf_op jit(solution)/shard_map/ppermute | solution.py:18
  13.0 7.7 %collective-permute-start.7 = (f32[16,512]{1,0:T(8,128)S(1)}, f32[16,512]{1,0:T(8,128)S(1)}, u32[]{:S(2)}, u32[]{:S(2)}) collective-permute-start(f32[16,512]{1,0:T(8,128)S(1)} %get-tuple-element.484.m2_ref), channel_id=1, source_target_pairs={{0,4},{1,5},{2,6},{3,7},{4,0},{5,1},{6,2},{7,3},{8,12},{9,13},{10,... | collective-permute-start | bytes 98312 | tf_op jit(solution)/shard_map/ppermute | solution.py:18
  14.5 6.3 %collective-permute-start.8 = (f32[16,512]{1,0:T(8,128)S(1)}, f32[16,512]{1,0:T(8,128)S(1)}, u32[]{:S(2)}, u32[]{:S(2)}) collective-permute-start(f32[16,512]{1,0:T(8,128)S(1)} %get-tuple-element.485.m3_ref), channel_id=1, source_target_pairs={{0,8},{1,9},{2,10},{3,11},{4,12},{5,13},{6,14},{7,15},{8,0},{9,1},... | collective-permute-start | bytes 98312 | tf_op jit(solution)/shard_map/ppermute | solution.py:18
  20.8 0.7 %copy-start.9 = (f32[1,12]{1,0:T(1,128)S(1)}, f32[1,12]{1,0:T(1,128)}, u32[]{:S(2)}) copy-start(f32[1,12]{1,0:T(1,128)} %coef_ref.1) | copy-start | bytes 148
  39.8 1.4 %collective-permute-start.9 = (f32[16,1,2176]{2,1,0:T(1,128)S(1)}, f32[16,1,2176]{2,1,0:T(1,128)S(1)}, u32[]{:S(2)}, u32[]{:S(2)}) collective-permute-start(f32[16,1,2176]{2,1,0:T(1,128)S(1)} %all_to_all.33), channel_id=1, source_target_pairs={{0,1},{1,0},{2,3},{3,2},{4,5},{5,4},{6,7},{7,6},{8,9},{9,8},{10,11... | collective-permute-start | bytes 417800 | tf_op jit(solution)/shard_map/ppermute | solution.py:18

commit v7 on v6

--- a/solution.py
+++ b/solution.py
@@ -386,6 +386,7 @@
 
 def pack_kernel(
     where_ref,
+    amplitude_ref,
     wave_ref,
     mass_ref,
     source_ref,
@@ -398,7 +399,10 @@
     m2_ref,
     m3_ref,
     count_ref,
+    time_ref,
 ):
+    for k in range(STEPS):
+        time_ref[0, k] = amplitude_ref[0, k]
     me = where_ref[1]
     me_f = me.astype(jnp.float32)
     is_box = where_ref[0] == 0
@@ -1005,13 +1009,13 @@
     def shape(*dims):
         return jax.ShapeDtypeStruct(dims, jnp.float32)
 
-    links, m0, m1, m2, m3, count = pl.pallas_call(
+    links, m0, m1, m2, m3, count, amplitude = pl.pallas_call(
         pack_kernel,
-        out_shape=[shape(blocks, 8, LANES)] + [shape(16, 4 * LANES)] * 4 + [shape(LANES, columns)],
-        in_specs=[smem] + [vmem] * 6,
-        out_specs=[vmem] * 6,
+        out_shape=[shape(blocks, 8, LANES)] + [shape(16, 4 * LANES)] * 4 + [shape(LANES, columns), shape(1, STEPS)],
+        in_specs=[smem] * 2 + [vmem] * 6,
+        out_specs=[vmem] * 6 + [smem],
         compiler_params=params,
-    )(place, wave, mass, source, weight, faces, coupling_links)
+    )(place, source_time, wave, mass, source, weight, faces, coupling_links)
     mine = [m0, m1, m2, m3]
     ghost = [partner_2(part, "blk", j) for j, part in enumerate(mine)]
     every = lax.all_to_all(links, "blk", 0, 0, tiled=True)
@@ -1038,7 +1042,7 @@
         + [pltpu.VMEM((8, 8, LANES), jnp.int32), pltpu.VMEM((STEPS, 8, LANES), jnp.float32)],
     )(
         place,
-        source_time,
+        amplitude,
         table,
         copies,
         *mine,
@@ -1074,7 +1078,7 @@
                 + [pltpu.VMEM((LANES, 3 * LANES), jnp.bfloat16)],
             )(
                 place,
-                source_time,
+                amplitude,
                 received,
                 sibling,
                 *own_tiles,

time: 55.5 us -> 55.1 us (level)
  local copies, waits for them, and re-layouts: 1.35 us -> 0.7 us
    unnamed x14, local copies, waits for them, and re-layouts: 1.35 us -> 0.7 us
where the time goes in v7:
time: 55.1 us; the launch traced here: 54.8 us
  Pallas kernels  24.9 us (45%)
  starting transfers between devices  13.4 us (24%)
  blocking collectives  10.9 us (20%)
  waiting for transfers between devices  2.68 us (5%)
  between operations  1.38 us (3%)
  other arithmetic  0.78 us (1%)
  local copies, waits for them, and re-layouts  0.7 us (1%)
    pallas_call x1, Pallas kernels, quick(): pl.pallas_call(final_kernel, out_shape=[shape(NODES, 1, columns)] * 2, in...  12.6 us
    all_to_all x1, blocking collectives, fast_body(): lax.all_to_all(payload, ('sec', 'blk'), 0, 0, axis_index_groups=same_core...  10.9 us
    all_to_all x1, starting transfers between devices, fast_body(): every = lax.all_to_all(links, 'blk', 0, 0, tiled=True)  7.5 us
    pallas_call x1, Pallas kernels, fast_body(): pl.pallas_call(response_kernel, out_shape=[shape(blocks, 1, PAYLOAD * LAN...  7.4 us
    ppermute x5, starting transfers between devices, partner_2(): lax.ppermute(value, axis, [(i, i ^ 1 << stride) for i in range(lax.axis_s...  5.92 us
    pallas_call x1, Pallas kernels, fast_body(): pl.pallas_call(point_kernel, out_shape=[shape(16, LANES), shape(4, LANES,...  2.54 us
    pallas_call x1, Pallas kernels, fast_body(): pl.pallas_call(pack_kernel, out_shape=[shape(blocks, 8, LANES)] + [shape(...  2.3 us
    ppermute x5, waiting for transfers between devices, partner_2(): lax.ppermute(value, axis, [(i, i ^ 1 << stride) for i in range(lax.axis_s...  1.37 us
  transfers between devices with their start and end apart: 6, of which 2 were waited for; matrix products, arithmetic and copies ran while one was open for 0% of the time, Pallas kernels for 5%

profile of v7, /device:TPU:0, one launch (start us, length us, event | category | flops | bytes accessed | tf_op | source)
XLA Modules:
  0.0 54.8 jit_solution(3496979972461229398)
XLA Ops:
  0.6 0.0 copy-start.7
  0.6 0.1 pad_add_fusion.2.where_ref
  0.7 0.6 %copy-done.7 = s32[5,512]{1,0:T(8,128)S(1)} copy-done((s32[5,512]{1,0:T(8,128)S(1)}, s32[5,512]{1,0:T(8,128)}, u32[]{:S(2)}) %copy-start.7) | copy-done | bytes 10264
  1.3 0.1 copy-done.8
  1.4 2.3 %shard_map.129 = (f32[16,8,128]{2,1,0:T(8,128)}, f32[16,512]{1,0:T(8,128)S(1)}, f32[16,512]{1,0:T(8,128)S(1)}, f32[16,512]{1,0:T(8,128)S(1)}, f32[16,512]{1,0:T(...) custom-call(s32[2]{0:T(128)S(1)} %pad_add_fusion.2.where_ref, f32[1,12]{1,0:T(1,128)S(1)} %copy-done.9, ...), custom_call_target="tpu_custom_call" | custom-call | tf_op jit(solution)/shard_map/pallas_call | solution.py:1012
  3.7 0.0 copy-start.3
  3.7 7.5 %all-to-all-start.2 = ((f32[16,8,128]{2,1,0:T(8,128)}), f32[16,8,128]{2,1,0:T(8,128)S(1)}, u32[]{:S(2)}, u32[]{:S(2)}) async-start(f32[16,8,128]{2,1,0:T(8,128)} %get-tuple-element.481), calls=%async_computation.2 | async-start | bytes 131072 | tf_op jit(solution)/shard_map/all_to_all | solution.py:1021
  11.2 0.4 collective-permute-start.5
  11.7 1.7 %collective-permute-start.6 = (f32[16,512]{1,0:T(8,128)S(1)}, f32[16,512]{1,0:T(8,128)S(1)}, u32[]{:S(2)}, u32[]{:S(2)}) collective-permute-start(f32[16,512]{1,0:T(8,128)S(1)} %get-tuple-element.485.m1_ref), channel_id=1, source_target_pairs={{0,2},{1,3},{2,0},{3,1},{4,6},{5,7},{6,4},{7,5},{8,10},{9,11},{10,... | collective-permute-start | bytes 98312 | tf_op jit(solution)/shard_map/ppermute | solution.py:18
  13.3 1.5 %collective-permute-start.7 = (f32[16,512]{1,0:T(8,128)S(1)}, f32[16,512]{1,0:T(8,128)S(1)}, u32[]{:S(2)}, u32[]{:S(2)}) collective-permute-start(f32[16,512]{1,0:T(8,128)S(1)} %get-tuple-element.486.m2_ref), channel_id=1, source_target_pairs={{0,4},{1,5},{2,6},{3,7},{4,0},{5,1},{6,2},{7,3},{8,12},{9,13},{10,... | collective-permute-start | bytes 98312 | tf_op jit(solution)/shard_map/ppermute | solution.py:18
  14.8 2.4 %collective-permute-start.8 = (f32[16,512]{1,0:T(8,128)S(1)}, f32[16,512]{1,0:T(8,128)S(1)}, u32[]{:S(2)}, u32[]{:S(2)}) collective-permute-start(f32[16,512]{1,0:T(8,128)S(1)} %get-tuple-element.487.m3_ref), channel_id=1, source_target_pairs={{0,8},{1,9},{2,10},{3,11},{4,12},{5,13},{6,14},{7,15},{8,0},{9,1},... | collective-permute-start | bytes 98312 | tf_op jit(solution)/shard_map/ppermute | solution.py:18
  17.2 1.3 %all-to-all-done.2.every_ref = f32[16,8,128]{2,1,0:T(8,128)S(1)} async-done(((f32[16,8,128]{2,1,0:T(8,128)}), f32[16,8,128]{2,1,0:T(8,128)S(1)}, u32[]{:S(2)}, u32[]{:S(2)}) %all-to-all-start.2) | async-done | bytes 65568 | tf_op jit(solution)/shard_map/all_to_all | solution.py:1021
  18.5 2.5 %shard_map.130 = (f32[16,128]{1,0:T(8,128)S(1)}, f32[4,128,128]{2,1,0:T(8,128)S(1)}, f32[400,128]{1,0:T(8,128)S(1)}, f32[400,128]{1,0:T(8,128)S(1)}, f32[400,128]{1,0:T(8,128)S(1)}, /*index=5*/f32[400,128]{1,0:T(8,128)S(1)}) custom-call(s32[2]{0:T(128)S(1)} %pad_add_fusion.2.where_ref, f32[125,1,256]{2,1,0:T(1,128)S(1)} %bitcast.338, ...), custom_call_target="tpu_custom_call" | custom-call | tf_op jit(solution)/shard_map/pallas_call | solution.py:1026
  21.0 0.0 collective-permute-done.5.g0_ref
  21.0 0.0 collective-permute-done.6.g1_ref
  21.1 0.0 collective-permute-done.7.g2_ref
  21.1 0.0 collective-permute-done.8.g3_ref
  21.1 7.4 %shard_map.131 = (f32[16,1,2176]{2,1,0:T(1,128)S(1)}, f32[4,128,128]{2,1,0:T(8,128)S(1)}, f32[16,128]{1,0:T(8,128)S(1)}) custom-call(s32[2]{0:T(128)S(1)} %pad_add_fusion.2.where_ref, f32[1,12]{1,0:T(1,128)S(1)} %get-tuple-element.479.coef_ref, f32[16,128]{1,0:T(8,128)S(1)} %get-tuple-element.482.table_ref, f32[4,128,128]{2,1,0:T(8,128)S(1)} %get-tuple-element.483.copy_ref, ...), custom_call_target="tpu_custom_call" | custom-call | tf_op jit(solution)/shard_map/pallas_call | solution.py:1034
  28.5 10.9 %all_to_all.33 = f32[16,1,2176]{2,1,0:T(1,128)S(1)} all-to-all(f32[16,1,2176]{2,1,0:T(1,128)S(1)} %get-tuple-element.488), channel_id=1, replica_groups={{0,2,4,6,8,10,12,14,16,18,20,22,24,26,28,30},{1,3,5,7,9,11,13,15,17,19,..., dimensions={0} | all-to-all | bytes 278528 | tf_op jit(solution)/shard_map/all_to_all | solution.py:1053
  39.4 0.0 collective-permute-start.9
  39.4 1.4 %collective-permute-done.9 = f32[16,1,2176]{2,1,0:T(1,128)S(1)} collective-permute-done((f32[16,1,2176]{2,1,0:T(1,128)S(1)}, f32[16,1,2176]{2,1,0:T(1,128)S(1)}, u32[]{:S(2)}, u32[]{:S(2)}) %collective-permute-start.9) | collective-permute-done | bytes 139296 | tf_op jit(solution)/shard_map/ppermute | solution.py:18
  40.8 0.7 %fusion.32 = f32[]{:T(128)} fusion(f32[16,1,2176]{2,1,0:T(1,128)S(1)} %collective-permute-done.9, f32[16,1,2176]{2,1,0:T(1,128)S(1)} %all_to_all.33), kind=kLoop, calls=%fused_computation.102 | loop fusion | flops 31 | bytes 132 | tf_op jit(solution)/shard_map/reduce_max | solution.py:1058
  42.1 12.6 %conditional.1 = (f32[1,125,256]{2,0,1:T(1,128)}, f32[1,125,256]{2,0,1:T(1,128)}) conditional(s32[]{:T(128)} %convert_element_type.23, (s32[2]{0:T(128)S(1)}, f32[1,12]{1,0:T(1,128)S(1)}, f32[16,1,2176]{2,1,0:T(1,128)S(1)}, f32[16,1,2176]{2,1,0:T(1,128)S(1)}, f32[400,128]{1,0:T(8,128)S(1)}, /*index=5*/f32[400,128]{1,0:T(8,128)S(1)}, ...), branch_computations={%region_1.0_spmd, %region_2.15_spmd} | conditional | flops 347599744 | bytes 9835607 | solution.py:1096
  42.1 12.6 %branch_0_fun.1 = (f32[125,1,256]{2,1,0:T(1,128)}, f32[125,1,256]{2,1,0:T(1,128)}) custom-call(s32[2]{0:T(128)S(1)} %get-tuple-element.411.where_ref, f32[1,12]{1,0:T(1,128)S(1)} %get-tuple-element.412.time_ref, f32[16,1,2176]{2,1,0:T(1,128)S(1)} %get-tuple-element.413.mine_ref, f32[16,1,2176]{2,1,0:T(1,128)S(1)} %get-tuple-element.414.other_ref, ...), custom_call_target="tpu_custom_call" | custom-call | tf_op jit(solution)/shard_map/cond/branch_0_fun/pallas_call | solution.py:1064
  (10 shorter events, 0.0 us)
Async XLA Ops:
  0.6 0.7 %copy-start.7 = (s32[5,512]{1,0:T(8,128)S(1)}, s32[5,512]{1,0:T(8,128)}, u32[]{:S(2)}) copy-start(s32[5,512]{1,0:T(8,128)} %couple_ref.1) | copy-start | bytes 30724
  0.7 0.7 %copy-start.8 = (s32[1,3,128]{2,0,1:T(1,128)S(1)}, s32[1,3,128]{2,0,1:T(1,128)}, u32[]{:S(2)}) copy-start(s32[1,3,128]{2,0,1:T(1,128)} %param.19) | copy-start | bytes 4612
  0.7 0.7 %copy-start.9 = (f32[1,12]{1,0:T(1,128)S(1)}, f32[1,12]{1,0:T(1,128)}, u32[]{:S(2)}) copy-start(f32[1,12]{1,0:T(1,128)} %amplitude_ref.1) | copy-start | bytes 148
  1.4 17.1 %copy-start.4 = (f32[1,125,256]{2,0,1:T(1,128)S(1)}, f32[1,125,256]{2,0,1:T(1,128)}, u32[]{:S(2)}) copy-start(f32[1,125,256]{2,0,1:T(1,128)} %param.15) | copy-start | bytes 384004
  1.4 17.1 %copy-start.5 = (f32[1,125,256]{2,0,1:T(1,128)S(1)}, f32[1,125,256]{2,0,1:T(1,128)}, u32[]{:S(2)}) copy-start(f32[1,125,256]{2,0,1:T(1,128)} %param.16) | copy-start | bytes 384004
  1.4 17.1 %copy-start.6 = (f32[125,1]{1,0:T(8,128)S(1)}, f32[125,1]{1,0:T(8,128)}, u32[]{:S(2)}) copy-start(f32[125,1]{1,0:T(8,128)} %constant.131.clone.weight_ref) | copy-start | bytes 1504
  3.7 14.8 %copy-start.3 = (f32[1,125,256]{2,0,1:T(1,128)S(1)}, f32[1,125,256]{2,0,1:T(1,128)}, u32[]{:S(2)}) copy-start(f32[1,125,256]{2,0,1:T(1,128)} %param.17) | copy-start | bytes 384004
  3.7 14.7 %all-to-all-start.2 = ((f32[16,8,128]{2,1,0:T(8,128)}), f32[16,8,128]{2,1,0:T(8,128)S(1)}, u32[]{:S(2)}, u32[]{:S(2)}) async-start(f32[16,8,128]{2,1,0:T(8,128)} %get-tuple-element.481), calls=%async_computation.2 | async-start | bytes 131072 | tf_op jit(solution)/shard_map/all_to_all | solution.py:1021
  11.2 9.8 %collective-permute-start.5 = (f32[16,512]{1,0:T(8,128)S(1)}, f32[16,512]{1,0:T(8,128)S(1)}, u32[]{:S(2)}, u32[]{:S(2)}) collective-permute-start(f32[16,512]{1,0:T(8,128)S(1)} %get-tuple-element.484.m0_ref), channel_id=1, source_target_pairs={{0,1},{1,0},{2,3},{3,2},{4,5},{5,4},{6,7},{7,6},{8,9},{9,8},{10,11... | collective-permute-start | bytes 98312 | tf_op jit(solution)/shard_map/ppermute | solution.py:18
  11.7 9.4 %collective-permute-start.6 = (f32[16,512]{1,0:T(8,128)S(1)}, f32[16,512]{1,0:T(8,128)S(1)}, u32[]{:S(2)}, u32[]{:S(2)}) collective-permute-start(f32[16,512]{1,0:T(8,128)S(1)} %get-tuple-element.485.m1_ref), channel_id=1, source_target_pairs={{0,2},{1,3},{2,0},{3,1},{4,6},{5,7},{6,4},{7,5},{8,10},{9,11},{10,... | collective-permute-start | bytes 98312 | tf_op jit(solution)/shard_map/ppermute | solution.py:18
  13.3 7.7 %collective-permute-start.7 = (f32[16,512]{1,0:T(8,128)S(1)}, f32[16,512]{1,0:T(8,128)S(1)}, u32[]{:S(2)}, u32[]{:S(2)}) collective-permute-start(f32[16,512]{1,0:T(8,128)S(1)} %get-tuple-element.486.m2_ref), channel_id=1, source_target_pairs={{0,4},{1,5},{2,6},{3,7},{4,0},{5,1},{6,2},{7,3},{8,12},{9,13},{10,... | collective-permute-start | bytes 98312 | tf_op jit(solution)/shard_map/ppermute | solution.py:18
  14.8 6.3 %collective-permute-start.8 = (f32[16,512]{1,0:T(8,128)S(1)}, f32[16,512]{1,0:T(8,128)S(1)}, u32[]{:S(2)}, u32[]{:S(2)}) collective-permute-start(f32[16,512]{1,0:T(8,128)S(1)} %get-tuple-element.487.m3_ref), channel_id=1, source_target_pairs={{0,8},{1,9},{2,10},{3,11},{4,12},{5,13},{6,14},{7,15},{8,0},{9,1},... | collective-permute-start | bytes 98312 | tf_op jit(solution)/shard_map/ppermute | solution.py:18
  39.4 1.4 %collective-permute-start.9 = (f32[16,1,2176]{2,1,0:T(1,128)S(1)}, f32[16,1,2176]{2,1,0:T(1,128)S(1)}, u32[]{:S(2)}, u32[]{:S(2)}) collective-permute-start(f32[16,1,2176]{2,1,0:T(1,128)S(1)} %all_to_all.33), channel_id=1, source_target_pairs={{0,1},{1,0},{2,3},{3,2},{4,5},{5,4},{6,7},{7,6},{8,9},{9,8},{10,11... | collective-permute-start | bytes 417800 | tf_op jit(solution)/shard_map/ppermute | solution.py:18
